TPU v7x, 256 devices: a whole 4x4x8 slice. The times are simulated.
256 devices in a mesh: dp: 8 (over z_lo, x), expert: 32 (over y, z_hi, core).
Axes of the slice: x: 4, y: 4, z: 8 (z_hi: 4, z_lo: 2; z = z_hi * 2 + z_lo), core: 2. Of those that a mesh axis runs over, the one named last changes fastest.
Arguments:
- tokens: bfloat16 [4096, 7168], P('expert', 'dp'), may hold values from -6 to 6
- cotangent: bfloat16 [4096, 7168], P('expert', 'dp'), may hold values from -6 to 6
- routes: int32 [4096, 4], P('expert'), may hold values from 0 to 31, all different within a row; in each aligned block of 128 rows (0 to 127, 128 to 255, ...) at most 24 rows name the same one
- combine_weights: float32 [4096, 4], P('expert'), may hold values from 0.2 to 1
- gate_weight: bfloat16 [32, 7168, 1024], P('expert', 'dp'), may hold values from -0.0625 to 0.0625
- up_weight: bfloat16 [32, 7168, 1024], P('expert', 'dp'), may hold values from -0.0625 to 0.0625
- down_weight: bfloat16 [32, 1024, 7168], P('expert', None, 'dp'), may hold values from -0.1875 to 0.1875
Outputs:
- grad_tokens: bfloat16 [4096, 7168], P('expert', 'dp')
- grad_gate: bfloat16 [32, 7168, 1024], P('expert', 'dp')
- grad_up: bfloat16 [32, 7168, 1024], P('expert', 'dp')
- grad_down: bfloat16 [32, 1024, 7168], P('expert', None, 'dp')
Inputs may be any that keep to these rules, and one draw needn't show every extreme that they name: `routes`: each row names 4 different experts. Within each aligned block of 128 tokens no expert is named by more than 24 tokens, and in every draw some block has an expert named by exactly 24 tokens.
All inputs are finite; a program needn't handle non-finite values.
Results may differ from a plain program's by a relative error of at most 0.029.
Values may be sent and summed in bfloat16 or wider, within the bound.
No kernel may reach another device: no remote copies, remote signals or barrier semaphores. Data moves between devices by JAX's collectives and lax.ppermute only.
A program may use at most 64 MiB of HBM per device.

v0:
```python
import jax
import jax.numpy as jnp
from jax import lax
from jax.sharding import PartitionSpec as P


def contract(left, right, left_dim, right_dim):
    return lax.dot_general(
        left, right, (((left_dim,), (right_dim,)), ((), ())), preferred_element_type=jnp.float32
    )


def local(tokens, cotangent, routes, combine_weights, gate_weight, up_weight, down_weight):
    experts = lax.axis_size("expert")
    tok_count = routes.shape[0]
    top_count = routes.shape[1]
    width = tokens.shape[1]
    capacity = 3 * tok_count * top_count // (2 * experts)
    flat_routes = routes.reshape(-1)
    onehot = (flat_routes[:, None] == jnp.arange(experts, dtype=jnp.int32)[None, :]).astype(
        jnp.int32
    )
    slot_rank = jnp.sum((jnp.cumsum(onehot, axis=0) - onehot) * onehot, axis=1)
    slots = flat_routes * capacity + slot_rank
    x_pairs = jnp.repeat(tokens, top_count, axis=0)
    scaled = (combine_weights[:, :, None] * cotangent[:, None, :].astype(jnp.float32)).astype(
        jnp.bfloat16
    )
    scaled = scaled.reshape(tok_count * top_count, width)
    empty = jnp.zeros((experts * capacity, width), jnp.bfloat16)
    send_x = empty.at[slots].set(x_pairs).reshape(experts, capacity, width)
    send_s = empty.at[slots].set(scaled).reshape(experts, capacity, width)
    weight_g = gate_weight[0]
    weight_u = up_weight[0]
    weight_d = down_weight[0]
    recv_x, recv_s = (
        lax.all_to_all(send_x, "expert", split_axis=0, concat_axis=0, tiled=True),
        lax.all_to_all(send_s, "expert", split_axis=0, concat_axis=0, tiled=True),
    )
    gate_part = jnp.dot(
        recv_x.reshape(-1, width), weight_g, preferred_element_type=jnp.float32
    ).astype(jnp.bfloat16)
    up_part = jnp.dot(
        recv_x.reshape(-1, width), weight_u, preferred_element_type=jnp.float32
    ).astype(jnp.bfloat16)
    rows_x = recv_x.reshape(-1, width)
    rows_s = recv_s.reshape(-1, width)
    back_part = contract(rows_s, weight_d, 1, 1).astype(jnp.bfloat16)
    gate_share, upper_share = (
        lax.psum_scatter(gate_part, "dp", scatter_dimension=1, tiled=True).astype(jnp.float32),
        lax.psum_scatter(up_part, "dp", scatter_dimension=1, tiled=True).astype(jnp.float32),
    )
    activation = jax.nn.silu(gate_share)
    hidden_share = (activation * upper_share).astype(jnp.bfloat16)
    hidden = lax.all_gather(hidden_share, "dp", axis=1, tiled=True)
    dhidden = lax.psum_scatter(back_part, "dp", scatter_dimension=1, tiled=True).astype(jnp.float32)
    sigmoid_g = jax.nn.sigmoid(gate_share)
    slope = sigmoid_g * (1.0 + gate_share * (1.0 - sigmoid_g))
    gate_grad_share = (dhidden * upper_share * slope).astype(jnp.bfloat16)
    up_grad_share = (dhidden * activation).astype(jnp.bfloat16)
    pre_gate, pre_up = (
        lax.all_gather(gate_grad_share, "dp", axis=1, tiled=True),
        lax.all_gather(up_grad_share, "dp", axis=1, tiled=True),
    )
    back_rows = (contract(pre_gate, weight_g, 1, 1) + contract(pre_up, weight_u, 1, 1)).astype(
        jnp.bfloat16
    )
    returned = lax.all_to_all(
        back_rows.reshape(experts, capacity, width),
        "expert",
        split_axis=0,
        concat_axis=0,
        tiled=True,
    )
    grad_down = contract(hidden, rows_s, 0, 0).astype(jnp.bfloat16)[None]
    grad_gate = contract(rows_x, pre_gate, 0, 0).astype(jnp.bfloat16)[None]
    grad_up = contract(rows_x, pre_up, 0, 0).astype(jnp.bfloat16)[None]
    picked = returned.reshape(experts * capacity, width)[slots]
    grad_tokens = jnp.sum(
        picked.reshape(tok_count, top_count, width).astype(jnp.float32), axis=1
    ).astype(jnp.bfloat16)
    return (grad_tokens, grad_gate, grad_up, grad_down)


def solution(mesh):
    placed = (
        P("expert", "dp"),
        P("expert", "dp"),
        P("expert", None),
        P("expert", None),
        P("expert", "dp", None),
        P("expert", "dp", None),
        P("expert", None, "dp"),
    )
    return jax.shard_map(
        local,
        mesh=mesh,
        in_specs=placed,
        out_specs=(
            P("expert", "dp"),
            P("expert", "dp", None),
            P("expert", "dp", None),
            P("expert", None, "dp"),
        ),
        check_vma=False,
    )
```

profile of v0, /device:TPU:1, one launch (start us, length us, event | category | flops | bytes accessed | tf_op | source)
XLA Modules:
  0.0 386.5 jit_solution(345836730867990617)
XLA Ops:
  7.2 0.9 copy.17
  8.1 0.1 eq.29
  8.2 0.1 eq.25
  8.4 0.7 broadcast_multiply_fusion
  9.1 1.2 reduce-window.6
  10.2 0.2 slice_reduce_fusion
  10.5 0.1 copy.16
  10.6 0.1 mul.61
  10.7 1.2 broadcast_in_dim.22
  11.9 1.1 reshape.116
  13.0 0.1 fusion.37
  13.1 3.5 scatter_custom_fusion.1
  16.7 49.8 %all_to_all.15 = bf16[32,24,896]{2,1,0:T(8,128)(2,1)S(1)} all-to-all(bf16[32,24,896]{2,1,0:T(8,128)(2,1)S(1)} %bitcast.76), channel_id=1, replica_groups=mesh['dp'=8,'expert'=32] {'expert'}, dimensions={0} | all-to-all | bytes 2752512 | tf_op jit(solution)/shard_map/all_to_all | solution.py:37
  66.5 1.2 copy-done.1
  67.7 1.8 fusion.13
  69.5 1.6 copy.23
  71.1 3.1 fusion.16
  74.3 1.6 copy.25
  75.9 0.9 copy-done.4
  76.8 1.5 mul.65
  78.3 2.8 mul.66
  81.1 0.1 copy.20
  81.2 0.1 mul.63
  81.3 3.9 %scatter_custom_fusion = bf16[768,896]{1,0:T(8,128)(2,1)S(1)} fusion(s32[512]{0:T(512)S(1)} %bitcast.88, f32[512,896]{1,0:T(8,128)} %mul.66, f32[512]{0:T(512)S(1)} %mul.63, bf16[]{:T(256)} %constant.5.clone.1), kind=kCustom, calls=%fused_computation.21 | custom fusion | flops 917504 | bytes 3213314 | tf_op jit(solution)/shard_map/scatter | solution.py:32
  85.3 48.7 %all_to_all.16 = bf16[32,24,896]{2,1,0:T(8,128)(2,1)S(1)} all-to-all(bf16[32,24,896]{2,1,0:T(8,128)(2,1)S(1)} %bitcast.75), channel_id=1, replica_groups=mesh['dp'=8,'expert'=32] {'expert'}, dimensions={0} | all-to-all | bytes 2752512 | tf_op jit(solution)/shard_map/all_to_all | solution.py:38
  133.9 1.1 copy-done.3
  135.1 1.8 fusion.10
  136.9 1.6 copy.21
  138.6 1.1 copy.24
  139.7 22.9 %reduce-scatter.14.cloned.1.call-done = bf16[128,768]{1,0:T(8,128)(2,1)} async-done(((bf16[1024,768]{1,0:T(8,128)(2,1)}), bf16[128,768]{1,0:T(8,128)(2,1)}) %reduce-scatter.14.cloned.1.call-update) | async-done | bytes 196624
  162.6 1.1 copy.26
  163.7 44.3 %reduce-scatter.10.cloned.1.call-done = bf16[128,768]{1,0:T(8,128)(2,1)} async-done(((bf16[1024,768]{1,0:T(8,128)(2,1)}), bf16[128,768]{1,0:T(8,128)(2,1)}) %reduce-scatter.10.cloned.1.call-update) | async-done | bytes 196624
  208.0 1.1 copy.22
  209.1 1.0 fusion.29
  210.2 0.5 all-gather.6.cloned.1.call-update
  210.8 0.5 all-gather.8.cloned.1.call-update
  211.3 42.8 %all-gather.4.cloned.1.call-done = bf16[768,1024]{1,0:T(8,128)(2,1)} async-done(((bf16[768,128]{1,0:T(8,128)(2,1)}), bf16[768,1024]{1,0:T(8,128)(2,1)}) %all-gather.4.cloned.1.call-update) | async-done | bytes 1572880 | tf_op jit(solution)/shard_map/all_gather | solution.py:62
  254.1 4.8 %fusion = f32[768,896]{1,0:T(8,128)} fusion(bf16[768,1024]{1,0:T(8,128)(2,1)} %all-gather.4.cloned.1.call-done, bf16[1,896,1024]{2,1,0:T(8,128)(2,1)S(1)} %copy-done), kind=kOutput, calls=%fused_computation.4 | convolution fusion | flops 1409286144 | bytes 6160384 | tf_op jit(solution)/shard_map/dot_general | solution.py:8
  258.9 42.3 %all-gather.6.cloned.1.call-done = bf16[768,1024]{1,0:T(8,128)(2,1)} async-done(((bf16[768,128]{1,0:T(8,128)(2,1)}), bf16[768,1024]{1,0:T(8,128)(2,1)}) %all-gather.6.cloned.1.call-update) | async-done | bytes 1572880 | tf_op jit(solution)/shard_map/all_gather | solution.py:63
  301.3 5.7 %add_convert_fusion = bf16[768,896]{1,0:T(8,128)(2,1)} fusion(f32[768,896]{1,0:T(8,128)} %fusion, bf16[768,1024]{1,0:T(8,128)(2,1)} %all-gather.6.cloned.1.call-done, bf16[1,896,1024]{2,1,0:T(8,128)(2,1)} %param.12), kind=kOutput, calls=%fused_computation.3 | convolution fusion | flops 1410662400 | bytes 7536640 | tf_op jit(solution)/shard_map/dot_general | solution.py:8
  307.0 14.1 %all-to-all-start.2 = ((bf16[32,24,896]{2,1,0:T(8,128)(2,1)}), bf16[32,24,896]{2,1,0:T(8,128)(2,1)S(1)}, u32[]{:S(2)}, u32[]{:S(2)}) async-start(bf16[32,24,896]{2,1,0:T(8,128)(2,1)} %bitcast.83), calls=%async_computation.2 | async-start | bytes 2752512 | tf_op jit(solution)/shard_map/all_to_all | solution.py:68
  321.1 4.8 %convert_bitcast_fusion.1 = bf16[1,896,1024]{2,1,0:T(8,128)(2,1)} fusion(bf16[768,896]{1,0:T(8,128)(2,1)} %bitcast.79, bf16[768,1024]{1,0:T(8,128)(2,1)} %all-gather.6.cloned.1.call-done), kind=kOutput, calls=%fused_computation.15 | convolution fusion | flops 1410203648 | bytes 4784128 | tf_op jit(solution)/shard_map/dot_general | solution.py:8
  325.9 2.9 convert_bitcast_fusion.2
  328.8 39.6 %all-gather.8.cloned.1.call-done = bf16[768,1024]{1,0:T(8,128)(2,1)} async-done(((bf16[768,128]{1,0:T(8,128)(2,1)}), bf16[768,1024]{1,0:T(8,128)(2,1)}) %all-gather.8.cloned.1.call-update) | async-done | bytes 1572880 | tf_op jit(solution)/shard_map/all_gather | solution.py:55
  368.4 4.9 %convert_bitcast_fusion = bf16[1,1024,896]{2,1,0:T(8,128)(2,1)} fusion(bf16[768,1024]{1,0:T(8,128)(2,1)} %all-gather.8.cloned.1.call-done, bf16[768,896]{1,0:T(8,128)(2,1)} %bitcast.82), kind=kOutput, calls=%fused_computation.14 | convolution fusion | flops 1410203648 | bytes 4784128 | tf_op jit(solution)/shard_map/dot_general | solution.py:8
  373.3 2.7 gather_fusion
  376.0 1.8 reshape.95
  377.8 1.9 reduce_sum.25
  (32 shorter events, 0.4 us)
Async XLA Ops:
  7.2 64.0 %copy-start = (bf16[1,896,1024]{2,1,0:T(8,128)(2,1)S(1)}, bf16[1,896,1024]{2,1,0:T(8,128)(2,1)}, u32[]{:S(2)}) copy-start(bf16[1,896,1024]{2,1,0:T(8,128)(2,1)} %param.11) | copy-start | bytes 5505028
  7.2 131.4 %reduce-scatter.12.cloned.1.call-start = ((), (), s32[]{:S(2)}) async-start(), calls=%async_computation.10 | async-start | bytes 1769472
  16.7 51.0 %copy-start.7 = (bf16[1,896,1024]{2,1,0:T(8,128)(2,1)S(1)}, bf16[1,896,1024]{2,1,0:T(8,128)(2,1)}, u32[]{:S(2)}) copy-start(bf16[1,896,1024]{2,1,0:T(8,128)(2,1)} %param.12) | copy-start | bytes 5505028
  66.5 1.2 copy-start.1
  71.1 91.6 %reduce-scatter.14.cloned.1.call-start = ((), (), s32[]{:S(2)}) async-start(), calls=%async_computation.11 | async-start | bytes 1769472
  75.9 0.9 copy-start.4
  75.9 132.1 %reduce-scatter.10.cloned.1.call-start = ((), (), s32[]{:S(2)}) async-start(), calls=%async_computation.9 | async-start | bytes 1769472
  78.3 2.9 copy-start.5
  85.3 49.8 %copy-start.6 = (bf16[1,1024,896]{2,1,0:T(8,128)(2,1)S(1)}, bf16[1,1024,896]{2,1,0:T(8,128)(2,1)}, u32[]{:S(2)}) copy-start(bf16[1,1024,896]{2,1,0:T(8,128)(2,1)} %param.13) | copy-start | bytes 5505028
  133.9 1.1 copy-start.3
  138.5 115.6 %all-gather.4.cloned.1.call-start = ((), (), s32[]{:S(2)}) async-start(), calls=%async_computation.6 | async-start | bytes 1769472 | tf_op jit(solution)/shard_map/all_gather | solution.py:62
  210.2 91.1 %all-gather.6.cloned.1.call-start = ((), (), s32[]{:S(2)}) async-start(), calls=%async_computation.7 | async-start | bytes 1769472 | tf_op jit(solution)/shard_map/all_gather | solution.py:63
  210.8 157.6 %all-gather.8.cloned.1.call-start = ((), (), s32[]{:S(2)}) async-start(), calls=%async_computation.8 | async-start | bytes 1769472 | tf_op jit(solution)/shard_map/all_gather | solution.py:55
  307.0 66.3 %all-to-all-start.2 = ((bf16[32,24,896]{2,1,0:T(8,128)(2,1)}), bf16[32,24,896]{2,1,0:T(8,128)(2,1)S(1)}, u32[]{:S(2)}, u32[]{:S(2)}) async-start(bf16[32,24,896]{2,1,0:T(8,128)(2,1)} %bitcast.83), calls=%async_computation.2 | async-start | bytes 2752512 | tf_op jit(solution)/shard_map/all_to_all | solution.py:68
  321.1 4.8 %copy-start.2 = (bf16[32,24,896]{2,1,0:T(8,128)(2,1)S(1)}, bf16[32,24,896]{2,1,0:T(8,128)(2,1)}, u32[]{:S(2)}) copy-start(bf16[32,24,896]{2,1,0:T(8,128)(2,1)} %copy-done.1) | copy-start | bytes 4128772
  321.1 4.8 %copy-start.8 = (bf16[768,1024]{1,0:T(8,128)(2,1)S(1)}, bf16[768,1024]{1,0:T(8,128)(2,1)}, u32[]{:S(2)}) copy-start(bf16[768,1024]{1,0:T(8,128)(2,1)} %all-gather.4.cloned.1.call-done) | copy-start | bytes 4718596
Sparse Core Ops, SparseCore 0:
  71.2 48.9 reduce-scatter.11
  122.7 39.8 reduce-scatter.13
  165.8 42.2 reduce-scatter.9
  210.3 43.8 all-gather.3
  256.3 44.9 all-gather.5
  303.4 64.9 all-gather.7
where the time goes:
time: 387 us
  waiting for transfers between devices  193 us (50%)
  blocking collectives  98.5 us (25%)
  matrix products  29.8 us (8%)
  local copies, waits for them, and re-layouts  27.7 us (7%)
  starting transfers between devices  14.3 us (4%)
  between operations  14.3 us (4%)
  other arithmetic  8.87 us (2%)
    unnamed x9, waiting for transfers between devices  68.4 us
    all_to_all x1, blocking collectives, local(): lax.all_to_all(send_x, 'expert', split_axis=0, concat_axis=0, tiled=True)  49.8 us
    all_to_all x1, blocking collectives, local(): lax.all_to_all(send_s, 'expert', split_axis=0, concat_axis=0, tiled=True)  48.7 us
    all_gather x1, waiting for transfers between devices, local(): lax.all_gather(gate_grad_share, 'dp', axis=1, tiled=True)  42.8 us
    all_gather x1, waiting for transfers between devices, local(): lax.all_gather(up_grad_share, 'dp', axis=1, tiled=True)  42.3 us
    all_gather x1, waiting for transfers between devices, local(): hidden = lax.all_gather(hidden_share, 'dp', axis=1, tiled=True)  39.6 us
    dot_general x6, matrix products, contract(): lax.dot_general(left, right, (((left_dim,), (right_dim,)), ((), ())), pre...  24.9 us
    all_to_all x1, starting transfers between devices, local(): lax.all_to_all(back_rows.reshape(experts, capacity, width), 'expert', spl...  14.1 us
  transfers between devices with their start and end apart: 7, of which 5 were waited for; matrix products, arithmetic and copies ran while one was open for 11% of the time, Pallas kernels for 0%

commit v1 on v0

v1 whole, which is shorter than its diff:
```python
import functools

import jax
import jax.numpy as jnp
from jax import lax
from jax.experimental import pallas as pl
from jax.experimental.pallas import tpu as pltpu
from jax.sharding import PartitionSpec as P

bf16 = jnp.bfloat16
f32 = jnp.float32
NX = 4
NZ = 2
BLK = 256


def call(body, ins, outs, scratch=(), steps=1, n_smem=0):
    def whole(shape):
        return pl.BlockSpec(shape, lambda i, n=len(shape): (0,) * n)

    def rowwise(shape, axis):
        block = tuple(v // steps if k == axis else v for k, v in enumerate(shape))
        return pl.BlockSpec(block, lambda i, n=len(shape), axis=axis: tuple(i if k == axis else 0 for k in range(n)))

    def run(*args):
        specs = [pl.BlockSpec(memory_space=pltpu.SMEM)] * n_smem
        for v, axis in zip(args[n_smem:], ins, strict=True):
            specs.append(whole(v.shape) if axis is None else rowwise(v.shape, axis))
        return pl.pallas_call(
            body,
            grid=(steps,),
            out_shape=tuple(jax.ShapeDtypeStruct(s, d) for s, d, _ in outs),
            in_specs=specs,
            out_specs=tuple(whole(s) if axis is None else rowwise(s, axis) for s, _, axis in outs),
            scratch_shapes=list(scratch),
            compiler_params=pltpu.CompilerParams(vmem_limit_bytes=24 * 1024 * 1024),
        )(*args)

    return run


def dot(a, b, ca, cb):
    return lax.dot_general(a, b, (((ca,), (cb,)), ((), ())), preferred_element_type=f32)


def prep_body(routes_ref, weights_ref, tokens_ref, x_ref, sel_ref, w_ref, *, experts, cap):
    top, tok = routes_ref.shape
    e_id = lax.broadcasted_iota(jnp.int32, (experts, tok), 0)
    names = jnp.zeros((experts, tok), f32)
    scale = jnp.zeros((experts, tok), f32)
    for k in range(top):
        hit = routes_ref[k : k + 1, :] == e_id
        names = jnp.where(hit, 1.0, names)
        scale = jnp.where(hit, weights_ref[k : k + 1, :], scale)
    row = lax.broadcasted_iota(jnp.int32, (tok, tok), 0)
    col = lax.broadcasted_iota(jnp.int32, (tok, tok), 1)
    earlier = jnp.where(row < col, 1.0, 0.0).astype(bf16)
    rank = dot(names.astype(bf16), earlier, 1, 0)
    rank = jnp.where(names > 0.0, rank, -1.0)
    slot = lax.broadcasted_iota(jnp.int32, (cap, tok), 0).astype(f32)
    for e in range(experts):
        here = rank[e : e + 1, :] == slot
        sel_ref[e * cap : (e + 1) * cap, :] = jnp.where(here, 1.0, 0.0)
        w_ref[e * cap : (e + 1) * cap, :] = jnp.sum(
            jnp.where(here, scale[e : e + 1, :], 0.0), axis=1, keepdims=True
        )
    x_ref[...] = dot(sel_ref[...].astype(bf16), tokens_ref[...], 1, 0).astype(bf16)


def scale_body(sel_ref, w_ref, cot_ref, s_ref):
    s_ref[...] = (dot(sel_ref[...].astype(bf16), cot_ref[...], 1, 0) * w_ref[...]).astype(bf16)


def lanes(tab, j):
    return pl.ds(pl.multiple_of(tab[j] * 128, 128), 128)


def gate_up_body(tab, x_ref, wg_ref, wu_ref, *refs):
    outs, (g_s, u_s) = refs[:-2], refs[-2:]
    g_s[...] = dot(x_ref[...], wg_ref[...], 1, 0).astype(bf16)
    u_s[...] = dot(x_ref[...], wu_ref[...], 1, 0).astype(bf16)
    for t in range(NZ):
        for s, o in enumerate(outs):
            o[t, :, 0:128] = g_s[:, lanes(tab, t * NX + s)]
            o[t, :, 128:256] = u_s[:, lanes(tab, t * NX + s)]


def dhid_body(tab, s_ref, wd_ref, *refs):
    outs, d_s = refs[:-1], refs[-1]
    d_s[...] = dot(s_ref[...], wd_ref[...], 1, 1).astype(bf16)
    for t in range(NZ):
        for s, o in enumerate(outs):
            o[t] = d_s[:, lanes(tab, t * NX + s)]


def back_body(tab, *refs):
    pieces, (wg_ref, wu_ref, back_ref, pg_ref, pu_ref) = refs[:-5], refs[-5:]
    for z in range(NZ):
        own, left, right, far_g, far_u = pieces[5 * z : 5 * z + 5]
        for q, v in enumerate((own, left, right)):
            pg_ref[:, lanes(tab, 4 * z + q)] = v[0]
            pu_ref[:, lanes(tab, 4 * z + q)] = v[1]
        pg_ref[:, lanes(tab, 4 * z + 3)] = far_g[...]
        pu_ref[:, lanes(tab, 4 * z + 3)] = far_u[...]
    t = dot(pg_ref[...], wg_ref[...], 1, 1) + dot(pu_ref[...], wu_ref[...], 1, 1)
    back_ref[...] = t.astype(bf16)


def hid_body(tab, *refs):
    pieces, o_ref = refs[:-1], refs[-1]
    half = o_ref.shape[0] // 2
    for z in range(NZ):
        own, left, right, far_a, far_b = pieces[5 * z : 5 * z + 5]
        for q, p in enumerate((own, left, right)):
            o_ref[:, lanes(tab, 4 * z + q)] = p[...]
        o_ref[0:half, lanes(tab, 4 * z + 3)] = far_a[...]
        o_ref[half : 2 * half, lanes(tab, 4 * z + 3)] = far_b[...]


def combine_body(sel_ref, ret_ref, o_ref):
    o_ref[...] = dot(sel_ref[...].astype(bf16), ret_ref[...], 0, 0).astype(bf16)


def dp_perm(dz, dx):
    return [
        (z * NX + x, ((z + dz) % NZ) * NX + (x + dx) % NX) for z in range(NZ) for x in range(NX)
    ]


def move(v, dz, dx):
    return lax.ppermute(v, "dp", dp_perm(dz, dx))


def scatter_sum(parts):
    parts = [parts[0]] + [move(parts[s], 0, s) for s in range(1, NX)]

    def total(t):
        return sum(p[t].astype(f32) for p in parts)

    return total(0) + move(total(1).astype(bf16), 1, 0).astype(f32)


def local(tokens, cotangent, routes, combine_weights, gate_weight, up_weight, down_weight):
    experts = lax.axis_size("expert")
    tok, top = routes.shape
    width = tokens.shape[1]
    hid = gate_weight.shape[2]
    cap = 3 * tok * top // (2 * experts)
    rows = experts * cap
    steps = rows // BLK
    wg, wu, wd = gate_weight[0], up_weight[0], down_weight[0]
    d = lax.axis_index("dp")
    z, x = d // NX, d % NX

    def table(shifts):
        s = jnp.array(shifts, jnp.int32)
        return (((z + jnp.arange(NZ))[:, None] % NZ) * NX + (x + s)[None, :] % NX).reshape(-1)

    dest = table((0, 1, 2, 3))
    orig = table((0, NX - 1, 1, 2))

    send_x, sel, w_slot = call(
        functools.partial(prep_body, experts=experts, cap=cap),
        [None] * 3,
        [((rows, width), bf16, None), ((rows, tok), f32, None), ((rows, 1), f32, None)],
    )(routes.T, combine_weights.T, tokens)
    (send_s,) = call(scale_body, [0, 0, None], [((rows, width), bf16, 0)], steps=steps)(
        sel, w_slot, cotangent
    )

    def a2a(v):
        return lax.all_to_all(
            v.reshape(experts, cap, width), "expert", split_axis=0, concat_axis=0, tiled=True
        ).reshape(rows, width)

    rows_x = a2a(send_x)
    gu = call(
        gate_up_body,
        [0, None, None],
        [((NZ, rows, 256), bf16, 1)] * NX,
        scratch=[pltpu.VMEM((BLK, hid), bf16)] * 2,
        steps=steps,
        n_smem=1,
    )(dest, rows_x, wg, wu)
    rows_s = a2a(send_s)
    dh = call(
        dhid_body,
        [0, None],
        [((NZ, rows, 128), bf16, 1)] * NX,
        scratch=[pltpu.VMEM((BLK, hid), bf16)],
        steps=steps,
        n_smem=1,
    )(dest, rows_s, wd)
    gu = scatter_sum(gu)
    gate, upper = gu[:, :128], gu[:, 128:]
    sig = jax.nn.sigmoid(gate)
    act = gate * sig
    hidden = (act * upper).astype(bf16)
    slope = upper * (sig * (1.0 + gate * (1.0 - sig)))
    dh = scatter_sum(dh)
    pre = jnp.stack([(dh * slope).astype(bf16), (dh * act).astype(bf16)])

    pieces = []
    for v in (pre, move(pre, 1, 0)):
        left, right = move(v, 0, 1), move(v, 0, NX - 1)
        pieces += [v, left, right, move(left[0], 0, 1), move(right[1], 0, NX - 1)]
    back, pre_gate, pre_up = call(
        back_body,
        [1, 1, 1, 0, 0] * NZ + [None, None],
        [((rows, width), bf16, 0), ((rows, hid), bf16, 0), ((rows, hid), bf16, 0)],
        steps=steps,
        n_smem=1,
    )(orig, *pieces, wg, wu)
    hidden_z = move(hidden, 1, 0)
    back, hidden, hidden_z = lax.optimization_barrier((back, hidden, hidden_z))
    returned = a2a(back)
    half = rows // 2
    pieces = []
    for v in (hidden, hidden_z):
        left, right = move(v, 0, 1), move(v, 0, NX - 1)
        pieces += [v, left, right, move(left[:half], 0, 1), move(right[half:], 0, NX - 1)]
    (hidden_all,) = call(hid_body, [None] * 10, [((rows, hid), bf16, None)], n_smem=1)(orig, *pieces)
    grad_gate = dot(rows_x, pre_gate, 0, 0).astype(bf16)[None]
    grad_up = dot(rows_x, pre_up, 0, 0).astype(bf16)[None]
    grad_down = dot(hidden_all, rows_s, 0, 0).astype(bf16)[None]
    (grad_tokens,) = call(combine_body, [None, None], [((tok, width), bf16, None)])(sel, returned)
    return (grad_tokens, grad_gate, grad_up, grad_down)


def solution(mesh):
    placed = (
        P("expert", "dp"),
        P("expert", "dp"),
        P("expert", None),
        P("expert", None),
        P("expert", "dp", None),
        P("expert", "dp", None),
        P("expert", None, "dp"),
    )
    return jax.shard_map(
        local,
        mesh=mesh,
        in_specs=placed,
        out_specs=(
            P("expert", "dp"),
            P("expert", "dp", None),
            P("expert", "dp", None),
            P("expert", None, "dp"),
        ),
        check_vma=False,
    )
```

time: 387 us -> 234 us (0.60)
  the two profiles are of different devices: /device:TPU:1 before, /device:TPU:39 now
where the time goes in v1:
time: 234 us; the launch traced here: 232 us
  waiting for transfers between devices  105 us (45%)
  starting transfers between devices  63 us (27%)
  local copies, waits for them, and re-layouts  29.1 us (12%)
  Pallas kernels  20.2 us (9%)
  matrix products  10.3 us (4%)
  other arithmetic  3.48 us (1%)
    all_to_all x3, waiting for transfers between devices, a2a(): lax.all_to_all(v.reshape(experts, cap, width), 'expert', split_axis=0, co...  63.7 us
    ppermute x26, waiting for transfers between devices, move(): return lax.ppermute(v, 'dp', dp_perm(dz, dx))  41.7 us
    ppermute x26, starting transfers between devices, move(): return lax.ppermute(v, 'dp', dp_perm(dz, dx))  33 us
    all_to_all x3, starting transfers between devices, a2a(): lax.all_to_all(v.reshape(experts, cap, width), 'expert', split_axis=0, co...  30 us
    unnamed x72, local copies, waits for them, and re-layouts  26.1 us
    pallas_call x7, Pallas kernels, run(): pl.pallas_call(body, grid=(steps,), out_shape=tuple((jax.ShapeDtypeStruct...  20.2 us
    dot_general x3, matrix products, dot(): lax.dot_general(a, b, (((ca,), (cb,)), ((), ())), preferred_element_type=...  10.3 us
  transfers between devices with their start and end apart: 29, of which 15 were waited for; matrix products, arithmetic and copies ran while one was open for 7% of the time, Pallas kernels for 7%

profile of v1, /device:TPU:39, one launch (start us, length us, event | category | flops | bytes accessed | tf_op | source)
XLA Modules:
  0.0 232.5 jit_solution(6327201237492265502)
XLA Ops:
  3.7 1.0 copy-done.13
  4.7 11.0 %all-to-all-start.1 = ((bf16[32,24,896]{2,1,0:T(8,128)(2,1)}), bf16[32,24,896]{2,1,0:T(8,128)(2,1)S(1)}, u32[]{:S(2)}, u32[]{:S(2)}) async-start(bf16[32,24,896]{2,1,0:T(8,128)(2,1)} %bitcast.59), calls=%async_computation.1 | async-start | bytes 2752512 | tf_op jit(solution)/shard_map/all_to_all | solution.py:172
  17.7 1.1 copy-done.6
  18.7 33.3 %all-to-all-done.1 = bf16[32,24,896]{2,1,0:T(8,128)(2,1)S(1)} async-done(((bf16[32,24,896]{2,1,0:T(8,128)(2,1)}), bf16[32,24,896]{2,1,0:T(8,128)(2,1)S(1)}, u32[]{:S(2)}, u32[]{:S(2)}) %all-to-all-start.1) | async-done | bytes 1376288 | tf_op jit(solution)/shard_map/all_to_all | solution.py:172
  52.0 1.1 copy-done.3
  53.1 4.5 %all-to-all-start = ((bf16[32,24,896]{2,1,0:T(8,128)(2,1)}), bf16[32,24,896]{2,1,0:T(8,128)(2,1)S(1)}, u32[]{:S(2)}, u32[]{:S(2)}) async-start(bf16[32,24,896]{2,1,0:T(8,128)(2,1)} %bitcast.56), calls=%async_computation | async-start | bytes 2752512 | tf_op jit(solution)/shard_map/all_to_all | solution.py:172
  57.8 1.5 copy-done.1
  59.3 1.3 copy-done.4
  60.6 6.1 %shard_map.123 = (bf16[2,768,256]{2,1,0:T(8,128)(2,1)S(1)}, bf16[2,768,256]{2,1,0:T(8,128)(2,1)}, bf16[2,768,256]{2,1,0:T(8,128)(2,1)}, bf16[2,768,256]{2,1,0:T(8,128)(2,1)}) custom-call(s32[8]{0:T(128)S(1)} %add.167.tab, bf16[768,896]{1,0:T(8,128)(2,1)S(1)} %bitcast.53, bf16[896,1024]{1,0:T(8,128)(2,1)S(1)} %bitcast.47, bf16[896,1024]{1,0:T(8,128)(2,1)S(1)} %bitcast.49), custom_call_target="tpu_custom_call" | custom-call | tf_op jit(solution)/shard_map/pallas_call | solution.py:29
  69.1 1.8 collective-permute-start.4
  70.9 16.6 %all-to-all-done = bf16[32,24,896]{2,1,0:T(8,128)(2,1)S(1)} async-done(((bf16[32,24,896]{2,1,0:T(8,128)(2,1)}), bf16[32,24,896]{2,1,0:T(8,128)(2,1)S(1)}, u32[]{:S(2)}, u32[]{:S(2)}) %all-to-all-start) | async-done | bytes 1376288 | tf_op jit(solution)/shard_map/all_to_all | solution.py:172
  87.4 1.5 copy-done.7
  88.9 3.3 %shard_map.122 = (bf16[2,768,128]{2,1,0:T(8,128)(2,1)S(1)}, bf16[2,768,128]{2,1,0:T(8,128)(2,1)S(1)}, bf16[2,768,128]{2,1,0:T(8,128)(2,1)S(1)}, bf16[2,768,128]{2,1,0:T(8,128)(2,1)S(1)}) custom-call(s32[8]{0:T(128)S(1)} %add.167.tab, bf16[768,896]{1,0:T(8,128)(2,1)S(1)} %bitcast.51, bf16[1024,896]{1,0:T(8,128)(2,1)S(1)} %bitcast.57), custom_call_target="tpu_custom_call" | custom-call | tf_op jit(solution)/shard_map/pallas_call | solution.py:29
  92.2 3.2 %collective-permute-start.2 = (bf16[2,768,128]{2,1,0:T(8,128)(2,1)S(1)}, bf16[2,768,128]{2,1,0:T(8,128)(2,1)S(1)}, u32[]{:S(2)}, u32[]{:S(2)}) collective-permute-start(bf16[2,768,128]{2,1,0:T(8,128)(2,1)S(1)} %get-tuple-element.26), channel_id=1, source_target_pairs={{0,96},{32,0},{64,32},{96,64},{128,224},{160,128},{192,160},{224,1... | collective-permute-start | bytes 1179656 | tf_op jit(solution)/shard_map/ppermute | solution.py:131
  95.5 9.4 %collective-permute-done.6 = bf16[2,768,256]{2,1,0:T(8,128)(2,1)} collective-permute-done((bf16[2,768,256]{2,1,0:T(8,128)(2,1)}, bf16[2,768,256]{2,1,0:T(8,128)(2,1)}, u32[]{:S(2)}, u32[]{:S(2)}) %collective-permute-start.6) | collective-permute-done | bytes 786464 | tf_op jit(solution)/shard_map/ppermute | solution.py:131
  105.4 1.4 fusion
  106.9 1.4 collective-permute-start.7
  108.2 13.5 %collective-permute-done.2 = bf16[2,768,128]{2,1,0:T(8,128)(2,1)S(1)} collective-permute-done((bf16[2,768,128]{2,1,0:T(8,128)(2,1)S(1)}, bf16[2,768,128]{2,1,0:T(8,128)(2,1)S(1)}, u32[]{:S(2)}, u32[]{:S(2)}) %collective-permute-start.2) | collective-permute-done | bytes 393248 | tf_op jit(solution)/shard_map/ppermute | solution.py:131
  122.2 1.1 collective-permute-start.3
  123.3 1.5 bitcast_add_fusion
  124.7 2.5 %collective-permute-done.3 = bf16[768,128]{1,0:T(8,128)(2,1)S(1)} collective-permute-done((bf16[768,128]{1,0:T(8,128)(2,1)S(1)}, bf16[768,128]{1,0:T(8,128)(2,1)S(1)}, u32[]{:S(2)}, u32[]{:S(2)}) %collective-permute-start.3) | collective-permute-done | bytes 196640 | tf_op jit(solution)/shard_map/ppermute | solution.py:131
  128.6 4.2 %collective-permute-start.8 = (bf16[2,768,128]{2,1,0:T(8,128)(2,1)S(1)}, bf16[2,768,128]{2,1,0:T(8,128)(2,1)S(1)}, u32[]{:S(2)}, u32[]{:S(2)}) collective-permute-start(bf16[2,768,128]{2,1,0:T(8,128)(2,1)S(1)} %pad_maximum_fusion.refs_0_), channel_id=1, source_target_pairs={{0,32},{32,64},{64,96},{96,0},{128,160},{160,192},{192,224},{224,1... | collective-permute-start | bytes 1179656 | tf_op jit(solution)/shard_map/ppermute | solution.py:131
  133.5 2.5 %collective-permute-done.12.refs_5_ = bf16[2,768,128]{2,1,0:T(8,128)(2,1)S(1)} collective-permute-done((bf16[2,768,128]{2,1,0:T(8,128)(2,1)S(1)}, bf16[2,768,128]{2,1,0:T(8,128)(2,1)S(1)}, u32[]{:S(2)}, u32[]{:S(2)}) %collective-permute-start.12) | collective-permute-done | bytes 393248 | tf_op jit(solution)/shard_map/ppermute | solution.py:131
  136.1 4.7 %collective-permute-start.13 = (bf16[2,768,128]{2,1,0:T(8,128)(2,1)S(1)}, bf16[2,768,128]{2,1,0:T(8,128)(2,1)S(1)}, u32[]{:S(2)}, u32[]{:S(2)}) collective-permute-start(bf16[2,768,128]{2,1,0:T(8,128)(2,1)S(1)} %collective-permute-done.12.refs_5_), channel_id=1, source_target_pairs={{0,32},{32,64},{64,96},{96,0},{128,160},{160,192},{192,224},{224,1... | collective-permute-start | bytes 1179656 | tf_op jit(solution)/shard_map/ppermute | solution.py:131
  141.5 2.1 collective-permute-start.10
  145.2 2.5 %collective-permute-done.13.refs_6_ = bf16[2,768,128]{2,1,0:T(8,128)(2,1)S(1)} collective-permute-done((bf16[2,768,128]{2,1,0:T(8,128)(2,1)S(1)}, bf16[2,768,128]{2,1,0:T(8,128)(2,1)S(1)}, u32[]{:S(2)}, u32[]{:S(2)}) %collective-permute-start.13) | collective-permute-done | bytes 393248 | tf_op jit(solution)/shard_map/ppermute | solution.py:131
  149.2 3.4 %collective-permute-start.15 = (bf16[768,128]{1,0:T(8,128)(2,1)}, bf16[768,128]{1,0:T(8,128)(2,1)}, u32[]{:S(2)}, u32[]{:S(2)}) collective-permute-start(bf16[768,128]{1,0:T(8,128)(2,1)} %slice_bitcast_fusion.1), channel_id=1, source_target_pairs={{0,32},{32,64},{64,96},{96,0},{128,160},{160,192},{192,224},{224,1... | collective-permute-start | bytes 589832 | tf_op jit(solution)/shard_map/ppermute | solution.py:131
  154.4 1.9 collective-permute-done.11.refs_4_
  156.6 5.6 %collective-permute-done.16.refs_9_ = bf16[768,128]{1,0:T(8,128)(2,1)} collective-permute-done((bf16[768,128]{1,0:T(8,128)(2,1)}, bf16[768,128]{1,0:T(8,128)(2,1)}, u32[]{:S(2)}, u32[]{:S(2)}) %collective-permute-start.16) | collective-permute-done | bytes 196640 | tf_op jit(solution)/shard_map/ppermute | solution.py:131
  162.2 1.5 copy-done.2
  164.7 1.0 copy-done.15
  168.7 1.0 copy-done.27
  169.7 5.5 %shard_map.124 = (bf16[768,896]{1,0:T(8,128)(2,1)S(1)}, bf16[768,1024]{1,0:T(8,128)(2,1)S(1)}, bf16[768,1024]{1,0:T(8,128)(2,1)S(1)}) custom-call(s32[8]{0:T(128)S(1)} %add.162.tab, bf16[2,768,128]{2,1,0:T(8,128)(2,1)S(1)} %copy-done.11, bf16[2,768,128]{2,1,0:T(8,128)(2,1)S(1)} %copy-done.15, bf16[2,768,128]{2,1,0:T(8,128)(2,1)S(1)} %copy-done.17, ...), custom_call_target="tpu_custom_call" | custom-call | tf_op jit(solution)/shard_map/pallas_call | solution.py:29
  175.2 1.1 copy-done.32
  176.3 1.1 copy-done.34
  177.9 14.5 %all-to-all-start.2 = ((bf16[32,24,896]{2,1,0:T(8,128)(2,1)}), bf16[32,24,896]{2,1,0:T(8,128)(2,1)}, u32[]{:S(2)}, u32[]{:S(2)}) async-start(bf16[32,24,896]{2,1,0:T(8,128)(2,1)} %bitcast.58), calls=%async_computation.2 | async-start | bytes 2752512 | tf_op jit(solution)/shard_map/all_to_all | solution.py:172
  192.5 1.5 collective-permute-start.19
  194.0 1.3 collective-permute-start.22
  195.4 4.4 %convert_bitcast_fusion.2 = bf16[1,896,1024]{2,1,0:T(8,128)(2,1)} fusion(bf16[768,896]{1,0:T(8,128)(2,1)S(1)} %bitcast.54, bf16[768,1024]{1,0:T(8,128)(2,1)} %copy-done.34), kind=kOutput, calls=%fused_computation.2 | convolution fusion | flops 1410203648 | bytes 4784128 | tf_op jit(solution)/shard_map/dot_general | solution.py:43
  199.8 2.6 %collective-permute-start.20 = (bf16[384,128]{1,0:T(8,128)(2,1)S(1)}, bf16[384,128]{1,0:T(8,128)(2,1)S(1)}, u32[]{:S(2)}, u32[]{:S(2)}) collective-permute-start(bf16[384,128]{1,0:T(8,128)(2,1)S(1)} %slice.122), channel_id=1, source_target_pairs={{0,32},{32,64},{64,96},{96,0},{128,160},{160,192},{192,224},{224,1... | collective-permute-start | bytes 294920 | tf_op jit(solution)/shard_map/ppermute | solution.py:131
  203.0 2.5 %collective-permute-start.24 = (bf16[384,128]{1,0:T(8,128)(2,1)S(1)}, bf16[384,128]{1,0:T(8,128)(2,1)S(1)}, u32[]{:S(2)}, u32[]{:S(2)}) collective-permute-start(bf16[384,128]{1,0:T(8,128)(2,1)S(1)} %slice.124), channel_id=1, source_target_pairs={{0,32},{32,64},{64,96},{96,0},{128,160},{160,192},{192,224},{224,1... | collective-permute-start | bytes 294920 | tf_op jit(solution)/shard_map/ppermute | solution.py:131
  205.6 2.9 %convert_bitcast_fusion.1 = bf16[1,896,1024]{2,1,0:T(8,128)(2,1)} fusion(bf16[768,896]{1,0:T(8,128)(2,1)S(1)} %bitcast.55, bf16[768,1024]{1,0:T(8,128)(2,1)S(1)} %copy-done.33), kind=kOutput, calls=%fused_computation.1 | convolution fusion | flops 1410203648 | bytes 4784128 | tf_op jit(solution)/shard_map/dot_general | solution.py:43
  208.5 2.3 collective-permute-done.25.refs_9_
  210.7 1.4 shard_map.126
  212.1 3.1 %convert_bitcast_fusion = bf16[1,1024,896]{2,1,0:T(8,128)(2,1)} fusion(bf16[768,1024]{1,0:T(8,128)(2,1)S(1)} %shard_map.126, bf16[768,896]{1,0:T(8,128)(2,1)S(1)} %bitcast.52), kind=kOutput, calls=%fused_computation | convolution fusion | flops 1410203648 | bytes 4784128 | tf_op jit(solution)/shard_map/dot_general | solution.py:43
  215.2 13.8 %all-to-all-done.2 = bf16[32,24,896]{2,1,0:T(8,128)(2,1)} async-done(((bf16[32,24,896]{2,1,0:T(8,128)(2,1)}), bf16[32,24,896]{2,1,0:T(8,128)(2,1)}, u32[]{:S(2)}, u32[]{:S(2)}) %all-to-all-start.2) | async-done | bytes 1376288 | tf_op jit(solution)/shard_map/all_to_all | solution.py:172
  229.0 1.0 copy-done.9
  230.0 2.4 %shard_map.125 = bf16[128,896]{1,0:T(8,128)(2,1)} custom-call(f32[768,128]{1,0:T(8,128)S(1)} %copy-done.9, bf16[768,896]{1,0:T(8,128)(2,1)} %bitcast.20.ret_ref), custom_call_target="tpu_custom_call" | custom-call | tf_op jit(solution)/shard_map/pallas_call | solution.py:29
  (110 shorter events, 21.7 us)
Async XLA Ops:
  0.6 15.2 %copy-start.28 = (bf16[128,896]{1,0:T(8,128)(2,1)S(1)}, bf16[128,896]{1,0:T(8,128)(2,1)}, u32[]{:S(2)}) copy-start(bf16[128,896]{1,0:T(8,128)(2,1)} %cot_ref.1) | copy-start | bytes 688132
  3.7 1.1 copy-start.13
  3.7 12.1 %copy-start.24 = (f32[768,1]{1,0:T(8,128)}, f32[768,1]{1,0:T(8,128)S(1)}, u32[]{:S(2)}) copy-start(f32[768,1]{1,0:T(8,128)S(1)} %get-tuple-element.22.w_ref) | copy-start | bytes 9220
  3.7 12.1 %copy-start.8 = (f32[768,128]{1,0:T(8,128)}, f32[768,128]{1,0:T(8,128)S(1)}, u32[]{:S(2)}) copy-start(f32[768,128]{1,0:T(8,128)S(1)} %get-tuple-element.21.sel_ref) | copy-start | bytes 1179652
  4.7 47.3 %all-to-all-start.1 = ((bf16[32,24,896]{2,1,0:T(8,128)(2,1)}), bf16[32,24,896]{2,1,0:T(8,128)(2,1)S(1)}, u32[]{:S(2)}, u32[]{:S(2)}) async-start(bf16[32,24,896]{2,1,0:T(8,128)(2,1)} %bitcast.59), calls=%async_computation.1 | async-start | bytes 2752512 | tf_op jit(solution)/shard_map/all_to_all | solution.py:172
  17.6 1.1 copy-start.6
  18.7 38.9 %copy-start.35 = (s32[4]{0:T(128)S(1)}, s32[4]{0:T(128)}, u32[]{:S(2)}) copy-start(s32[4]{0:T(128)} %constant.67.clone) | copy-start | bytes 52
  18.7 39.1 %copy-start = (bf16[1,896,1024]{2,1,0:T(8,128)(2,1)S(1)}, bf16[1,896,1024]{2,1,0:T(8,128)(2,1)}, u32[]{:S(2)}) copy-start(bf16[1,896,1024]{2,1,0:T(8,128)(2,1)} %param.13) | copy-start | bytes 5505028
  52.0 1.1 copy-start.3
  53.1 34.3 %all-to-all-start = ((bf16[32,24,896]{2,1,0:T(8,128)(2,1)}), bf16[32,24,896]{2,1,0:T(8,128)(2,1)S(1)}, u32[]{:S(2)}, u32[]{:S(2)}) async-start(bf16[32,24,896]{2,1,0:T(8,128)(2,1)} %bitcast.56), calls=%async_computation | async-start | bytes 2752512 | tf_op jit(solution)/shard_map/all_to_all | solution.py:172
  57.8 1.5 copy-start.1
  59.3 1.3 copy-start.4
  67.7 37.2 %collective-permute-start.6 = (bf16[2,768,256]{2,1,0:T(8,128)(2,1)}, bf16[2,768,256]{2,1,0:T(8,128)(2,1)}, u32[]{:S(2)}, u32[]{:S(2)}) collective-permute-start(bf16[2,768,256]{2,1,0:T(8,128)(2,1)} %get-tuple-element.31), channel_id=1, source_target_pairs={{0,96},{32,0},{64,32},{96,64},{128,224},{160,128},{192,160},{224,1... | collective-permute-start | bytes 2359304 | tf_op jit(solution)/shard_map/ppermute | solution.py:131
  68.2 36.7 %collective-permute-start.5 = (bf16[2,768,256]{2,1,0:T(8,128)(2,1)}, bf16[2,768,256]{2,1,0:T(8,128)(2,1)}, u32[]{:S(2)}, u32[]{:S(2)}) collective-permute-start(bf16[2,768,256]{2,1,0:T(8,128)(2,1)} %get-tuple-element.30), channel_id=1, source_target_pairs={{0,64},{32,96},{64,0},{96,32},{128,192},{160,224},{192,128},{224,1... | collective-permute-start | bytes 2359304 | tf_op jit(solution)/shard_map/ppermute | solution.py:131
  69.1 36.3 %collective-permute-start.4 = (bf16[2,768,256]{2,1,0:T(8,128)(2,1)}, bf16[2,768,256]{2,1,0:T(8,128)(2,1)}, u32[]{:S(2)}, u32[]{:S(2)}) collective-permute-start(bf16[2,768,256]{2,1,0:T(8,128)(2,1)} %get-tuple-element.29), channel_id=1, source_target_pairs={{0,32},{32,64},{64,96},{96,0},{128,160},{160,192},{192,224},{224,1... | collective-permute-start | bytes 2359304 | tf_op jit(solution)/shard_map/ppermute | solution.py:131
  87.4 1.5 copy-start.7
  88.9 16.5 %copy-start.23 = (bf16[2,768,256]{2,1,0:T(8,128)(2,1)S(1)}, bf16[2,768,256]{2,1,0:T(8,128)(2,1)}, u32[]{:S(2)}) copy-start(bf16[2,768,256]{2,1,0:T(8,128)(2,1)} %copy-done.22) | copy-start | bytes 2359300
  92.2 29.5 %collective-permute-start.2 = (bf16[2,768,128]{2,1,0:T(8,128)(2,1)S(1)}, bf16[2,768,128]{2,1,0:T(8,128)(2,1)S(1)}, u32[]{:S(2)}, u32[]{:S(2)}) collective-permute-start(bf16[2,768,128]{2,1,0:T(8,128)(2,1)S(1)} %get-tuple-element.26), channel_id=1, source_target_pairs={{0,96},{32,0},{64,32},{96,64},{128,224},{160,128},{192,160},{224,1... | collective-permute-start | bytes 1179656 | tf_op jit(solution)/shard_map/ppermute | solution.py:131
  95.4 26.3 %collective-permute-start.1 = (bf16[2,768,128]{2,1,0:T(8,128)(2,1)S(1)}, bf16[2,768,128]{2,1,0:T(8,128)(2,1)S(1)}, u32[]{:S(2)}, u32[]{:S(2)}) collective-permute-start(bf16[2,768,128]{2,1,0:T(8,128)(2,1)S(1)} %get-tuple-element.25), channel_id=1, source_target_pairs={{0,64},{32,96},{64,0},{96,32},{128,192},{160,224},{192,128},{224,1... | collective-permute-start | bytes 1179656 | tf_op jit(solution)/shard_map/ppermute | solution.py:131
  104.9 17.2 %collective-permute-start = (bf16[2,768,128]{2,1,0:T(8,128)(2,1)S(1)}, bf16[2,768,128]{2,1,0:T(8,128)(2,1)S(1)}, u32[]{:S(2)}, u32[]{:S(2)}) collective-permute-start(bf16[2,768,128]{2,1,0:T(8,128)(2,1)S(1)} %get-tuple-element.24), channel_id=1, source_target_pairs={{0,32},{32,64},{64,96},{96,0},{128,160},{160,192},{192,224},{224,1... | collective-permute-start | bytes 1179656 | tf_op jit(solution)/shard_map/ppermute | solution.py:131
  106.9 16.4 %collective-permute-start.7 = (bf16[768,256]{1,0:T(8,128)(2,1)S(1)}, bf16[768,256]{1,0:T(8,128)(2,1)S(1)}, u32[]{:S(2)}, u32[]{:S(2)}) collective-permute-start(bf16[768,256]{1,0:T(8,128)(2,1)S(1)} %fusion), channel_id=1, source_target_pairs={{0,128},{32,160},{64,192},{96,224},{128,0},{160,32},{192,64},{224,... | collective-permute-start | bytes 1179656 | tf_op jit(solution)/shard_map/ppermute | solution.py:131
  122.2 5.1 %collective-permute-start.3 = (bf16[768,128]{1,0:T(8,128)(2,1)S(1)}, bf16[768,128]{1,0:T(8,128)(2,1)S(1)}, u32[]{:S(2)}, u32[]{:S(2)}) collective-permute-start(bf16[768,128]{1,0:T(8,128)(2,1)S(1)} %fusion.2), channel_id=1, source_target_pairs={{0,128},{32,160},{64,192},{96,224},{128,0},{160,32},{192,64},{224,... | collective-permute-start | bytes 589832 | tf_op jit(solution)/shard_map/ppermute | solution.py:131
  127.7 8.4 %collective-permute-start.12 = (bf16[2,768,128]{2,1,0:T(8,128)(2,1)S(1)}, bf16[2,768,128]{2,1,0:T(8,128)(2,1)S(1)}, u32[]{:S(2)}, u32[]{:S(2)}) collective-permute-start(bf16[2,768,128]{2,1,0:T(8,128)(2,1)S(1)} %pad_maximum_fusion.refs_0_), channel_id=1, source_target_pairs={{0,128},{32,160},{64,192},{96,224},{128,0},{160,32},{192,64},{224,... | collective-permute-start | bytes 1179656 | tf_op jit(solution)/shard_map/ppermute | solution.py:131
  128.6 12.1 %collective-permute-start.8 = (bf16[2,768,128]{2,1,0:T(8,128)(2,1)S(1)}, bf16[2,768,128]{2,1,0:T(8,128)(2,1)S(1)}, u32[]{:S(2)}, u32[]{:S(2)}) collective-permute-start(bf16[2,768,128]{2,1,0:T(8,128)(2,1)S(1)} %pad_maximum_fusion.refs_0_), channel_id=1, source_target_pairs={{0,32},{32,64},{64,96},{96,0},{128,160},{160,192},{192,224},{224,1... | collective-permute-start | bytes 1179656 | tf_op jit(solution)/shard_map/ppermute | solution.py:131
  132.8 11.6 %collective-permute-start.9 = (bf16[2,768,128]{2,1,0:T(8,128)(2,1)S(1)}, bf16[2,768,128]{2,1,0:T(8,128)(2,1)S(1)}, u32[]{:S(2)}, u32[]{:S(2)}) collective-permute-start(bf16[2,768,128]{2,1,0:T(8,128)(2,1)S(1)} %pad_maximum_fusion.refs_0_), channel_id=1, source_target_pairs={{0,96},{32,0},{64,32},{96,64},{128,224},{160,128},{192,160},{224,1... | collective-permute-start | bytes 1179656 | tf_op jit(solution)/shard_map/ppermute | solution.py:131
  136.1 11.6 %collective-permute-start.13 = (bf16[2,768,128]{2,1,0:T(8,128)(2,1)S(1)}, bf16[2,768,128]{2,1,0:T(8,128)(2,1)S(1)}, u32[]{:S(2)}, u32[]{:S(2)}) collective-permute-start(bf16[2,768,128]{2,1,0:T(8,128)(2,1)S(1)} %collective-permute-done.12.refs_5_), channel_id=1, source_target_pairs={{0,32},{32,64},{64,96},{96,0},{128,160},{160,192},{192,224},{224,1... | collective-permute-start | bytes 1179656 | tf_op jit(solution)/shard_map/ppermute | solution.py:131
  140.8 3.6 %copy-start.14 = (bf16[2,768,128]{2,1,0:T(8,128)(2,1)}, bf16[2,768,128]{2,1,0:T(8,128)(2,1)S(1)}, u32[]{:S(2)}) copy-start(bf16[2,768,128]{2,1,0:T(8,128)(2,1)S(1)} %collective-permute-done.8.refs_1_) | copy-start | bytes 1179652
  141.5 12.9 %collective-permute-start.10 = (bf16[768,128]{1,0:T(8,128)(2,1)}, bf16[768,128]{1,0:T(8,128)(2,1)}, u32[]{:S(2)}, u32[]{:S(2)}) collective-permute-start(bf16[768,128]{1,0:T(8,128)(2,1)} %slice_bitcast_fusion.3), channel_id=1, source_target_pairs={{0,32},{32,64},{64,96},{96,0},{128,160},{160,192},{192,224},{224,1... | collective-permute-start | bytes 589832 | tf_op jit(solution)/shard_map/ppermute | solution.py:131
  143.6 9.0 %collective-permute-start.14 = (bf16[2,768,128]{2,1,0:T(8,128)(2,1)S(1)}, bf16[2,768,128]{2,1,0:T(8,128)(2,1)S(1)}, u32[]{:S(2)}, u32[]{:S(2)}) collective-permute-start(bf16[2,768,128]{2,1,0:T(8,128)(2,1)S(1)} %collective-permute-done.12.refs_5_), channel_id=1, source_target_pairs={{0,96},{32,0},{64,32},{96,64},{128,224},{160,128},{192,160},{224,1... | collective-permute-start | bytes 1179656 | tf_op jit(solution)/shard_map/ppermute | solution.py:131
  145.2 11.1 %collective-permute-start.11 = (bf16[768,128]{1,0:T(8,128)(2,1)}, bf16[768,128]{1,0:T(8,128)(2,1)}, u32[]{:S(2)}, u32[]{:S(2)}) collective-permute-start(bf16[768,128]{1,0:T(8,128)(2,1)} %slice_bitcast_fusion.2), channel_id=1, source_target_pairs={{0,96},{32,0},{64,32},{96,64},{128,224},{160,128},{192,160},{224,1... | collective-permute-start | bytes 589832 | tf_op jit(solution)/shard_map/ppermute | solution.py:131
  149.2 7.4 %collective-permute-start.15 = (bf16[768,128]{1,0:T(8,128)(2,1)}, bf16[768,128]{1,0:T(8,128)(2,1)}, u32[]{:S(2)}, u32[]{:S(2)}) collective-permute-start(bf16[768,128]{1,0:T(8,128)(2,1)} %slice_bitcast_fusion.1), channel_id=1, source_target_pairs={{0,32},{32,64},{64,96},{96,0},{128,160},{160,192},{192,224},{224,1... | collective-permute-start | bytes 589832 | tf_op jit(solution)/shard_map/ppermute | solution.py:131
  154.0 8.2 %collective-permute-start.16 = (bf16[768,128]{1,0:T(8,128)(2,1)}, bf16[768,128]{1,0:T(8,128)(2,1)}, u32[]{:S(2)}, u32[]{:S(2)}) collective-permute-start(bf16[768,128]{1,0:T(8,128)(2,1)} %slice_bitcast_fusion), channel_id=1, source_target_pairs={{0,96},{32,0},{64,32},{96,64},{128,224},{160,128},{192,160},{224,1... | collective-permute-start | bytes 589832 | tf_op jit(solution)/shard_map/ppermute | solution.py:131
  154.0 22.3 %collective-permute-start.17 = (bf16[768,128]{1,0:T(8,128)(2,1)S(1)}, bf16[768,128]{1,0:T(8,128)(2,1)}, u32[]{:S(2)}, u32[]{:S(2)}) collective-permute-start(bf16[768,128]{1,0:T(8,128)(2,1)S(1)} %get-tuple-element.36.refs_0_), channel_id=1, source_target_pairs={{0,128},{32,160},{64,192},{96,224},{128,0},{160,32},{192,64},{224,... | collective-permute-start | bytes 589832 | tf_op jit(solution)/shard_map/ppermute | solution.py:131
  162.2 1.5 copy-start.2
  175.2 1.1 copy-start.32
  176.3 1.1 copy-start.34
  176.3 1.6 copy-start.12
  176.3 19.1 %copy-start.5 = (bf16[32,24,896]{2,1,0:T(8,128)(2,1)S(1)}, bf16[32,24,896]{2,1,0:T(8,128)(2,1)}, u32[]{:S(2)}) copy-start(bf16[32,24,896]{2,1,0:T(8,128)(2,1)} %copy-done.3) | copy-start | bytes 4128772
  177.9 51.1 %all-to-all-start.2 = ((bf16[32,24,896]{2,1,0:T(8,128)(2,1)}), bf16[32,24,896]{2,1,0:T(8,128)(2,1)}, u32[]{:S(2)}, u32[]{:S(2)}) async-start(bf16[32,24,896]{2,1,0:T(8,128)(2,1)} %bitcast.58), calls=%async_computation.2 | async-start | bytes 2752512 | tf_op jit(solution)/shard_map/all_to_all | solution.py:172
  192.4 7.4 %collective-permute-start.18 = (bf16[768,128]{1,0:T(8,128)(2,1)S(1)}, bf16[768,128]{1,0:T(8,128)(2,1)S(1)}, u32[]{:S(2)}, u32[]{:S(2)}) collective-permute-start(bf16[768,128]{1,0:T(8,128)(2,1)S(1)} %get-tuple-element.36.refs_0_), channel_id=1, source_target_pairs={{0,32},{32,64},{64,96},{96,0},{128,160},{160,192},{192,224},{224,1... | collective-permute-start | bytes 589832 | tf_op jit(solution)/shard_map/ppermute | solution.py:131
  192.5 9.9 %collective-permute-start.19 = (bf16[768,128]{1,0:T(8,128)(2,1)S(1)}, bf16[768,128]{1,0:T(8,128)(2,1)S(1)}, u32[]{:S(2)}, u32[]{:S(2)}) collective-permute-start(bf16[768,128]{1,0:T(8,128)(2,1)S(1)} %get-tuple-element.36.refs_0_), channel_id=1, source_target_pairs={{0,96},{32,0},{64,32},{96,64},{128,224},{160,128},{192,160},{224,1... | collective-permute-start | bytes 589832 | tf_op jit(solution)/shard_map/ppermute | solution.py:131
  194.0 9.0 %collective-permute-start.22 = (bf16[768,128]{1,0:T(8,128)(2,1)}, bf16[768,128]{1,0:T(8,128)(2,1)S(1)}, u32[]{:S(2)}, u32[]{:S(2)}) collective-permute-start(bf16[768,128]{1,0:T(8,128)(2,1)} %collective-permute-done.17.refs_5_), channel_id=1, source_target_pairs={{0,32},{32,64},{64,96},{96,0},{128,160},{160,192},{192,224},{224,1... | collective-permute-start | bytes 589832 | tf_op jit(solution)/shard_map/ppermute | solution.py:131
  195.3 10.2 %collective-permute-start.23 = (bf16[768,128]{1,0:T(8,128)(2,1)}, bf16[768,128]{1,0:T(8,128)(2,1)S(1)}, u32[]{:S(2)}, u32[]{:S(2)}) collective-permute-start(bf16[768,128]{1,0:T(8,128)(2,1)} %collective-permute-done.17.refs_5_), channel_id=1, source_target_pairs={{0,96},{32,0},{64,32},{96,64},{128,224},{160,128},{192,160},{224,1... | collective-permute-start | bytes 589832 | tf_op jit(solution)/shard_map/ppermute | solution.py:131
  195.4 10.2 %copy-start.33 = (bf16[768,1024]{1,0:T(8,128)(2,1)S(1)}, bf16[768,1024]{1,0:T(8,128)(2,1)}, u32[]{:S(2)}) copy-start(bf16[768,1024]{1,0:T(8,128)(2,1)} %copy-done.32) | copy-start | bytes 4718596
  199.8 8.7 %collective-permute-start.20 = (bf16[384,128]{1,0:T(8,128)(2,1)S(1)}, bf16[384,128]{1,0:T(8,128)(2,1)S(1)}, u32[]{:S(2)}, u32[]{:S(2)}) collective-permute-start(bf16[384,128]{1,0:T(8,128)(2,1)S(1)} %slice.122), channel_id=1, source_target_pairs={{0,32},{32,64},{64,96},{96,0},{128,160},{160,192},{192,224},{224,1... | collective-permute-start | bytes 294920 | tf_op jit(solution)/shard_map/ppermute | solution.py:131
  202.4 6.1 %collective-permute-start.21 = (bf16[384,128]{1,0:T(8,128)(2,1)S(1)}, bf16[384,128]{1,0:T(8,128)(2,1)S(1)}, u32[]{:S(2)}, u32[]{:S(2)}) collective-permute-start(bf16[384,128]{1,0:T(8,128)(2,1)S(1)} %slice.123), channel_id=1, source_target_pairs={{0,96},{32,0},{64,32},{96,64},{128,224},{160,128},{192,160},{224,1... | collective-permute-start | bytes 294920 | tf_op jit(solution)/shard_map/ppermute | solution.py:131
  203.0 5.5 %collective-permute-start.24 = (bf16[384,128]{1,0:T(8,128)(2,1)S(1)}, bf16[384,128]{1,0:T(8,128)(2,1)S(1)}, u32[]{:S(2)}, u32[]{:S(2)}) collective-permute-start(bf16[384,128]{1,0:T(8,128)(2,1)S(1)} %slice.124), channel_id=1, source_target_pairs={{0,32},{32,64},{64,96},{96,0},{128,160},{160,192},{192,224},{224,1... | collective-permute-start | bytes 294920 | tf_op jit(solution)/shard_map/ppermute | solution.py:131
  205.5 5.2 %collective-permute-start.25 = (bf16[384,128]{1,0:T(8,128)(2,1)S(1)}, bf16[384,128]{1,0:T(8,128)(2,1)S(1)}, u32[]{:S(2)}, u32[]{:S(2)}) collective-permute-start(bf16[384,128]{1,0:T(8,128)(2,1)S(1)} %slice.125), channel_id=1, source_target_pairs={{0,96},{32,0},{64,32},{96,64},{128,224},{160,128},{192,160},{224,1... | collective-permute-start | bytes 294920 | tf_op jit(solution)/shard_map/ppermute | solution.py:131
  (17 other events, 15.1 us)

commit v2 on v1

--- a/solution.py
+++ b/solution.py
@@ -14,7 +14,10 @@
 BLK = 256
 
 
-def call(body, ins, outs, scratch=(), steps=1, n_smem=0):
+FIRST, LAST = "first", "last"
+
+
+def call(body, ins, outs, scratch=(), steps=1, n_smem=0, hbm=()):
     def whole(shape):
         return pl.BlockSpec(shape, lambda i, n=len(shape): (0,) * n)
 
@@ -22,16 +25,28 @@
         block = tuple(v // steps if k == axis else v for k, v in enumerate(shape))
         return pl.BlockSpec(block, lambda i, n=len(shape), axis=axis: tuple(i if k == axis else 0 for k in range(n)))
 
+    def out_spec(shape, axis):
+        if axis in (FIRST, LAST):
+            block = (shape[0], shape[1] // 2, shape[2])
+            first = axis == FIRST
+            return pl.BlockSpec(
+                block, lambda i: (0, jnp.minimum(i, 1) if first else jnp.maximum(i - 2, 0), 0)
+            )
+        return whole(shape) if axis is None else rowwise(shape, axis)
+
     def run(*args):
         specs = [pl.BlockSpec(memory_space=pltpu.SMEM)] * n_smem
+        args = list(args)
+        for k in hbm:
+            args[n_smem + k] = pltpu.with_memory_space_constraint(args[n_smem + k], pltpu.HBM)
         for v, axis in zip(args[n_smem:], ins, strict=True):
             specs.append(whole(v.shape) if axis is None else rowwise(v.shape, axis))
         return pl.pallas_call(
             body,
             grid=(steps,),
-            out_shape=tuple(jax.ShapeDtypeStruct(s, d) for s, d, _ in outs),
+            out_shape=tuple((pltpu.HBM if hbm else jax.ShapeDtypeStruct)(s, d) for s, d, _ in outs),
             in_specs=specs,
-            out_specs=tuple(whole(s) if axis is None else rowwise(s, axis) for s, _, axis in outs),
+            out_specs=tuple(out_spec(s, axis) for s, _, axis in outs),
             scratch_shapes=list(scratch),
             compiler_params=pltpu.CompilerParams(vmem_limit_bytes=24 * 1024 * 1024),
         )(*args)
@@ -76,7 +91,7 @@
 
 
 def gate_up_body(tab, x_ref, wg_ref, wu_ref, *refs):
-    outs, (g_s, u_s) = refs[:-2], refs[-2:]
+    outs, (g_s, u_s) = refs[:NX], refs[NX:]
     g_s[...] = dot(x_ref[...], wg_ref[...], 1, 0).astype(bf16)
     u_s[...] = dot(x_ref[...], wu_ref[...], 1, 0).astype(bf16)
     for t in range(NZ):
@@ -86,7 +101,7 @@
 
 
 def dhid_body(tab, s_ref, wd_ref, *refs):
-    outs, d_s = refs[:-1], refs[-1]
+    outs, d_s = refs[:NX], refs[NX]
     d_s[...] = dot(s_ref[...], wd_ref[...], 1, 1).astype(bf16)
     for t in range(NZ):
         for s, o in enumerate(outs):
@@ -94,14 +109,11 @@
 
 
 def back_body(tab, *refs):
-    pieces, (wg_ref, wu_ref, back_ref, pg_ref, pu_ref) = refs[:-5], refs[-5:]
-    for z in range(NZ):
-        own, left, right, far_g, far_u = pieces[5 * z : 5 * z + 5]
-        for q, v in enumerate((own, left, right)):
-            pg_ref[:, lanes(tab, 4 * z + q)] = v[0]
-            pu_ref[:, lanes(tab, 4 * z + q)] = v[1]
-        pg_ref[:, lanes(tab, 4 * z + 3)] = far_g[...]
-        pu_ref[:, lanes(tab, 4 * z + 3)] = far_u[...]
+    gates, ups = refs[: NZ * NX], refs[NZ * NX : 2 * NZ * NX]
+    wg_ref, wu_ref, back_ref, pg_ref, pu_ref = refs[-5:]
+    for q in range(NZ * NX):
+        pg_ref[:, lanes(tab, q)] = gates[q][...]
+        pu_ref[:, lanes(tab, q)] = ups[q][...]
     t = dot(pg_ref[...], wg_ref[...], 1, 1) + dot(pu_ref[...], wu_ref[...], 1, 1)
     back_ref[...] = t.astype(bf16)
 
@@ -131,13 +143,31 @@
     return lax.ppermute(v, "dp", dp_perm(dz, dx))
 
 
-def scatter_sum(parts):
-    parts = [parts[0]] + [move(parts[s], 0, s) for s in range(1, NX)]
-
-    def total(t):
-        return sum(p[t].astype(f32) for p in parts)
-
-    return total(0) + move(total(1).astype(bf16), 1, 0).astype(f32)
+def add(*parts):
+    return sum(p.astype(f32) for p in parts)
+
+
+def sum_x_first(by_s):
+    parts = [by_s[0]] + [move(by_s[s], 0, s) for s in range(1, NX)]
+    other = move(add(*(p[1] for p in parts)).astype(bf16), 1, 0)
+    return add(other, *(p[0] for p in parts))
+
+
+def sum_z_first(by_t):
+    other = move(by_t[1], 1, 0)
+    sums = [add(by_t[0][s], other[s]) for s in range(NX)]
+    return add(sums[0], *(move(sums[s].astype(bf16), 0, s) for s in range(1, NX)))
+
+
+def gather(gate, up):
+    gl, gr = move(gate, 0, 1), move(gate, 0, NX - 1)
+    uz = move(up, 1, 0)
+    ul, ur = move(up, 0, 1), move(up, 0, NX - 1)
+    gates = [gate, gl, gr, move(gl, 0, 1)]
+    gates += [move(v, 1, 0) for v in gates]
+    uzl, uzr = move(uz, 0, 1), move(uz, 0, NX - 1)
+    ups = [up, ul, ur, move(ur, 0, NX - 1), uz, uzl, uzr, move(uzl, 0, 1)]
+    return gates + ups
 
 
 def local(tokens, cotangent, routes, combine_weights, gate_weight, up_weight, down_weight):
@@ -174,56 +204,54 @@
         ).reshape(rows, width)
 
     rows_x = a2a(send_x)
+    rows_x, send_s = lax.optimization_barrier((rows_x, send_s))
     gu = call(
         gate_up_body,
         [0, None, None],
         [((NZ, rows, 256), bf16, 1)] * NX,
         scratch=[pltpu.VMEM((BLK, hid), bf16)] * 2,
         steps=steps,
+        hbm=(0,),
         n_smem=1,
     )(dest, rows_x, wg, wu)
     rows_s = a2a(send_s)
+    half = rows // 2
     dh = call(
         dhid_body,
         [0, None],
         [((NZ, rows, 128), bf16, 1)] * NX,
         scratch=[pltpu.VMEM((BLK, hid), bf16)],
         steps=steps,
+        hbm=(0,),
         n_smem=1,
     )(dest, rows_s, wd)
-    gu = scatter_sum(gu)
+    gu = sum_x_first(gu)
     gate, upper = gu[:, :128], gu[:, 128:]
     sig = jax.nn.sigmoid(gate)
     act = gate * sig
     hidden = (act * upper).astype(bf16)
     slope = upper * (sig * (1.0 + gate * (1.0 - sig)))
-    dh = scatter_sum(dh)
-    pre = jnp.stack([(dh * slope).astype(bf16), (dh * act).astype(bf16)])
-
-    pieces = []
-    for v in (pre, move(pre, 1, 0)):
-        left, right = move(v, 0, 1), move(v, 0, NX - 1)
-        pieces += [v, left, right, move(left[0], 0, 1), move(right[1], 0, NX - 1)]
+    dh = sum_x_first(dh)
     back, pre_gate, pre_up = call(
         back_body,
-        [1, 1, 1, 0, 0] * NZ + [None, None],
+        [0] * (2 * NZ * NX) + [None, None],
         [((rows, width), bf16, 0), ((rows, hid), bf16, 0), ((rows, hid), bf16, 0)],
         steps=steps,
+        hbm=tuple(range(2 * NZ * NX)),
         n_smem=1,
-    )(orig, *pieces, wg, wu)
+    )(orig, *gather((dh * slope).astype(bf16), (dh * act).astype(bf16)), wg, wu)
     hidden_z = move(hidden, 1, 0)
     back, hidden, hidden_z = lax.optimization_barrier((back, hidden, hidden_z))
     returned = a2a(back)
-    half = rows // 2
     pieces = []
     for v in (hidden, hidden_z):
         left, right = move(v, 0, 1), move(v, 0, NX - 1)
         pieces += [v, left, right, move(left[:half], 0, 1), move(right[half:], 0, NX - 1)]
-    (hidden_all,) = call(hid_body, [None] * 10, [((rows, hid), bf16, None)], n_smem=1)(orig, *pieces)
+    (hidden_all,) = call(hid_body, [None] * 10, [((rows, hid), bf16, None)], n_smem=1, hbm=tuple(range(10)))(orig, *pieces)
     grad_gate = dot(rows_x, pre_gate, 0, 0).astype(bf16)[None]
     grad_up = dot(rows_x, pre_up, 0, 0).astype(bf16)[None]
     grad_down = dot(hidden_all, rows_s, 0, 0).astype(bf16)[None]
-    (grad_tokens,) = call(combine_body, [None, None], [((tok, width), bf16, None)])(sel, returned)
+    (grad_tokens,) = call(combine_body, [None, None], [((tok, width), bf16, None)], hbm=(0, 1))(sel, returned)
     return (grad_tokens, grad_gate, grad_up, grad_down)
 
 

time: 234 us -> 219 us (0.936)
  the two profiles are of different devices: /device:TPU:39 before, /device:TPU:1 now
where the time goes in v2:
time: 219 us
  waiting for transfers between devices  98.7 us (45%)
  starting transfers between devices  63.6 us (29%)
  Pallas kernels  27.7 us (13%)
  matrix products  13.5 us (6%)
  local copies, waits for them, and re-layouts  10.6 us (5%)
  other arithmetic  3.42 us (2%)
    all_to_all x3, waiting for transfers between devices, a2a(): lax.all_to_all(v.reshape(experts, cap, width), 'expert', split_axis=0, co...  62.7 us
    ppermute x31, waiting for transfers between devices, move(): return lax.ppermute(v, 'dp', dp_perm(dz, dx))  36 us
    all_to_all x3, starting transfers between devices, a2a(): lax.all_to_all(v.reshape(experts, cap, width), 'expert', split_axis=0, co...  33.4 us
    ppermute x31, starting transfers between devices, move(): return lax.ppermute(v, 'dp', dp_perm(dz, dx))  30.2 us
    pallas_call x7, Pallas kernels, run(): pl.pallas_call(body, grid=(steps,), out_shape=tuple(((pltpu.HBM if hbm el...  27.7 us
    dot_general x3, matrix products, dot(): lax.dot_general(a, b, (((ca,), (cb,)), ((), ())), preferred_element_type=...  13.5 us
    unnamed x68, local copies, waits for them, and re-layouts  10.4 us
  transfers between devices with their start and end apart: 34, of which 15 were waited for; matrix products, arithmetic and copies ran while one was open for 8% of the time, Pallas kernels for 11%

profile of v2, /device:TPU:1, one launch (start us, length us, event | category | flops | bytes accessed | tf_op | source)
XLA Modules:
  0.0 218.5 jit_solution(2869978461442890947)
XLA Ops:
  0.7 1.0 copy-done.6
  3.0 1.8 shard_map.120
  4.7 12.8 %all-to-all-start = ((bf16[32,24,896]{2,1,0:T(8,128)(2,1)}), bf16[32,24,896]{2,1,0:T(8,128)(2,1)}, u32[]{:S(2)}, u32[]{:S(2)}) async-start(bf16[32,24,896]{2,1,0:T(8,128)(2,1)} %bitcast.2), calls=%async_computation | async-start | bytes 2752512 | tf_op jit(solution)/shard_map/all_to_all | solution.py:202
  17.6 2.1 shard_map.121
  19.7 32.9 %all-to-all-done = bf16[32,24,896]{2,1,0:T(8,128)(2,1)} async-done(((bf16[32,24,896]{2,1,0:T(8,128)(2,1)}), bf16[32,24,896]{2,1,0:T(8,128)(2,1)}, u32[]{:S(2)}, u32[]{:S(2)}) %all-to-all-start) | async-done | bytes 1376288 | tf_op jit(solution)/shard_map/all_to_all | solution.py:202
  52.6 6.2 %all-to-all-start.1 = ((bf16[32,24,896]{2,1,0:T(8,128)(2,1)}), bf16[32,24,896]{2,1,0:T(8,128)(2,1)S(1)}, u32[]{:S(2)}, u32[]{:S(2)}) async-start(bf16[32,24,896]{2,1,0:T(8,128)(2,1)} %bitcast.4), calls=%async_computation.1 | async-start | bytes 2752512 | tf_op jit(solution)/shard_map/all_to_all | solution.py:202
  59.0 1.5 copy-done.1
  60.5 6.7 %shard_map.123 = (bf16[2,768,256]{2,1,0:T(8,128)(2,1)}, bf16[2,768,256]{2,1,0:T(8,128)(2,1)}, bf16[2,768,256]{2,1,0:T(8,128)(2,1)}, bf16[2,768,256]{2,1,0:T(8,128)(2,1)}) custom-call(s32[8]{0:T(128)S(1)} %add.157.tab, bf16[768,896]{1,0:T(8,128)(2,1)} %bitcast.3.x_ref, bf16[896,1024]{1,0:T(8,128)(2,1)S(1)} %bitcast.79, bf16[896,1024]{1,0:T(8,128)(2,1)S(1)} %bitcast.81), custom_call_target="tpu_custom_call" | custom-call | tf_op jit(solution)/shard_map/pallas_call | solution.py:44
  67.1 2.5 %collective-permute-start.6 = (bf16[2,768,256]{2,1,0:T(8,128)(2,1)}, bf16[2,768,256]{2,1,0:T(8,128)(2,1)}, u32[]{:S(2)}, u32[]{:S(2)}) collective-permute-start(bf16[2,768,256]{2,1,0:T(8,128)(2,1)} %get-tuple-element.35), channel_id=1, source_target_pairs={{0,96},{32,0},{64,32},{96,64},{128,224},{160,128},{192,160},{224,1... | collective-permute-start | bytes 2359304 | tf_op jit(solution)/shard_map/ppermute | solution.py:143
  70.5 23.6 %all-to-all-done.1 = bf16[32,24,896]{2,1,0:T(8,128)(2,1)S(1)} async-done(((bf16[32,24,896]{2,1,0:T(8,128)(2,1)}), bf16[32,24,896]{2,1,0:T(8,128)(2,1)S(1)}, u32[]{:S(2)}, u32[]{:S(2)}) %all-to-all-start.1) | async-done | bytes 1376288 | tf_op jit(solution)/shard_map/all_to_all | solution.py:202
  94.2 1.1 copy-done.9
  95.3 1.5 copy-done.3
  96.8 4.9 %shard_map.122 = (bf16[2,768,128]{2,1,0:T(8,128)(2,1)}, bf16[2,768,128]{2,1,0:T(8,128)(2,1)}, bf16[2,768,128]{2,1,0:T(8,128)(2,1)}, bf16[2,768,128]{2,1,0:T(8,128)(2,1)}) custom-call(s32[8]{0:T(128)S(1)} %add.157.tab, bf16[768,896]{1,0:T(8,128)(2,1)} %bitcast.86, bf16[1024,896]{1,0:T(8,128)(2,1)S(1)} %bitcast.83), custom_call_target="tpu_custom_call" | custom-call | tf_op jit(solution)/shard_map/pallas_call | solution.py:44
  101.6 2.5 %collective-permute-start.2 = (bf16[2,768,128]{2,1,0:T(8,128)(2,1)}, bf16[2,768,128]{2,1,0:T(8,128)(2,1)S(1)}, u32[]{:S(2)}, u32[]{:S(2)}) collective-permute-start(bf16[2,768,128]{2,1,0:T(8,128)(2,1)} %get-tuple-element.30), channel_id=1, source_target_pairs={{0,96},{32,0},{64,32},{96,64},{128,224},{160,128},{192,160},{224,1... | collective-permute-start | bytes 1179656 | tf_op jit(solution)/shard_map/ppermute | solution.py:143
  105.0 2.7 %collective-permute-done.4 = bf16[2,768,256]{2,1,0:T(8,128)(2,1)} collective-permute-done((bf16[2,768,256]{2,1,0:T(8,128)(2,1)}, bf16[2,768,256]{2,1,0:T(8,128)(2,1)}, u32[]{:S(2)}, u32[]{:S(2)}) %collective-permute-start.4) | collective-permute-done | bytes 786464 | tf_op jit(solution)/shard_map/ppermute | solution.py:143
  107.8 1.4 fusion
  109.2 1.2 collective-permute-start.7
  110.4 1.5 collective-permute-done.2
  111.9 2.6 %collective-permute-done.1 = bf16[2,768,128]{2,1,0:T(8,128)(2,1)S(1)} collective-permute-done((bf16[2,768,128]{2,1,0:T(8,128)(2,1)}, bf16[2,768,128]{2,1,0:T(8,128)(2,1)S(1)}, u32[]{:S(2)}, u32[]{:S(2)}) %collective-permute-start.1) | collective-permute-done | bytes 393248 | tf_op jit(solution)/shard_map/ppermute | solution.py:143
  114.5 10.8 %collective-permute-done = bf16[2,768,128]{2,1,0:T(8,128)(2,1)S(1)} collective-permute-done((bf16[2,768,128]{2,1,0:T(8,128)(2,1)}, bf16[2,768,128]{2,1,0:T(8,128)(2,1)S(1)}, u32[]{:S(2)}, u32[]{:S(2)}) %collective-permute-start) | collective-permute-done | bytes 393248 | tf_op jit(solution)/shard_map/ppermute | solution.py:143
  125.5 1.5 convert_add_fusion
  127.0 4.5 %collective-permute-done.3 = bf16[768,128]{1,0:T(8,128)(2,1)S(1)} collective-permute-done((bf16[768,128]{1,0:T(8,128)(2,1)S(1)}, bf16[768,128]{1,0:T(8,128)(2,1)S(1)}, u32[]{:S(2)}, u32[]{:S(2)}) %collective-permute-start.3) | collective-permute-done | bytes 196640 | tf_op jit(solution)/shard_map/ppermute | solution.py:143
  132.0 2.7 %collective-permute-start.9 = (bf16[768,128]{1,0:T(8,128)(2,1)S(1)}, bf16[768,128]{1,0:T(8,128)(2,1)S(1)}, u32[]{:S(2)}, u32[]{:S(2)}) collective-permute-start(bf16[768,128]{1,0:T(8,128)(2,1)S(1)} %get-tuple-element.43.refs_0_), channel_id=1, source_target_pairs={{0,96},{32,0},{64,32},{96,64},{128,224},{160,128},{192,160},{224,1... | collective-permute-start | bytes 589832 | tf_op jit(solution)/shard_map/ppermute | solution.py:143
  134.9 1.1 collective-permute-start.18
  136.1 2.1 collective-permute-done.8.refs_1_
  138.8 0.9 collective-permute-start.10
  140.3 3.0 %collective-permute-done.18.refs_12_ = bf16[768,128]{1,0:T(8,128)(2,1)S(1)} collective-permute-done((bf16[768,128]{1,0:T(8,128)(2,1)S(1)}, bf16[768,128]{1,0:T(8,128)(2,1)S(1)}, u32[]{:S(2)}, u32[]{:S(2)}) %collective-permute-start.18) | collective-permute-done | bytes 196640 | tf_op jit(solution)/shard_map/ppermute | solution.py:143
  143.4 0.8 collective-permute-start.13
  144.2 2.6 %collective-permute-start.20 = (bf16[768,128]{1,0:T(8,128)(2,1)S(1)}, bf16[768,128]{1,0:T(8,128)(2,1)}, u32[]{:S(2)}, u32[]{:S(2)}) collective-permute-start(bf16[768,128]{1,0:T(8,128)(2,1)S(1)} %collective-permute-done.18.refs_12_), channel_id=1, source_target_pairs={{0,96},{32,0},{64,32},{96,64},{128,224},{160,128},{192,160},{224,1... | collective-permute-start | bytes 589832 | tf_op jit(solution)/shard_map/ppermute | solution.py:143
  146.9 0.8 collective-permute-done.12.refs_5_
  148.3 2.6 %collective-permute-done.19.refs_13_ = bf16[768,128]{1,0:T(8,128)(2,1)} collective-permute-done((bf16[768,128]{1,0:T(8,128)(2,1)S(1)}, bf16[768,128]{1,0:T(8,128)(2,1)}, u32[]{:S(2)}, u32[]{:S(2)}) %collective-permute-start.19) | collective-permute-done | bytes 196640 | tf_op jit(solution)/shard_map/ppermute | solution.py:143
  150.9 0.8 collective-permute-done.13.refs_6_
  152.5 3.5 %collective-permute-done.14.refs_7_ = bf16[768,128]{1,0:T(8,128)(2,1)} collective-permute-done((bf16[768,128]{1,0:T(8,128)(2,1)}, bf16[768,128]{1,0:T(8,128)(2,1)}, u32[]{:S(2)}, u32[]{:S(2)}) %collective-permute-start.14) | collective-permute-done | bytes 196640 | tf_op jit(solution)/shard_map/ppermute | solution.py:143
  156.1 0.9 collective-permute-done.21.refs_15_
  157.0 1.5 copy-done.2
  158.5 6.6 %shard_map.124 = (bf16[768,896]{1,0:T(8,128)(2,1)}, bf16[768,1024]{1,0:T(8,128)(2,1)}, bf16[768,1024]{1,0:T(8,128)(2,1)}) custom-call(s32[8]{0:T(128)S(1)} %add.152.tab, bf16[768,128]{1,0:T(8,128)(2,1)} %copy-done.13, bf16[768,128]{1,0:T(8,128)(2,1)} %copy-done.21, bf16[768,128]{1,0:T(8,128)(2,1)} %copy-done.22, ...), custom_call_target="tpu_custom_call" | custom-call | tf_op jit(solution)/shard_map/pallas_call | solution.py:44
  165.2 14.4 %all-to-all-start.2 = ((bf16[32,24,896]{2,1,0:T(8,128)(2,1)}), bf16[32,24,896]{2,1,0:T(8,128)(2,1)S(1)}, u32[]{:S(2)}, u32[]{:S(2)}) async-start(bf16[32,24,896]{2,1,0:T(8,128)(2,1)} %bitcast.89), calls=%async_computation.2 | async-start | bytes 2752512 | tf_op jit(solution)/shard_map/all_to_all | solution.py:202
  179.7 2.7 %collective-permute-start.24 = (bf16[768,128]{1,0:T(8,128)(2,1)S(1)}, bf16[768,128]{1,0:T(8,128)(2,1)S(1)}, u32[]{:S(2)}, u32[]{:S(2)}) collective-permute-start(bf16[768,128]{1,0:T(8,128)(2,1)S(1)} %get-tuple-element.40.refs_0_), channel_id=1, source_target_pairs={{0,96},{32,0},{64,32},{96,64},{128,224},{160,128},{192,160},{224,1... | collective-permute-start | bytes 589832 | tf_op jit(solution)/shard_map/ppermute | solution.py:143
  182.4 2.7 %collective-permute-start.28 = (bf16[768,128]{1,0:T(8,128)(2,1)}, bf16[768,128]{1,0:T(8,128)(2,1)S(1)}, u32[]{:S(2)}, u32[]{:S(2)}) collective-permute-start(bf16[768,128]{1,0:T(8,128)(2,1)} %collective-permute-done.22.refs_5_), channel_id=1, source_target_pairs={{0,96},{32,0},{64,32},{96,64},{128,224},{160,128},{192,160},{224,1... | collective-permute-start | bytes 589832 | tf_op jit(solution)/shard_map/ppermute | solution.py:143
  185.0 4.8 %convert_bitcast_fusion.2 = bf16[1,896,1024]{2,1,0:T(8,128)(2,1)} fusion(bf16[768,896]{1,0:T(8,128)(2,1)} %bitcast.3.x_ref, bf16[768,1024]{1,0:T(8,128)(2,1)} %get-tuple-element.38), kind=kOutput, calls=%fused_computation.2 | convolution fusion | flops 1410203648 | bytes 4784128 | tf_op jit(solution)/shard_map/dot_general | solution.py:58
  190.0 2.7 %collective-permute-start.26 = (bf16[384,128]{1,0:T(8,128)(2,1)S(1)}, bf16[384,128]{1,0:T(8,128)(2,1)S(1)}, u32[]{:S(2)}, u32[]{:S(2)}) collective-permute-start(bf16[384,128]{1,0:T(8,128)(2,1)S(1)} %slice.103), channel_id=1, source_target_pairs={{0,96},{32,0},{64,32},{96,64},{128,224},{160,128},{192,160},{224,1... | collective-permute-start | bytes 294920 | tf_op jit(solution)/shard_map/ppermute | solution.py:143
  192.8 2.7 %collective-permute-start.30 = (bf16[384,128]{1,0:T(8,128)(2,1)S(1)}, bf16[384,128]{1,0:T(8,128)(2,1)S(1)}, u32[]{:S(2)}, u32[]{:S(2)}) collective-permute-start(bf16[384,128]{1,0:T(8,128)(2,1)S(1)} %slice.105), channel_id=1, source_target_pairs={{0,96},{32,0},{64,32},{96,64},{128,224},{160,128},{192,160},{224,1... | collective-permute-start | bytes 294920 | tf_op jit(solution)/shard_map/ppermute | solution.py:143
  195.6 4.2 %convert_bitcast_fusion.1 = bf16[1,896,1024]{2,1,0:T(8,128)(2,1)} fusion(bf16[768,896]{1,0:T(8,128)(2,1)} %bitcast.3.x_ref, bf16[768,1024]{1,0:T(8,128)(2,1)S(1)} %copy-done.33), kind=kOutput, calls=%fused_computation.1 | convolution fusion | flops 1410203648 | bytes 4784128 | tf_op jit(solution)/shard_map/dot_general | solution.py:58
  201.2 3.1 %shard_map.126 = bf16[768,1024]{1,0:T(8,128)(2,1)} custom-call(s32[8]{0:T(128)S(1)} %add.152.tab, bf16[768,128]{1,0:T(8,128)(2,1)} %copy-done.15, bf16[768,128]{1,0:T(8,128)(2,1)} %copy-done.16, bf16[768,128]{1,0:T(8,128)(2,1)} %copy-done.17, bf16[384,128]{1,0:T(8,128)(2,1)} %copy-done.28, bf16[384,128]{1,0:T(8,128)(2,1)} %copy-done.29, ...), custom_call_target="tpu_custom_call" | custom-call | tf_op jit(solution)/shard_map/pallas_call | solution.py:44
  204.3 4.5 %convert_bitcast_fusion = bf16[1,1024,896]{2,1,0:T(8,128)(2,1)} fusion(bf16[768,1024]{1,0:T(8,128)(2,1)} %shard_map.126, bf16[768,896]{1,0:T(8,128)(2,1)S(1)} %bitcast.87), kind=kOutput, calls=%fused_computation | convolution fusion | flops 1410203648 | bytes 4784128 | tf_op jit(solution)/shard_map/dot_general | solution.py:58
  208.7 6.2 %all-to-all-done.2 = bf16[32,24,896]{2,1,0:T(8,128)(2,1)S(1)} async-done(((bf16[32,24,896]{2,1,0:T(8,128)(2,1)}), bf16[32,24,896]{2,1,0:T(8,128)(2,1)S(1)}, u32[]{:S(2)}, u32[]{:S(2)}) %all-to-all-start.2) | async-done | bytes 1376288 | tf_op jit(solution)/shard_map/all_to_all | solution.py:202
  214.9 1.1 copy-done.11
  216.0 2.6 %shard_map.125 = bf16[128,896]{1,0:T(8,128)(2,1)} custom-call(f32[768,128]{1,0:T(8,128)} %copy-done.4, bf16[768,896]{1,0:T(8,128)(2,1)} %bitcast.88), custom_call_target="tpu_custom_call" | custom-call | tf_op jit(solution)/shard_map/pallas_call | solution.py:44
  (111 shorter events, 8.7 us)
Async XLA Ops:
  0.6 16.9 %copy-start.5 = (bf16[128,896]{1,0:T(8,128)(2,1)S(1)}, bf16[128,896]{1,0:T(8,128)(2,1)}, u32[]{:S(2)}) copy-start(bf16[128,896]{1,0:T(8,128)(2,1)} %cot_ref.1) | copy-start | bytes 688132
  4.7 14.9 %copy-start.4 = (f32[768,128]{1,0:T(8,128)}, f32[768,128]{1,0:T(8,128)S(1)}, u32[]{:S(2)}) copy-start(f32[768,128]{1,0:T(8,128)S(1)} %get-tuple-element.23.sel_ref) | copy-start | bytes 1179652
  4.7 47.8 %all-to-all-start = ((bf16[32,24,896]{2,1,0:T(8,128)(2,1)}), bf16[32,24,896]{2,1,0:T(8,128)(2,1)}, u32[]{:S(2)}, u32[]{:S(2)}) async-start(bf16[32,24,896]{2,1,0:T(8,128)(2,1)} %bitcast.2), calls=%async_computation | async-start | bytes 2752512 | tf_op jit(solution)/shard_map/all_to_all | solution.py:202
  19.7 39.1 %copy-start.32 = (s32[4]{0:T(128)S(1)}, s32[4]{0:T(128)}, u32[]{:S(2)}) copy-start(s32[4]{0:T(128)} %constant.67.clone) | copy-start | bytes 52
  19.7 39.3 %copy-start = (bf16[1,896,1024]{2,1,0:T(8,128)(2,1)S(1)}, bf16[1,896,1024]{2,1,0:T(8,128)(2,1)}, u32[]{:S(2)}) copy-start(bf16[1,896,1024]{2,1,0:T(8,128)(2,1)} %param.13) | copy-start | bytes 5505028
  52.6 41.6 %all-to-all-start.1 = ((bf16[32,24,896]{2,1,0:T(8,128)(2,1)}), bf16[32,24,896]{2,1,0:T(8,128)(2,1)S(1)}, u32[]{:S(2)}, u32[]{:S(2)}) async-start(bf16[32,24,896]{2,1,0:T(8,128)(2,1)} %bitcast.4), calls=%async_computation.1 | async-start | bytes 2752512 | tf_op jit(solution)/shard_map/all_to_all | solution.py:202
  67.1 37.5 %collective-permute-start.6 = (bf16[2,768,256]{2,1,0:T(8,128)(2,1)}, bf16[2,768,256]{2,1,0:T(8,128)(2,1)}, u32[]{:S(2)}, u32[]{:S(2)}) collective-permute-start(bf16[2,768,256]{2,1,0:T(8,128)(2,1)} %get-tuple-element.35), channel_id=1, source_target_pairs={{0,96},{32,0},{64,32},{96,64},{128,224},{160,128},{192,160},{224,1... | collective-permute-start | bytes 2359304 | tf_op jit(solution)/shard_map/ppermute | solution.py:143
  69.6 35.4 %collective-permute-start.5 = (bf16[2,768,256]{2,1,0:T(8,128)(2,1)}, bf16[2,768,256]{2,1,0:T(8,128)(2,1)}, u32[]{:S(2)}, u32[]{:S(2)}) collective-permute-start(bf16[2,768,256]{2,1,0:T(8,128)(2,1)} %get-tuple-element.34), channel_id=1, source_target_pairs={{0,64},{32,96},{64,0},{96,32},{128,192},{160,224},{192,128},{224,1... | collective-permute-start | bytes 2359304 | tf_op jit(solution)/shard_map/ppermute | solution.py:143
  70.2 37.6 %collective-permute-start.4 = (bf16[2,768,256]{2,1,0:T(8,128)(2,1)}, bf16[2,768,256]{2,1,0:T(8,128)(2,1)}, u32[]{:S(2)}, u32[]{:S(2)}) collective-permute-start(bf16[2,768,256]{2,1,0:T(8,128)(2,1)} %get-tuple-element.33), channel_id=1, source_target_pairs={{0,32},{32,64},{64,96},{96,0},{128,160},{160,192},{192,224},{224,1... | collective-permute-start | bytes 2359304 | tf_op jit(solution)/shard_map/ppermute | solution.py:143
  96.8 11.0 %copy-start.14 = (bf16[2,768,256]{2,1,0:T(8,128)(2,1)S(1)}, bf16[2,768,256]{2,1,0:T(8,128)(2,1)}, u32[]{:S(2)}) copy-start(bf16[2,768,256]{2,1,0:T(8,128)(2,1)} %get-tuple-element.32) | copy-start | bytes 2359300
  101.6 23.7 %copy-start.20 = (bf16[2,768,128]{2,1,0:T(8,128)(2,1)S(1)}, bf16[2,768,128]{2,1,0:T(8,128)(2,1)}, u32[]{:S(2)}) copy-start(bf16[2,768,128]{2,1,0:T(8,128)(2,1)} %get-tuple-element.27) | copy-start | bytes 1179652
  101.6 10.2 %collective-permute-start.2 = (bf16[2,768,128]{2,1,0:T(8,128)(2,1)}, bf16[2,768,128]{2,1,0:T(8,128)(2,1)S(1)}, u32[]{:S(2)}, u32[]{:S(2)}) collective-permute-start(bf16[2,768,128]{2,1,0:T(8,128)(2,1)} %get-tuple-element.30), channel_id=1, source_target_pairs={{0,96},{32,0},{64,32},{96,64},{128,224},{160,128},{192,160},{224,1... | collective-permute-start | bytes 1179656 | tf_op jit(solution)/shard_map/ppermute | solution.py:143
  104.1 10.3 %collective-permute-start.1 = (bf16[2,768,128]{2,1,0:T(8,128)(2,1)}, bf16[2,768,128]{2,1,0:T(8,128)(2,1)S(1)}, u32[]{:S(2)}, u32[]{:S(2)}) collective-permute-start(bf16[2,768,128]{2,1,0:T(8,128)(2,1)} %get-tuple-element.29), channel_id=1, source_target_pairs={{0,64},{32,96},{64,0},{96,32},{128,192},{160,224},{192,128},{224,1... | collective-permute-start | bytes 1179656 | tf_op jit(solution)/shard_map/ppermute | solution.py:143
  104.7 20.7 %collective-permute-start = (bf16[2,768,128]{2,1,0:T(8,128)(2,1)}, bf16[2,768,128]{2,1,0:T(8,128)(2,1)S(1)}, u32[]{:S(2)}, u32[]{:S(2)}) collective-permute-start(bf16[2,768,128]{2,1,0:T(8,128)(2,1)} %get-tuple-element.28), channel_id=1, source_target_pairs={{0,32},{32,64},{64,96},{96,0},{128,160},{160,192},{192,224},{224,1... | collective-permute-start | bytes 1179656 | tf_op jit(solution)/shard_map/ppermute | solution.py:143
  109.2 16.4 %collective-permute-start.7 = (bf16[768,256]{1,0:T(8,128)(2,1)S(1)}, bf16[768,256]{1,0:T(8,128)(2,1)S(1)}, u32[]{:S(2)}, u32[]{:S(2)}) collective-permute-start(bf16[768,256]{1,0:T(8,128)(2,1)S(1)} %fusion), channel_id=1, source_target_pairs={{0,128},{32,160},{64,192},{96,224},{128,0},{160,32},{192,64},{224,... | collective-permute-start | bytes 1179656 | tf_op jit(solution)/shard_map/ppermute | solution.py:143
  125.4 6.1 %collective-permute-start.3 = (bf16[768,128]{1,0:T(8,128)(2,1)S(1)}, bf16[768,128]{1,0:T(8,128)(2,1)S(1)}, u32[]{:S(2)}, u32[]{:S(2)}) collective-permute-start(bf16[768,128]{1,0:T(8,128)(2,1)S(1)} %fusion.2), channel_id=1, source_target_pairs={{0,128},{32,160},{64,192},{96,224},{128,0},{160,32},{192,64},{224,... | collective-permute-start | bytes 589832 | tf_op jit(solution)/shard_map/ppermute | solution.py:143
  131.8 25.1 %copy-start.12 = (bf16[768,128]{1,0:T(8,128)(2,1)}, bf16[768,128]{1,0:T(8,128)(2,1)S(1)}, u32[]{:S(2)}) copy-start(bf16[768,128]{1,0:T(8,128)(2,1)S(1)} %get-tuple-element.42.refs_8_) | copy-start | bytes 589828
  131.8 25.1 %copy-start.13 = (bf16[768,128]{1,0:T(8,128)(2,1)}, bf16[768,128]{1,0:T(8,128)(2,1)S(1)}, u32[]{:S(2)}) copy-start(bf16[768,128]{1,0:T(8,128)(2,1)S(1)} %get-tuple-element.43.refs_0_) | copy-start | bytes 589828
  131.9 47.8 %copy-start.15 = (bf16[768,128]{1,0:T(8,128)(2,1)}, bf16[768,128]{1,0:T(8,128)(2,1)S(1)}, u32[]{:S(2)}) copy-start(bf16[768,128]{1,0:T(8,128)(2,1)S(1)} %get-tuple-element.40.refs_0_) | copy-start | bytes 589828
  131.9 6.3 %collective-permute-start.8 = (bf16[768,128]{1,0:T(8,128)(2,1)S(1)}, bf16[768,128]{1,0:T(8,128)(2,1)S(1)}, u32[]{:S(2)}, u32[]{:S(2)}) collective-permute-start(bf16[768,128]{1,0:T(8,128)(2,1)S(1)} %get-tuple-element.43.refs_0_), channel_id=1, source_target_pairs={{0,32},{32,64},{64,96},{96,0},{128,160},{160,192},{192,224},{224,1... | collective-permute-start | bytes 589832 | tf_op jit(solution)/shard_map/ppermute | solution.py:143
  132.0 6.8 %collective-permute-start.9 = (bf16[768,128]{1,0:T(8,128)(2,1)S(1)}, bf16[768,128]{1,0:T(8,128)(2,1)S(1)}, u32[]{:S(2)}, u32[]{:S(2)}) collective-permute-start(bf16[768,128]{1,0:T(8,128)(2,1)S(1)} %get-tuple-element.43.refs_0_), channel_id=1, source_target_pairs={{0,96},{32,0},{64,32},{96,64},{128,224},{160,128},{192,160},{224,1... | collective-permute-start | bytes 589832 | tf_op jit(solution)/shard_map/ppermute | solution.py:143
  134.6 5.1 %collective-permute-start.11 = (bf16[768,128]{1,0:T(8,128)(2,1)S(1)}, bf16[768,128]{1,0:T(8,128)(2,1)S(1)}, u32[]{:S(2)}, u32[]{:S(2)}) collective-permute-start(bf16[768,128]{1,0:T(8,128)(2,1)S(1)} %get-tuple-element.43.refs_0_), channel_id=1, source_target_pairs={{0,128},{32,160},{64,192},{96,224},{128,0},{160,32},{192,64},{224,... | collective-permute-start | bytes 589832 | tf_op jit(solution)/shard_map/ppermute | solution.py:143
  134.9 8.4 %collective-permute-start.18 = (bf16[768,128]{1,0:T(8,128)(2,1)S(1)}, bf16[768,128]{1,0:T(8,128)(2,1)S(1)}, u32[]{:S(2)}, u32[]{:S(2)}) collective-permute-start(bf16[768,128]{1,0:T(8,128)(2,1)S(1)} %get-tuple-element.42.refs_8_), channel_id=1, source_target_pairs={{0,128},{32,160},{64,192},{96,224},{128,0},{160,32},{192,64},{224,... | collective-permute-start | bytes 589832 | tf_op jit(solution)/shard_map/ppermute | solution.py:143
  136.1 7.3 %collective-permute-start.15 = (bf16[768,128]{1,0:T(8,128)(2,1)S(1)}, bf16[768,128]{1,0:T(8,128)(2,1)S(1)}, u32[]{:S(2)}, u32[]{:S(2)}) collective-permute-start(bf16[768,128]{1,0:T(8,128)(2,1)S(1)} %get-tuple-element.42.refs_8_), channel_id=1, source_target_pairs={{0,32},{32,64},{64,96},{96,0},{128,160},{160,192},{192,224},{224,1... | collective-permute-start | bytes 589832 | tf_op jit(solution)/shard_map/ppermute | solution.py:143
  138.2 18.8 %copy-start.21 = (bf16[768,128]{1,0:T(8,128)(2,1)}, bf16[768,128]{1,0:T(8,128)(2,1)S(1)}, u32[]{:S(2)}) copy-start(bf16[768,128]{1,0:T(8,128)(2,1)S(1)} %collective-permute-done.8.refs_1_) | copy-start | bytes 589828
  138.2 6.0 %collective-permute-start.16 = (bf16[768,128]{1,0:T(8,128)(2,1)S(1)}, bf16[768,128]{1,0:T(8,128)(2,1)}, u32[]{:S(2)}, u32[]{:S(2)}) collective-permute-start(bf16[768,128]{1,0:T(8,128)(2,1)S(1)} %get-tuple-element.42.refs_8_), channel_id=1, source_target_pairs={{0,96},{32,0},{64,32},{96,64},{128,224},{160,128},{192,160},{224,1... | collective-permute-start | bytes 589832 | tf_op jit(solution)/shard_map/ppermute | solution.py:143
  138.8 18.2 %copy-start.22 = (bf16[768,128]{1,0:T(8,128)(2,1)}, bf16[768,128]{1,0:T(8,128)(2,1)S(1)}, u32[]{:S(2)}) copy-start(bf16[768,128]{1,0:T(8,128)(2,1)S(1)} %collective-permute-done.9.refs_2_) | copy-start | bytes 589828
  138.8 8.0 %collective-permute-start.10 = (bf16[768,128]{1,0:T(8,128)(2,1)S(1)}, bf16[768,128]{1,0:T(8,128)(2,1)}, u32[]{:S(2)}, u32[]{:S(2)}) collective-permute-start(bf16[768,128]{1,0:T(8,128)(2,1)S(1)} %collective-permute-done.8.refs_1_), channel_id=1, source_target_pairs={{0,32},{32,64},{64,96},{96,0},{128,160},{160,192},{192,224},{224,1... | collective-permute-start | bytes 589832 | tf_op jit(solution)/shard_map/ppermute | solution.py:143
  139.7 17.3 %copy-start.23 = (bf16[768,128]{1,0:T(8,128)(2,1)}, bf16[768,128]{1,0:T(8,128)(2,1)S(1)}, u32[]{:S(2)}) copy-start(bf16[768,128]{1,0:T(8,128)(2,1)S(1)} %collective-permute-done.11.refs_4_) | copy-start | bytes 589828
  139.7 8.0 %collective-permute-start.12 = (bf16[768,128]{1,0:T(8,128)(2,1)S(1)}, bf16[768,128]{1,0:T(8,128)(2,1)S(1)}, u32[]{:S(2)}, u32[]{:S(2)}) collective-permute-start(bf16[768,128]{1,0:T(8,128)(2,1)S(1)} %collective-permute-done.8.refs_1_), channel_id=1, source_target_pairs={{0,128},{32,160},{64,192},{96,224},{128,0},{160,32},{192,64},{224,... | collective-permute-start | bytes 589832 | tf_op jit(solution)/shard_map/ppermute | solution.py:143
  143.3 13.7 %copy-start.24 = (bf16[768,128]{1,0:T(8,128)(2,1)}, bf16[768,128]{1,0:T(8,128)(2,1)S(1)}, u32[]{:S(2)}) copy-start(bf16[768,128]{1,0:T(8,128)(2,1)S(1)} %collective-permute-done.18.refs_12_) | copy-start | bytes 589828
  143.3 7.6 %collective-permute-start.19 = (bf16[768,128]{1,0:T(8,128)(2,1)S(1)}, bf16[768,128]{1,0:T(8,128)(2,1)}, u32[]{:S(2)}, u32[]{:S(2)}) collective-permute-start(bf16[768,128]{1,0:T(8,128)(2,1)S(1)} %collective-permute-done.18.refs_12_), channel_id=1, source_target_pairs={{0,32},{32,64},{64,96},{96,0},{128,160},{160,192},{192,224},{224,1... | collective-permute-start | bytes 589832 | tf_op jit(solution)/shard_map/ppermute | solution.py:143
  143.3 13.7 %copy-start.25 = (bf16[768,128]{1,0:T(8,128)(2,1)}, bf16[768,128]{1,0:T(8,128)(2,1)S(1)}, u32[]{:S(2)}) copy-start(bf16[768,128]{1,0:T(8,128)(2,1)S(1)} %collective-permute-done.15.refs_9_) | copy-start | bytes 589828
  143.4 8.4 %collective-permute-start.13 = (bf16[768,128]{1,0:T(8,128)(2,1)S(1)}, bf16[768,128]{1,0:T(8,128)(2,1)S(1)}, u32[]{:S(2)}, u32[]{:S(2)}) collective-permute-start(bf16[768,128]{1,0:T(8,128)(2,1)S(1)} %collective-permute-done.9.refs_2_), channel_id=1, source_target_pairs={{0,128},{32,160},{64,192},{96,224},{128,0},{160,32},{192,64},{224,... | collective-permute-start | bytes 589832 | tf_op jit(solution)/shard_map/ppermute | solution.py:143
  144.2 8.3 %collective-permute-start.20 = (bf16[768,128]{1,0:T(8,128)(2,1)S(1)}, bf16[768,128]{1,0:T(8,128)(2,1)}, u32[]{:S(2)}, u32[]{:S(2)}) collective-permute-start(bf16[768,128]{1,0:T(8,128)(2,1)S(1)} %collective-permute-done.18.refs_12_), channel_id=1, source_target_pairs={{0,96},{32,0},{64,32},{96,64},{128,224},{160,128},{192,160},{224,1... | collective-permute-start | bytes 589832 | tf_op jit(solution)/shard_map/ppermute | solution.py:143
  146.8 5.8 %collective-permute-start.17 = (bf16[768,128]{1,0:T(8,128)(2,1)}, bf16[768,128]{1,0:T(8,128)(2,1)}, u32[]{:S(2)}, u32[]{:S(2)}) collective-permute-start(bf16[768,128]{1,0:T(8,128)(2,1)} %collective-permute-done.16.refs_10_), channel_id=1, source_target_pairs={{0,96},{32,0},{64,32},{96,64},{128,224},{160,128},{192,160},{224,1... | collective-permute-start | bytes 589832 | tf_op jit(solution)/shard_map/ppermute | solution.py:143
  147.7 8.4 %collective-permute-start.14 = (bf16[768,128]{1,0:T(8,128)(2,1)}, bf16[768,128]{1,0:T(8,128)(2,1)}, u32[]{:S(2)}, u32[]{:S(2)}) collective-permute-start(bf16[768,128]{1,0:T(8,128)(2,1)} %collective-permute-done.10.refs_3_), channel_id=1, source_target_pairs={{0,128},{32,160},{64,192},{96,224},{128,0},{160,32},{192,64},{224,... | collective-permute-start | bytes 589832 | tf_op jit(solution)/shard_map/ppermute | solution.py:143
  150.9 6.0 %collective-permute-start.21 = (bf16[768,128]{1,0:T(8,128)(2,1)}, bf16[768,128]{1,0:T(8,128)(2,1)}, u32[]{:S(2)}, u32[]{:S(2)}) collective-permute-start(bf16[768,128]{1,0:T(8,128)(2,1)} %collective-permute-done.19.refs_13_), channel_id=1, source_target_pairs={{0,32},{32,64},{64,96},{96,0},{128,160},{160,192},{192,224},{224,1... | collective-permute-start | bytes 589832 | tf_op jit(solution)/shard_map/ppermute | solution.py:143
  151.8 13.4 %collective-permute-start.22 = (bf16[768,128]{1,0:T(8,128)(2,1)S(1)}, bf16[768,128]{1,0:T(8,128)(2,1)}, u32[]{:S(2)}, u32[]{:S(2)}) collective-permute-start(bf16[768,128]{1,0:T(8,128)(2,1)S(1)} %get-tuple-element.40.refs_0_), channel_id=1, source_target_pairs={{0,128},{32,160},{64,192},{96,224},{128,0},{160,32},{192,64},{224,... | collective-permute-start | bytes 589832 | tf_op jit(solution)/shard_map/ppermute | solution.py:143
  165.2 49.7 %all-to-all-start.2 = ((bf16[32,24,896]{2,1,0:T(8,128)(2,1)}), bf16[32,24,896]{2,1,0:T(8,128)(2,1)S(1)}, u32[]{:S(2)}, u32[]{:S(2)}) async-start(bf16[32,24,896]{2,1,0:T(8,128)(2,1)} %bitcast.89), calls=%async_computation.2 | async-start | bytes 2752512 | tf_op jit(solution)/shard_map/all_to_all | solution.py:202
  179.6 10.2 %collective-permute-start.23 = (bf16[768,128]{1,0:T(8,128)(2,1)S(1)}, bf16[768,128]{1,0:T(8,128)(2,1)S(1)}, u32[]{:S(2)}, u32[]{:S(2)}) collective-permute-start(bf16[768,128]{1,0:T(8,128)(2,1)S(1)} %get-tuple-element.40.refs_0_), channel_id=1, source_target_pairs={{0,32},{32,64},{64,96},{96,0},{128,160},{160,192},{192,224},{224,1... | collective-permute-start | bytes 589832 | tf_op jit(solution)/shard_map/ppermute | solution.py:143
  179.7 10.2 %collective-permute-start.24 = (bf16[768,128]{1,0:T(8,128)(2,1)S(1)}, bf16[768,128]{1,0:T(8,128)(2,1)S(1)}, u32[]{:S(2)}, u32[]{:S(2)}) collective-permute-start(bf16[768,128]{1,0:T(8,128)(2,1)S(1)} %get-tuple-element.40.refs_0_), channel_id=1, source_target_pairs={{0,96},{32,0},{64,32},{96,64},{128,224},{160,128},{192,160},{224,1... | collective-permute-start | bytes 589832 | tf_op jit(solution)/shard_map/ppermute | solution.py:143
  182.4 10.3 %collective-permute-start.27 = (bf16[768,128]{1,0:T(8,128)(2,1)}, bf16[768,128]{1,0:T(8,128)(2,1)S(1)}, u32[]{:S(2)}, u32[]{:S(2)}) collective-permute-start(bf16[768,128]{1,0:T(8,128)(2,1)} %collective-permute-done.22.refs_5_), channel_id=1, source_target_pairs={{0,32},{32,64},{64,96},{96,0},{128,160},{160,192},{192,224},{224,1... | collective-permute-start | bytes 589832 | tf_op jit(solution)/shard_map/ppermute | solution.py:143
  182.4 10.4 %collective-permute-start.28 = (bf16[768,128]{1,0:T(8,128)(2,1)}, bf16[768,128]{1,0:T(8,128)(2,1)S(1)}, u32[]{:S(2)}, u32[]{:S(2)}) collective-permute-start(bf16[768,128]{1,0:T(8,128)(2,1)} %collective-permute-done.22.refs_5_), channel_id=1, source_target_pairs={{0,96},{32,0},{64,32},{96,64},{128,224},{160,128},{192,160},{224,1... | collective-permute-start | bytes 589832 | tf_op jit(solution)/shard_map/ppermute | solution.py:143
  189.8 10.0 %collective-permute-start.25 = (bf16[384,128]{1,0:T(8,128)(2,1)S(1)}, bf16[384,128]{1,0:T(8,128)(2,1)S(1)}, u32[]{:S(2)}, u32[]{:S(2)}) collective-permute-start(bf16[384,128]{1,0:T(8,128)(2,1)S(1)} %slice.102), channel_id=1, source_target_pairs={{0,32},{32,64},{64,96},{96,0},{128,160},{160,192},{192,224},{224,1... | collective-permute-start | bytes 294920 | tf_op jit(solution)/shard_map/ppermute | solution.py:143
  190.0 9.8 %collective-permute-start.26 = (bf16[384,128]{1,0:T(8,128)(2,1)S(1)}, bf16[384,128]{1,0:T(8,128)(2,1)S(1)}, u32[]{:S(2)}, u32[]{:S(2)}) collective-permute-start(bf16[384,128]{1,0:T(8,128)(2,1)S(1)} %slice.103), channel_id=1, source_target_pairs={{0,96},{32,0},{64,32},{96,64},{128,224},{160,128},{192,160},{224,1... | collective-permute-start | bytes 294920 | tf_op jit(solution)/shard_map/ppermute | solution.py:143
  192.7 7.1 %collective-permute-start.29 = (bf16[384,128]{1,0:T(8,128)(2,1)S(1)}, bf16[384,128]{1,0:T(8,128)(2,1)S(1)}, u32[]{:S(2)}, u32[]{:S(2)}) collective-permute-start(bf16[384,128]{1,0:T(8,128)(2,1)S(1)} %slice.104), channel_id=1, source_target_pairs={{0,32},{32,64},{64,96},{96,0},{128,160},{160,192},{192,224},{224,1... | collective-permute-start | bytes 294920 | tf_op jit(solution)/shard_map/ppermute | solution.py:143
  192.8 7.0 %collective-permute-start.30 = (bf16[384,128]{1,0:T(8,128)(2,1)S(1)}, bf16[384,128]{1,0:T(8,128)(2,1)S(1)}, u32[]{:S(2)}, u32[]{:S(2)}) collective-permute-start(bf16[384,128]{1,0:T(8,128)(2,1)S(1)} %slice.105), channel_id=1, source_target_pairs={{0,96},{32,0},{64,32},{96,64},{128,224},{160,128},{192,160},{224,1... | collective-permute-start | bytes 294920 | tf_op jit(solution)/shard_map/ppermute | solution.py:143
  (20 other events, 65.9 us)

commit v3 on v2

v3 whole, which is shorter than its diff:
```python
import functools

import jax
import jax.numpy as jnp
from jax import lax
from jax.experimental import pallas as pl
from jax.experimental.pallas import tpu as pltpu
from jax.sharding import PartitionSpec as P

bf16 = jnp.bfloat16
f32 = jnp.float32
NX = 4
NZ = 2
BLK = 384


def call(body, ins, outs, scratch=(), steps=1, n_smem=0, hbm=(), out_hbm=True):
    def whole(shape):
        return pl.BlockSpec(shape, lambda i, n=len(shape): (0,) * n)

    def rowwise(shape, axis):
        block = tuple(v // steps if k == axis else v for k, v in enumerate(shape))
        return pl.BlockSpec(block, lambda i, n=len(shape), axis=axis: tuple(i if k == axis else 0 for k in range(n)))

    def run(*args):
        specs = [pl.BlockSpec(memory_space=pltpu.SMEM)] * n_smem
        args = list(args)
        for k in hbm:
            args[n_smem + k] = pltpu.with_memory_space_constraint(args[n_smem + k], pltpu.HBM)
        for v, axis in zip(args[n_smem:], ins, strict=True):
            specs.append(whole(v.shape) if axis is None else rowwise(v.shape, axis))
        return pl.pallas_call(
            body,
            grid=(steps,),
            out_shape=tuple((pltpu.HBM if hbm and out_hbm else jax.ShapeDtypeStruct)(s, d) for s, d, _ in outs),
            in_specs=specs,
            out_specs=tuple(whole(s) if axis is None else rowwise(s, axis) for s, _, axis in outs),
            scratch_shapes=list(scratch),
            compiler_params=pltpu.CompilerParams(vmem_limit_bytes=24 * 1024 * 1024),
        )(*args)

    return run


def dot(a, b, ca, cb):
    return lax.dot_general(a, b, (((ca,), (cb,)), ((), ())), preferred_element_type=f32)


def prep_body(routes_ref, weights_ref, tokens_ref, x_ref, sel_ref, w_ref, sel_s, *, experts, cap):
    top, tok = routes_ref.shape
    e_id = lax.broadcasted_iota(jnp.int32, (experts, tok), 0)
    names = jnp.zeros((experts, tok), f32)
    scale = jnp.zeros((experts, tok), f32)
    for k in range(top):
        hit = routes_ref[k : k + 1, :] == e_id
        names = jnp.where(hit, 1.0, names)
        scale = jnp.where(hit, weights_ref[k : k + 1, :], scale)
    row = lax.broadcasted_iota(jnp.int32, (tok, tok), 0)
    col = lax.broadcasted_iota(jnp.int32, (tok, tok), 1)
    earlier = jnp.where(row < col, 1.0, 0.0).astype(bf16)
    rank = dot(names.astype(bf16), earlier, 1, 0)
    rank = jnp.where(names > 0.0, rank, -1.0)
    slot = lax.broadcasted_iota(jnp.int32, (cap, tok), 0).astype(f32)
    for e in range(experts):
        here = rank[e : e + 1, :] == slot
        sel_s[e * cap : (e + 1) * cap, :] = jnp.where(here, 1.0, 0.0)
        w_ref[e * cap : (e + 1) * cap, :] = jnp.sum(
            jnp.where(here, scale[e : e + 1, :], 0.0), axis=1, keepdims=True
        )
    sel = sel_s[...].astype(bf16)
    sel_ref[...] = sel
    x_ref[...] = dot(sel, tokens_ref[...], 1, 0).astype(bf16)


def scale_body(sel_ref, w_ref, cot_ref, s_ref):
    s_ref[...] = (dot(sel_ref[...], cot_ref[...], 1, 0) * w_ref[...]).astype(bf16)


def lanes(tab, j):
    return pl.ds(pl.multiple_of(tab[j] * 128, 128), 128)


def beside(a, b):
    return jnp.concatenate([a, b], axis=1)


def gate_up_body(tab, x_ref, wg_ref, wu_ref, *outs):
    for t in range(NZ):
        for s, o in enumerate(outs):
            c = lanes(tab, t * NX + s)
            o[t] = dot(x_ref[...], beside(wg_ref[:, c], wu_ref[:, c]), 1, 0).astype(bf16)


def dhid_body(tab, s_ref, wd_ref, *refs):
    by_s, by_t, d_s = refs[:NX], refs[NX : NX + NZ], refs[-1]
    d_s[...] = dot(s_ref[...], wd_ref[...], 1, 1).astype(bf16)

    @pl.when(pl.program_id(0) == 0)
    def _():
        for t in range(NZ):
            for s in range(NX):
                by_s[s][t] = d_s[:, lanes(tab, t * NX + s)]

    @pl.when(pl.program_id(0) == 1)
    def _():
        for t in range(NZ):
            for s in range(NX):
                by_t[t][s] = d_s[:, lanes(tab, t * NX + s)]


def back_body(tab, *refs):
    gates, ups = refs[: NZ * NX], refs[NZ * NX : 2 * NZ * NX]
    wg_ref, wu_ref, back_ref, pg_ref, pu_ref = refs[-5:]
    total = None
    for q in range(NZ * NX):
        c = lanes(tab, q)
        g, u = gates[q][...], ups[q][...]
        pg_ref[:, c] = g
        pu_ref[:, c] = u
        t = dot(beside(g, u), beside(wg_ref[:, c], wu_ref[:, c]), 1, 1)
        total = t if total is None else total + t
    back_ref[...] = total.astype(bf16)


def hid_body(tab, *refs):
    own, left, right, far_0, far_1, o_ref = refs
    for z in range(NZ):
        for q, p in enumerate((own, left, right)):
            o_ref[:, lanes(tab, 4 * z + q)] = p[z]
    o_ref[:, lanes(tab, 3)] = far_0[...]
    o_ref[:, lanes(tab, 4 + 3)] = far_1[...]


def combine_body(sel_ref, ret_ref, o_ref):
    o_ref[...] = dot(sel_ref[...], ret_ref[...], 0, 0).astype(bf16)


def dp_perm(dz, dx):
    return [
        (z * NX + x, ((z + dz) % NZ) * NX + (x + dx) % NX) for z in range(NZ) for x in range(NX)
    ]


def move(v, dz, dx):
    return lax.ppermute(v, "dp", dp_perm(dz, dx))


def add(*parts):
    return sum(p.astype(f32) for p in parts)


def send_x(by_s):
    return [by_s[0]] + [move(by_s[s], 0, s) for s in range(1, NX)]


def sum_x_first(parts):
    other = move(add(*(p[1] for p in parts)).astype(bf16), 1, 0)
    return add(other, *(p[0] for p in parts))


def sum_z_first(by_t):
    other = move(by_t[1], 1, 0)
    sums = [add(by_t[0][s], other[s]) for s in range(NX)]
    return add(sums[0], *(move(sums[s].astype(bf16), 0, s) for s in range(1, NX)))


def gather(gate, up):
    gl, gr = move(gate, 0, 1), move(gate, 0, NX - 1)
    uz = move(up, 1, 0)
    ul, ur = move(up, 0, 1), move(up, 0, NX - 1)
    gates = [gate, gl, gr, move(gl, 0, 1)]
    gates += [move(v, 1, 0) for v in gates]
    uzl, uzr = move(uz, 0, 1), move(uz, 0, NX - 1)
    ups = [up, ul, ur, move(ur, 0, NX - 1), uz, uzl, uzr, move(uzl, 0, 1)]
    return gates + ups


def local(tokens, cotangent, routes, combine_weights, gate_weight, up_weight, down_weight):
    experts = lax.axis_size("expert")
    tok, top = routes.shape
    width = tokens.shape[1]
    hid = gate_weight.shape[2]
    cap = 3 * tok * top // (2 * experts)
    rows = experts * cap
    steps = rows // BLK
    wg, wu, wd = gate_weight[0], up_weight[0], down_weight[0]
    d = lax.axis_index("dp")
    z, x = d // NX, d % NX

    def table(shifts):
        s = jnp.array(shifts, jnp.int32)
        return (((z + jnp.arange(NZ))[:, None] % NZ) * NX + (x + s)[None, :] % NX).reshape(-1)

    dest = table((0, 1, 2, 3))
    orig = table((0, NX - 1, 1, 2))

    slots_x, sel, w_slot = call(
        functools.partial(prep_body, experts=experts, cap=cap),
        [None] * 3,
        [((rows, width), bf16, None), ((rows, tok), bf16, None), ((rows, 1), f32, None)],
        scratch=[pltpu.VMEM((rows, tok), f32)],
        hbm=(0, 1, 2),
        out_hbm=False,
    )(routes.T, combine_weights.T, tokens)
    (send_s,) = call(scale_body, [0, 0, None], [((rows, width), bf16, 0)], steps=steps)(
        sel, w_slot, cotangent
    )

    def a2a(v):
        return lax.all_to_all(
            v.reshape(experts, cap, width), "expert", split_axis=0, concat_axis=0, tiled=True
        ).reshape(rows, width)

    rows_x = a2a(slots_x)
    rows_x, send_s = lax.optimization_barrier((rows_x, send_s))
    gu = call(
        gate_up_body,
        [0, None, None],
        [((NZ, rows, 256), bf16, 1)] * NX,
        steps=steps,
        hbm=(0, 2),
        n_smem=1,
    )(dest, rows_x, wg, wu)
    gu = send_x(gu)
    rows_s = a2a(send_s)
    half = rows // 2
    dh = call(
        dhid_body,
        [0, None],
        [((NZ, half, 128), bf16, None)] * NX + [((NX, half, 128), bf16, None)] * NZ,
        scratch=[pltpu.VMEM((half, hid), bf16)],
        steps=2,
        hbm=(0, 1),
        n_smem=1,
    )(dest, rows_s, wd)
    gu, _ = lax.optimization_barrier((gu, dh[0]))
    gu = sum_x_first(gu)
    gate, upper = gu[:, :128], gu[:, 128:]
    sig = jax.nn.sigmoid(gate)
    act = gate * sig
    hidden = (act * upper).astype(bf16)
    slope = upper * (sig * (1.0 + gate * (1.0 - sig)))
    dh = jnp.concatenate([sum_x_first(send_x(dh[:NX])), sum_z_first(dh[NX:])], axis=0)
    back, pre_gate, pre_up = call(
        back_body,
        [0] * (2 * NZ * NX) + [None, None],
        [((rows, width), bf16, 0), ((rows, hid), bf16, 0), ((rows, hid), bf16, 0)],
        steps=steps,
        hbm=tuple(range(2 * NZ * NX)) + (2 * NZ * NX + 1,),
        n_smem=1,
    )(orig, *gather((dh * slope).astype(bf16), (dh * act).astype(bf16)), wg, wu)
    hidden_z = move(hidden, 1, 0)
    back, hidden, hidden_z = lax.optimization_barrier((back, hidden, hidden_z))
    returned = a2a(back)
    both = jnp.stack([hidden, hidden_z])
    left, right = move(both, 0, 1), move(both, 0, NX - 1)
    (hidden_all,) = call(
        hid_body, [1, 1, 1, 0, 0], [((rows, hid), bf16, 0)], steps=steps, n_smem=1, hbm=tuple(range(5))
    )(orig, both, left, right, move(left[0], 0, 1), move(right[1], 0, NX - 1))
    grad_gate = dot(rows_x, pre_gate, 0, 0).astype(bf16)[None]
    grad_up = dot(rows_x, pre_up, 0, 0).astype(bf16)[None]
    grad_down = dot(hidden_all, rows_s, 0, 0).astype(bf16)[None]
    (grad_tokens,) = call(combine_body, [None, None], [((tok, width), bf16, None)], hbm=(0,))(sel, returned)
    return (grad_tokens, grad_gate, grad_up, grad_down)


def solution(mesh):
    placed = (
        P("expert", "dp"),
        P("expert", "dp"),
        P("expert", None),
        P("expert", None),
        P("expert", "dp", None),
        P("expert", "dp", None),
        P("expert", None, "dp"),
    )
    return jax.shard_map(
        local,
        mesh=mesh,
        in_specs=placed,
        out_specs=(
            P("expert", "dp"),
            P("expert", "dp", None),
            P("expert", "dp", None),
            P("expert", None, "dp"),
        ),
        check_vma=False,
    )
```

time: 219 us -> 217 us (level)
  waiting for transfers between devices: 98.7 us -> 106 us
  local copies, waits for them, and re-layouts: 10.6 us -> 4.46 us
  starting transfers between devices: 63.6 us -> 59.3 us
    unnamed x68 -> x52, local copies, waits for them, and re-layouts: 10.4 us -> 4.26 us
    ppermute x31, starting transfers between devices: 30.2 us -> 25.6 us  [move(): return lax.ppermute(v, 'dp', dp_perm(dz, dx))]
    ppermute x31, waiting for transfers between devices: 36 us -> 40.2 us  [move(): return lax.ppermute(v, 'dp', dp_perm(dz, dx))]
    all_to_all x3, waiting for transfers between devices: 62.7 us -> 65.4 us  [a2a(): lax.all_to_all(v.reshape(experts, cap, width), 'expert', split_axis=0, co...]
  transfers between devices with their start and end apart: 34 -> 34, of which waited for: 15 -> 18; matrix products, arithmetic and copies ran while one was open for 8% -> 8% of each run, Pallas kernels for 11% -> 11%
where the time goes in v3:
time: 217 us; the launch traced here: 216 us
  waiting for transfers between devices  106 us (49%)
  starting transfers between devices  59.3 us (27%)
  Pallas kernels  28.5 us (13%)
  matrix products  11.7 us (5%)
  other arithmetic  5.36 us (2%)
  local copies, waits for them, and re-layouts  4.46 us (2%)
    all_to_all x3, waiting for transfers between devices, a2a(): lax.all_to_all(v.reshape(experts, cap, width), 'expert', split_axis=0, co...  65.4 us
    ppermute x31, waiting for transfers between devices, move(): return lax.ppermute(v, 'dp', dp_perm(dz, dx))  40.2 us
    all_to_all x3, starting transfers between devices, a2a(): lax.all_to_all(v.reshape(experts, cap, width), 'expert', split_axis=0, co...  33.7 us
    pallas_call x7, Pallas kernels, run(): pl.pallas_call(body, grid=(steps,), out_shape=tuple(((pltpu.HBM if hbm an...  28.5 us
    ppermute x31, starting transfers between devices, move(): return lax.ppermute(v, 'dp', dp_perm(dz, dx))  25.6 us
    dot_general x3, matrix products, dot(): lax.dot_general(a, b, (((ca,), (cb,)), ((), ())), preferred_element_type=...  11.7 us
  transfers between devices with their start and end apart: 34, of which 18 were waited for; matrix products, arithmetic and copies ran while one was open for 8% of the time, Pallas kernels for 11%

profile of v3, /device:TPU:1, one launch (start us, length us, event | category | flops | bytes accessed | tf_op | source)
XLA Modules:
  0.0 215.9 jit_solution(1116047855613347240)
XLA Ops:
  0.6 2.8 %shard_map.120 = (bf16[768,896]{1,0:T(8,128)(2,1)}, bf16[768,128]{1,0:T(8,128)(2,1)S(1)}, f32[768,1]{1,0:T(8,128)S(1)}) custom-call(s32[4,128]{1,0:T(4,128)} %bitcast.88, f32[4,128]{1,0:T(4,128)} %bitcast.89, bf16[128,896]{1,0:T(8,128)(2,1)} %tokens_ref.1), custom_call_target="tpu_custom_call" | custom-call | tf_op jit(solution)/shard_map/pallas_call | solution.py:32
  3.4 12.8 %all-to-all-start = ((bf16[32,24,896]{2,1,0:T(8,128)(2,1)}), bf16[32,24,896]{2,1,0:T(8,128)(2,1)S(1)}, u32[]{:S(2)}, u32[]{:S(2)}) async-start(bf16[32,24,896]{2,1,0:T(8,128)(2,1)} %bitcast.2), calls=%async_computation | async-start | bytes 2752512 | tf_op jit(solution)/shard_map/all_to_all | solution.py:210
  16.2 1.6 shard_map.121
  17.7 33.3 %all-to-all-done = bf16[32,24,896]{2,1,0:T(8,128)(2,1)S(1)} async-done(((bf16[32,24,896]{2,1,0:T(8,128)(2,1)}), bf16[32,24,896]{2,1,0:T(8,128)(2,1)S(1)}, u32[]{:S(2)}, u32[]{:S(2)}) %all-to-all-start) | async-done | bytes 1376288 | tf_op jit(solution)/shard_map/all_to_all | solution.py:210
  51.0 1.1 copy-done.5
  52.1 6.2 %all-to-all-start.1 = ((bf16[32,24,896]{2,1,0:T(8,128)(2,1)}), bf16[32,24,896]{2,1,0:T(8,128)(2,1)S(1)}, u32[]{:S(2)}, u32[]{:S(2)}) async-start(bf16[32,24,896]{2,1,0:T(8,128)(2,1)} %bitcast.4), calls=%async_computation.1 | async-start | bytes 2752512 | tf_op jit(solution)/shard_map/all_to_all | solution.py:210
  58.6 7.0 %shard_map.123 = (bf16[2,768,256]{2,1,0:T(8,128)(2,1)}, bf16[2,768,256]{2,1,0:T(8,128)(2,1)}, bf16[2,768,256]{2,1,0:T(8,128)(2,1)}, bf16[2,768,256]{2,1,0:T(8,128)(2,1)}) custom-call(s32[8]{0:T(128)S(1)} %add.184.tab, bf16[768,896]{1,0:T(8,128)(2,1)} %bitcast.82, bf16[896,1024]{1,0:T(8,128)(2,1)S(1)} %bitcast.75, bf16[896,1024]{1,0:T(8,128)(2,1)} %bitcast.78), custom_call_target="tpu_custom_call" | custom-call | tf_op jit(solution)/shard_map/pallas_call | solution.py:32
  65.5 1.2 collective-permute-start.8
  66.8 2.4 %collective-permute-start.9 = (bf16[2,768,256]{2,1,0:T(8,128)(2,1)}, bf16[2,768,256]{2,1,0:T(8,128)(2,1)}, u32[]{:S(2)}, u32[]{:S(2)}) collective-permute-start(bf16[2,768,256]{2,1,0:T(8,128)(2,1)} %get-tuple-element.42), channel_id=1, source_target_pairs={{0,64},{32,96},{64,0},{96,32},{128,192},{160,224},{192,128},{224,1... | collective-permute-start | bytes 2359304 | tf_op jit(solution)/shard_map/ppermute | solution.py:145
  69.2 1.0 collective-permute-start.10
  70.2 23.7 %all-to-all-done.1 = bf16[32,24,896]{2,1,0:T(8,128)(2,1)S(1)} async-done(((bf16[32,24,896]{2,1,0:T(8,128)(2,1)}), bf16[32,24,896]{2,1,0:T(8,128)(2,1)S(1)}, u32[]{:S(2)}, u32[]{:S(2)}) %all-to-all-start.1) | async-done | bytes 1376288 | tf_op jit(solution)/shard_map/all_to_all | solution.py:210
  93.9 1.1 copy-done.3
  94.9 5.4 %shard_map.122 = (bf16[2,384,128]{2,1,0:T(8,128)(2,1)}, bf16[2,384,128]{2,1,0:T(8,128)(2,1)}, bf16[2,384,128]{2,1,0:T(8,128)(2,1)}, bf16[2,384,128]{2,1,0:T(8,12...) custom-call(s32[8]{0:T(128)S(1)} %add.184.tab, bf16[768,896]{1,0:T(8,128)(2,1)} %bitcast.80, ...), custom_call_target="tpu_custom_call" | custom-call | tf_op jit(solution)/shard_map/pallas_call | solution.py:32
  100.3 2.5 %collective-permute-start.2 = (bf16[2,384,128]{2,1,0:T(8,128)(2,1)}, bf16[2,384,128]{2,1,0:T(8,128)(2,1)S(1)}, u32[]{:S(2)}, u32[]{:S(2)}) collective-permute-start(bf16[2,384,128]{2,1,0:T(8,128)(2,1)} %get-tuple-element.36), channel_id=1, source_target_pairs={{0,96},{32,0},{64,32},{96,64},{128,224},{160,128},{192,160},{224,1... | collective-permute-start | bytes 589832 | tf_op jit(solution)/shard_map/ppermute | solution.py:145
  104.2 2.4 %collective-permute-done.2 = bf16[2,384,128]{2,1,0:T(8,128)(2,1)S(1)} collective-permute-done((bf16[2,384,128]{2,1,0:T(8,128)(2,1)}, bf16[2,384,128]{2,1,0:T(8,128)(2,1)S(1)}, u32[]{:S(2)}, u32[]{:S(2)}) %collective-permute-start.2) | collective-permute-done | bytes 196640 | tf_op jit(solution)/shard_map/ppermute | solution.py:145
  106.6 2.6 %collective-permute-done.1 = bf16[2,384,128]{2,1,0:T(8,128)(2,1)S(1)} collective-permute-done((bf16[2,384,128]{2,1,0:T(8,128)(2,1)}, bf16[2,384,128]{2,1,0:T(8,128)(2,1)S(1)}, u32[]{:S(2)}, u32[]{:S(2)}) %collective-permute-start.1) | collective-permute-done | bytes 196640 | tf_op jit(solution)/shard_map/ppermute | solution.py:145
  109.2 5.7 %collective-permute-done = bf16[2,384,128]{2,1,0:T(8,128)(2,1)S(1)} collective-permute-done((bf16[2,384,128]{2,1,0:T(8,128)(2,1)}, bf16[2,384,128]{2,1,0:T(8,128)(2,1)S(1)}, u32[]{:S(2)}, u32[]{:S(2)}) %collective-permute-start) | collective-permute-done | bytes 196640 | tf_op jit(solution)/shard_map/ppermute | solution.py:145
  114.9 0.9 fusion.4
  115.9 1.4 fusion
  117.4 1.5 collective-permute-start.11
  120.0 1.2 collective-permute-start.5
  121.1 7.4 %collective-permute-done.11 = bf16[768,256]{1,0:T(8,128)(2,1)S(1)} collective-permute-done((bf16[768,256]{1,0:T(8,128)(2,1)S(1)}, bf16[768,256]{1,0:T(8,128)(2,1)S(1)}, u32[]{:S(2)}, u32[]{:S(2)}) %collective-permute-start.11) | collective-permute-done | bytes 393248 | tf_op jit(solution)/shard_map/ppermute | solution.py:145
  128.5 1.5 convert_add_fusion
  130.4 2.7 %collective-permute-start.13 = (bf16[768,128]{1,0:T(8,128)(2,1)S(1)}, bf16[768,128]{1,0:T(8,128)(2,1)S(1)}, u32[]{:S(2)}, u32[]{:S(2)}) collective-permute-start(bf16[768,128]{1,0:T(8,128)(2,1)S(1)} %get-tuple-element.55.refs_0_), channel_id=1, source_target_pairs={{0,96},{32,0},{64,32},{96,64},{128,224},{160,128},{192,160},{224,1... | collective-permute-start | bytes 589832 | tf_op jit(solution)/shard_map/ppermute | solution.py:145
  133.1 1.5 collective-permute-start.22
  134.6 1.9 collective-permute-done.12.refs_1_
  136.5 0.8 collective-permute-start.20
  137.3 0.7 collective-permute-start.14
  138.0 3.6 %collective-permute-done.22.refs_12_ = bf16[768,128]{1,0:T(8,128)(2,1)S(1)} collective-permute-done((bf16[768,128]{1,0:T(8,128)(2,1)S(1)}, bf16[768,128]{1,0:T(8,128)(2,1)S(1)}, u32[]{:S(2)}, u32[]{:S(2)}) %collective-permute-start.22) | collective-permute-done | bytes 196640 | tf_op jit(solution)/shard_map/ppermute | solution.py:145
  141.7 2.6 %collective-permute-start.24 = (bf16[768,128]{1,0:T(8,128)(2,1)S(1)}, bf16[768,128]{1,0:T(8,128)(2,1)}, u32[]{:S(2)}, u32[]{:S(2)}) collective-permute-start(bf16[768,128]{1,0:T(8,128)(2,1)S(1)} %collective-permute-done.22.refs_12_), channel_id=1, source_target_pairs={{0,96},{32,0},{64,32},{96,64},{128,224},{160,128},{192,160},{224,1... | collective-permute-start | bytes 589832 | tf_op jit(solution)/shard_map/ppermute | solution.py:145
  145.1 0.9 collective-permute-done.16.refs_5_
  145.9 3.6 %collective-permute-done.23.refs_13_ = bf16[768,128]{1,0:T(8,128)(2,1)} collective-permute-done((bf16[768,128]{1,0:T(8,128)(2,1)S(1)}, bf16[768,128]{1,0:T(8,128)(2,1)}, u32[]{:S(2)}, u32[]{:S(2)}) %collective-permute-start.23) | collective-permute-done | bytes 196640 | tf_op jit(solution)/shard_map/ppermute | solution.py:145
  150.1 0.7 copy-done.20
  150.8 3.4 %collective-permute-done.18.refs_7_ = bf16[768,128]{1,0:T(8,128)(2,1)} collective-permute-done((bf16[768,128]{1,0:T(8,128)(2,1)}, bf16[768,128]{1,0:T(8,128)(2,1)}, u32[]{:S(2)}, u32[]{:S(2)}) %collective-permute-start.18) | collective-permute-done | bytes 196640 | tf_op jit(solution)/shard_map/ppermute | solution.py:145
  154.3 1.4 collective-permute-done.25.refs_15_
  155.7 7.2 %shard_map.124 = (bf16[768,896]{1,0:T(8,128)(2,1)}, bf16[768,1024]{1,0:T(8,128)(2,1)}, bf16[768,1024]{1,0:T(8,128)(2,1)}) custom-call(s32[8]{0:T(128)S(1)} %add.179.tab, bf16[768,128]{1,0:T(8,128)(2,1)} %copy-done.11, bf16[768,128]{1,0:T(8,128)(2,1)} %copy-done.14, bf16[768,128]{1,0:T(8,128)(2,1)} %copy-done.15, ...), custom_call_target="tpu_custom_call" | custom-call | tf_op jit(solution)/shard_map/pallas_call | solution.py:32
  162.9 14.7 %all-to-all-start.2 = ((bf16[32,24,896]{2,1,0:T(8,128)(2,1)}), bf16[32,24,896]{2,1,0:T(8,128)(2,1)S(1)}, u32[]{:S(2)}, u32[]{:S(2)}) async-start(bf16[32,24,896]{2,1,0:T(8,128)(2,1)} %bitcast.86), calls=%async_computation.2 | async-start | bytes 2752512 | tf_op jit(solution)/shard_map/all_to_all | solution.py:210
  177.7 1.0 pad_maximum_fusion.1.refs_0_
  178.7 2.7 %collective-permute-start.28 = (bf16[2,768,128]{2,1,0:T(8,128)(2,1)S(1)}, bf16[2,768,128]{2,1,0:T(8,128)(2,1)S(1)}, u32[]{:S(2)}, u32[]{:S(2)}) collective-permute-start(bf16[2,768,128]{2,1,0:T(8,128)(2,1)S(1)} %pad_maximum_fusion.1.refs_0_), channel_id=1, source_target_pairs={{0,96},{32,0},{64,32},{96,64},{128,224},{160,128},{192,160},{224,1... | collective-permute-start | bytes 1179656 | tf_op jit(solution)/shard_map/ppermute | solution.py:145
  181.4 4.4 %convert_bitcast_fusion.2 = bf16[1,896,1024]{2,1,0:T(8,128)(2,1)} fusion(bf16[768,896]{1,0:T(8,128)(2,1)S(1)} %bitcast.83, bf16[768,1024]{1,0:T(8,128)(2,1)} %get-tuple-element.50), kind=kOutput, calls=%fused_computation.2 | convolution fusion | flops 1410203648 | bytes 4784128 | tf_op jit(solution)/shard_map/dot_general | solution.py:46
  185.8 4.6 %collective-permute-done.27.refs_1_ = bf16[2,768,128]{2,1,0:T(8,128)(2,1)S(1)} collective-permute-done((bf16[2,768,128]{2,1,0:T(8,128)(2,1)S(1)}, bf16[2,768,128]{2,1,0:T(8,128)(2,1)S(1)}, u32[]{:S(2)}, u32[]{:S(2)}) %collective-permute-start.27) | collective-permute-done | bytes 393248 | tf_op jit(solution)/shard_map/ppermute | solution.py:145
  190.6 2.7 %collective-permute-start.30 = (bf16[768,128]{1,0:T(8,128)(2,1)S(1)}, bf16[768,128]{1,0:T(8,128)(2,1)S(1)}, u32[]{:S(2)}, u32[]{:S(2)}) collective-permute-start(bf16[768,128]{1,0:T(8,128)(2,1)S(1)} %slice_bitcast_fusion), channel_id=1, source_target_pairs={{0,96},{32,0},{64,32},{96,64},{128,224},{160,128},{192,160},{224,1... | collective-permute-start | bytes 589832 | tf_op jit(solution)/shard_map/ppermute | solution.py:145
  193.3 2.9 %convert_bitcast_fusion.1 = bf16[1,896,1024]{2,1,0:T(8,128)(2,1)} fusion(bf16[768,896]{1,0:T(8,128)(2,1)S(1)} %bitcast.84, bf16[768,1024]{1,0:T(8,128)(2,1)S(1)} %copy-done.25), kind=kOutput, calls=%fused_computation.1 | convolution fusion | flops 1410203648 | bytes 4784128 | tf_op jit(solution)/shard_map/dot_general | solution.py:46
  196.2 0.9 collective-permute-done.29.refs_3_
  198.4 2.7 %shard_map.126 = bf16[768,1024]{1,0:T(8,128)(2,1)} custom-call(s32[8]{0:T(128)S(1)} %add.179.tab, bf16[2,768,128]{2,1,0:T(8,128)(2,1)} %copy-done.7, bf16[2,768,128]{2,1,0:T(8,128)(2,1)} %copy-done.8, bf16[2,768,128]{2,1,0:T(8,128)(2,1)} %copy-done.9, bf16[768,128]{1,0:T(8,128)(2,1)} %copy-done.22, bf16[768,128]{1,0:T(8,128)(2,1)} %copy-done.23), custom_call_target="tpu_custom_call" | custom-call | tf_op jit(solution)/shard_map/pallas_call | solution.py:32
  201.1 4.5 %convert_bitcast_fusion = bf16[1,1024,896]{2,1,0:T(8,128)(2,1)} fusion(bf16[768,1024]{1,0:T(8,128)(2,1)} %shard_map.126, bf16[768,896]{1,0:T(8,128)(2,1)S(1)} %bitcast.81), kind=kOutput, calls=%fused_computation | convolution fusion | flops 1410203648 | bytes 4784128 | tf_op jit(solution)/shard_map/dot_general | solution.py:46
  205.6 8.3 %all-to-all-done.2 = bf16[32,24,896]{2,1,0:T(8,128)(2,1)S(1)} async-done(((bf16[32,24,896]{2,1,0:T(8,128)(2,1)}), bf16[32,24,896]{2,1,0:T(8,128)(2,1)S(1)}, u32[]{:S(2)}, u32[]{:S(2)}) %all-to-all-start.2) | async-done | bytes 1376288 | tf_op jit(solution)/shard_map/all_to_all | solution.py:210
  213.9 2.0 shard_map.125
  (97 shorter events, 6.1 us)
Async XLA Ops:
  0.6 15.5 %copy-start.2 = (bf16[128,896]{1,0:T(8,128)(2,1)S(1)}, bf16[128,896]{1,0:T(8,128)(2,1)}, u32[]{:S(2)}) copy-start(bf16[128,896]{1,0:T(8,128)(2,1)} %cot_ref.1) | copy-start | bytes 688132
  3.4 14.3 %copy-start.1 = (bf16[768,128]{1,0:T(8,128)(2,1)}, bf16[768,128]{1,0:T(8,128)(2,1)S(1)}, u32[]{:S(2)}) copy-start(bf16[768,128]{1,0:T(8,128)(2,1)S(1)} %get-tuple-element.29.sel_ref) | copy-start | bytes 589828
  3.4 47.6 %all-to-all-start = ((bf16[32,24,896]{2,1,0:T(8,128)(2,1)}), bf16[32,24,896]{2,1,0:T(8,128)(2,1)S(1)}, u32[]{:S(2)}, u32[]{:S(2)}) async-start(bf16[32,24,896]{2,1,0:T(8,128)(2,1)} %bitcast.2), calls=%async_computation | async-start | bytes 2752512 | tf_op jit(solution)/shard_map/all_to_all | solution.py:210
  17.7 40.7 %copy-start.24 = (s32[4]{0:T(128)S(1)}, s32[4]{0:T(128)}, u32[]{:S(2)}) copy-start(s32[4]{0:T(128)} %constant.67.clone) | copy-start | bytes 52
  17.7 40.9 %copy-start = (bf16[1,896,1024]{2,1,0:T(8,128)(2,1)S(1)}, bf16[1,896,1024]{2,1,0:T(8,128)(2,1)}, u32[]{:S(2)}) copy-start(bf16[1,896,1024]{2,1,0:T(8,128)(2,1)} %param.13) | copy-start | bytes 5505028
  52.1 41.8 %all-to-all-start.1 = ((bf16[32,24,896]{2,1,0:T(8,128)(2,1)}), bf16[32,24,896]{2,1,0:T(8,128)(2,1)S(1)}, u32[]{:S(2)}, u32[]{:S(2)}) async-start(bf16[32,24,896]{2,1,0:T(8,128)(2,1)} %bitcast.4), calls=%async_computation.1 | async-start | bytes 2752512 | tf_op jit(solution)/shard_map/all_to_all | solution.py:210
  65.5 37.7 %collective-permute-start.8 = (bf16[2,768,256]{2,1,0:T(8,128)(2,1)}, bf16[2,768,256]{2,1,0:T(8,128)(2,1)}, u32[]{:S(2)}, u32[]{:S(2)}) collective-permute-start(bf16[2,768,256]{2,1,0:T(8,128)(2,1)} %get-tuple-element.41), channel_id=1, source_target_pairs={{0,32},{32,64},{64,96},{96,0},{128,160},{160,192},{192,224},{224,1... | collective-permute-start | bytes 2359304 | tf_op jit(solution)/shard_map/ppermute | solution.py:145
  66.8 36.9 %collective-permute-start.9 = (bf16[2,768,256]{2,1,0:T(8,128)(2,1)}, bf16[2,768,256]{2,1,0:T(8,128)(2,1)}, u32[]{:S(2)}, u32[]{:S(2)}) collective-permute-start(bf16[2,768,256]{2,1,0:T(8,128)(2,1)} %get-tuple-element.42), channel_id=1, source_target_pairs={{0,64},{32,96},{64,0},{96,32},{128,192},{160,224},{192,128},{224,1... | collective-permute-start | bytes 2359304 | tf_op jit(solution)/shard_map/ppermute | solution.py:145
  69.2 35.0 %collective-permute-start.10 = (bf16[2,768,256]{2,1,0:T(8,128)(2,1)}, bf16[2,768,256]{2,1,0:T(8,128)(2,1)}, u32[]{:S(2)}, u32[]{:S(2)}) collective-permute-start(bf16[2,768,256]{2,1,0:T(8,128)(2,1)} %get-tuple-element.43), channel_id=1, source_target_pairs={{0,96},{32,0},{64,32},{96,64},{128,224},{160,128},{192,160},{224,1... | collective-permute-start | bytes 2359304 | tf_op jit(solution)/shard_map/ppermute | solution.py:145
  94.9 21.0 %copy-start.12 = (bf16[2,768,256]{2,1,0:T(8,128)(2,1)S(1)}, bf16[2,768,256]{2,1,0:T(8,128)(2,1)}, u32[]{:S(2)}) copy-start(bf16[2,768,256]{2,1,0:T(8,128)(2,1)} %get-tuple-element.44) | copy-start | bytes 2359300
  100.3 19.1 %copy-start.21 = (bf16[2,384,128]{2,1,0:T(8,128)(2,1)S(1)}, bf16[2,384,128]{2,1,0:T(8,128)(2,1)}, u32[]{:S(2)}) copy-start(bf16[2,384,128]{2,1,0:T(8,128)(2,1)} %get-tuple-element.33) | copy-start | bytes 589828
  100.3 6.2 %collective-permute-start.2 = (bf16[2,384,128]{2,1,0:T(8,128)(2,1)}, bf16[2,384,128]{2,1,0:T(8,128)(2,1)S(1)}, u32[]{:S(2)}, u32[]{:S(2)}) collective-permute-start(bf16[2,384,128]{2,1,0:T(8,128)(2,1)} %get-tuple-element.36), channel_id=1, source_target_pairs={{0,96},{32,0},{64,32},{96,64},{128,224},{160,128},{192,160},{224,1... | collective-permute-start | bytes 589832 | tf_op jit(solution)/shard_map/ppermute | solution.py:145
  102.8 6.3 %collective-permute-start.1 = (bf16[2,384,128]{2,1,0:T(8,128)(2,1)}, bf16[2,384,128]{2,1,0:T(8,128)(2,1)S(1)}, u32[]{:S(2)}, u32[]{:S(2)}) collective-permute-start(bf16[2,384,128]{2,1,0:T(8,128)(2,1)} %get-tuple-element.35), channel_id=1, source_target_pairs={{0,64},{32,96},{64,0},{96,32},{128,192},{160,224},{192,128},{224,1... | collective-permute-start | bytes 589832 | tf_op jit(solution)/shard_map/ppermute | solution.py:145
  103.3 11.6 %collective-permute-start = (bf16[2,384,128]{2,1,0:T(8,128)(2,1)}, bf16[2,384,128]{2,1,0:T(8,128)(2,1)S(1)}, u32[]{:S(2)}, u32[]{:S(2)}) collective-permute-start(bf16[2,384,128]{2,1,0:T(8,128)(2,1)} %get-tuple-element.34), channel_id=1, source_target_pairs={{0,32},{32,64},{64,96},{96,0},{128,160},{160,192},{192,224},{224,1... | collective-permute-start | bytes 589832 | tf_op jit(solution)/shard_map/ppermute | solution.py:145
  103.7 15.8 %collective-permute-start.4 = (bf16[4,384,128]{2,1,0:T(8,128)(2,1)}, bf16[4,384,128]{2,1,0:T(8,128)(2,1)S(1)}, u32[]{:S(2)}, u32[]{:S(2)}) collective-permute-start(bf16[4,384,128]{2,1,0:T(8,128)(2,1)} %get-tuple-element.38), channel_id=1, source_target_pairs={{0,128},{32,160},{64,192},{96,224},{128,0},{160,32},{192,64},{224,... | collective-permute-start | bytes 1179656 | tf_op jit(solution)/shard_map/ppermute | solution.py:145
  104.2 15.3 %copy-start.13 = (bf16[4,384,128]{2,1,0:T(8,128)(2,1)S(1)}, bf16[4,384,128]{2,1,0:T(8,128)(2,1)}, u32[]{:S(2)}) copy-start(bf16[4,384,128]{2,1,0:T(8,128)(2,1)} %get-tuple-element.37) | copy-start | bytes 1179652
  115.8 3.6 %collective-permute-start.3 = (bf16[384,128]{1,0:T(8,128)(2,1)S(1)}, bf16[384,128]{1,0:T(8,128)(2,1)S(1)}, u32[]{:S(2)}, u32[]{:S(2)}) collective-permute-start(bf16[384,128]{1,0:T(8,128)(2,1)S(1)} %fusion.4), channel_id=1, source_target_pairs={{0,128},{32,160},{64,192},{96,224},{128,0},{160,32},{192,64},{224,... | collective-permute-start | bytes 294920 | tf_op jit(solution)/shard_map/ppermute | solution.py:145
  117.4 11.1 %collective-permute-start.11 = (bf16[768,256]{1,0:T(8,128)(2,1)S(1)}, bf16[768,256]{1,0:T(8,128)(2,1)S(1)}, u32[]{:S(2)}, u32[]{:S(2)}) collective-permute-start(bf16[768,256]{1,0:T(8,128)(2,1)S(1)} %fusion), channel_id=1, source_target_pairs={{0,128},{32,160},{64,192},{96,224},{128,0},{160,32},{192,64},{224,... | collective-permute-start | bytes 1179656 | tf_op jit(solution)/shard_map/ppermute | solution.py:145
  119.6 10.4 %collective-permute-start.7 = (bf16[384,128]{1,0:T(8,128)(2,1)S(1)}, bf16[384,128]{1,0:T(8,128)(2,1)S(1)}, u32[]{:S(2)}, u32[]{:S(2)}) collective-permute-start(bf16[384,128]{1,0:T(8,128)(2,1)S(1)} %get-tuple-element.58), channel_id=1, source_target_pairs={{0,96},{32,0},{64,32},{96,64},{128,224},{160,128},{192,160},{224,1... | collective-permute-start | bytes 294920 | tf_op jit(solution)/shard_map/ppermute | solution.py:145
  119.7 10.3 %collective-permute-start.6 = (bf16[384,128]{1,0:T(8,128)(2,1)S(1)}, bf16[384,128]{1,0:T(8,128)(2,1)S(1)}, u32[]{:S(2)}, u32[]{:S(2)}) collective-permute-start(bf16[384,128]{1,0:T(8,128)(2,1)S(1)} %get-tuple-element.59), channel_id=1, source_target_pairs={{0,64},{32,96},{64,0},{96,32},{128,192},{160,224},{192,128},{224,1... | collective-permute-start | bytes 294920 | tf_op jit(solution)/shard_map/ppermute | solution.py:145
  120.0 10.0 %collective-permute-start.5 = (bf16[384,128]{1,0:T(8,128)(2,1)S(1)}, bf16[384,128]{1,0:T(8,128)(2,1)S(1)}, u32[]{:S(2)}, u32[]{:S(2)}) collective-permute-start(bf16[384,128]{1,0:T(8,128)(2,1)S(1)} %get-tuple-element.57), channel_id=1, source_target_pairs={{0,32},{32,64},{64,96},{96,0},{128,160},{160,192},{192,224},{224,1... | collective-permute-start | bytes 294920 | tf_op jit(solution)/shard_map/ppermute | solution.py:145
  130.3 25.3 %copy-start.10 = (bf16[768,128]{1,0:T(8,128)(2,1)}, bf16[768,128]{1,0:T(8,128)(2,1)S(1)}, u32[]{:S(2)}) copy-start(bf16[768,128]{1,0:T(8,128)(2,1)S(1)} %get-tuple-element.54.refs_8_) | copy-start | bytes 589828
  130.3 25.3 %copy-start.11 = (bf16[768,128]{1,0:T(8,128)(2,1)}, bf16[768,128]{1,0:T(8,128)(2,1)S(1)}, u32[]{:S(2)}) copy-start(bf16[768,128]{1,0:T(8,128)(2,1)S(1)} %get-tuple-element.55.refs_0_) | copy-start | bytes 589828
  130.4 6.1 %collective-permute-start.12 = (bf16[768,128]{1,0:T(8,128)(2,1)S(1)}, bf16[768,128]{1,0:T(8,128)(2,1)S(1)}, u32[]{:S(2)}, u32[]{:S(2)}) collective-permute-start(bf16[768,128]{1,0:T(8,128)(2,1)S(1)} %get-tuple-element.55.refs_0_), channel_id=1, source_target_pairs={{0,32},{32,64},{64,96},{96,0},{128,160},{160,192},{192,224},{224,1... | collective-permute-start | bytes 589832 | tf_op jit(solution)/shard_map/ppermute | solution.py:145
  130.4 6.8 %collective-permute-start.13 = (bf16[768,128]{1,0:T(8,128)(2,1)S(1)}, bf16[768,128]{1,0:T(8,128)(2,1)S(1)}, u32[]{:S(2)}, u32[]{:S(2)}) collective-permute-start(bf16[768,128]{1,0:T(8,128)(2,1)S(1)} %get-tuple-element.55.refs_0_), channel_id=1, source_target_pairs={{0,96},{32,0},{64,32},{96,64},{128,224},{160,128},{192,160},{224,1... | collective-permute-start | bytes 589832 | tf_op jit(solution)/shard_map/ppermute | solution.py:145
  133.1 4.9 %collective-permute-start.15 = (bf16[768,128]{1,0:T(8,128)(2,1)S(1)}, bf16[768,128]{1,0:T(8,128)(2,1)S(1)}, u32[]{:S(2)}, u32[]{:S(2)}) collective-permute-start(bf16[768,128]{1,0:T(8,128)(2,1)S(1)} %get-tuple-element.55.refs_0_), channel_id=1, source_target_pairs={{0,128},{32,160},{64,192},{96,224},{128,0},{160,32},{192,64},{224,... | collective-permute-start | bytes 589832 | tf_op jit(solution)/shard_map/ppermute | solution.py:145
  133.1 8.5 %collective-permute-start.22 = (bf16[768,128]{1,0:T(8,128)(2,1)S(1)}, bf16[768,128]{1,0:T(8,128)(2,1)S(1)}, u32[]{:S(2)}, u32[]{:S(2)}) collective-permute-start(bf16[768,128]{1,0:T(8,128)(2,1)S(1)} %get-tuple-element.54.refs_8_), channel_id=1, source_target_pairs={{0,128},{32,160},{64,192},{96,224},{128,0},{160,32},{192,64},{224,... | collective-permute-start | bytes 589832 | tf_op jit(solution)/shard_map/ppermute | solution.py:145
  134.6 7.0 %collective-permute-start.19 = (bf16[768,128]{1,0:T(8,128)(2,1)S(1)}, bf16[768,128]{1,0:T(8,128)(2,1)S(1)}, u32[]{:S(2)}, u32[]{:S(2)}) collective-permute-start(bf16[768,128]{1,0:T(8,128)(2,1)S(1)} %get-tuple-element.54.refs_8_), channel_id=1, source_target_pairs={{0,32},{32,64},{64,96},{96,0},{128,160},{160,192},{192,224},{224,1... | collective-permute-start | bytes 589832 | tf_op jit(solution)/shard_map/ppermute | solution.py:145
  136.5 19.2 %copy-start.14 = (bf16[768,128]{1,0:T(8,128)(2,1)}, bf16[768,128]{1,0:T(8,128)(2,1)S(1)}, u32[]{:S(2)}) copy-start(bf16[768,128]{1,0:T(8,128)(2,1)S(1)} %collective-permute-done.12.refs_1_) | copy-start | bytes 589828
  136.5 5.2 %collective-permute-start.20 = (bf16[768,128]{1,0:T(8,128)(2,1)S(1)}, bf16[768,128]{1,0:T(8,128)(2,1)}, u32[]{:S(2)}, u32[]{:S(2)}) collective-permute-start(bf16[768,128]{1,0:T(8,128)(2,1)S(1)} %get-tuple-element.54.refs_8_), channel_id=1, source_target_pairs={{0,96},{32,0},{64,32},{96,64},{128,224},{160,128},{192,160},{224,1... | collective-permute-start | bytes 589832 | tf_op jit(solution)/shard_map/ppermute | solution.py:145
  137.3 18.4 %copy-start.15 = (bf16[768,128]{1,0:T(8,128)(2,1)}, bf16[768,128]{1,0:T(8,128)(2,1)S(1)}, u32[]{:S(2)}) copy-start(bf16[768,128]{1,0:T(8,128)(2,1)S(1)} %collective-permute-done.13.refs_2_) | copy-start | bytes 589828
  137.3 7.8 %collective-permute-start.14 = (bf16[768,128]{1,0:T(8,128)(2,1)S(1)}, bf16[768,128]{1,0:T(8,128)(2,1)}, u32[]{:S(2)}, u32[]{:S(2)}) collective-permute-start(bf16[768,128]{1,0:T(8,128)(2,1)S(1)} %collective-permute-done.12.refs_1_), channel_id=1, source_target_pairs={{0,32},{32,64},{64,96},{96,0},{128,160},{160,192},{192,224},{224,1... | collective-permute-start | bytes 589832 | tf_op jit(solution)/shard_map/ppermute | solution.py:145
  138.0 17.7 %copy-start.16 = (bf16[768,128]{1,0:T(8,128)(2,1)}, bf16[768,128]{1,0:T(8,128)(2,1)S(1)}, u32[]{:S(2)}) copy-start(bf16[768,128]{1,0:T(8,128)(2,1)S(1)} %collective-permute-done.15.refs_4_) | copy-start | bytes 589828
  138.0 8.0 %collective-permute-start.16 = (bf16[768,128]{1,0:T(8,128)(2,1)S(1)}, bf16[768,128]{1,0:T(8,128)(2,1)S(1)}, u32[]{:S(2)}, u32[]{:S(2)}) collective-permute-start(bf16[768,128]{1,0:T(8,128)(2,1)S(1)} %collective-permute-done.12.refs_1_), channel_id=1, source_target_pairs={{0,128},{32,160},{64,192},{96,224},{128,0},{160,32},{192,64},{224,... | collective-permute-start | bytes 589832 | tf_op jit(solution)/shard_map/ppermute | solution.py:145
  141.6 14.1 %copy-start.17 = (bf16[768,128]{1,0:T(8,128)(2,1)}, bf16[768,128]{1,0:T(8,128)(2,1)S(1)}, u32[]{:S(2)}) copy-start(bf16[768,128]{1,0:T(8,128)(2,1)S(1)} %collective-permute-done.22.refs_12_) | copy-start | bytes 589828
  141.6 7.9 %collective-permute-start.23 = (bf16[768,128]{1,0:T(8,128)(2,1)S(1)}, bf16[768,128]{1,0:T(8,128)(2,1)}, u32[]{:S(2)}, u32[]{:S(2)}) collective-permute-start(bf16[768,128]{1,0:T(8,128)(2,1)S(1)} %collective-permute-done.22.refs_12_), channel_id=1, source_target_pairs={{0,32},{32,64},{64,96},{96,0},{128,160},{160,192},{192,224},{224,1... | collective-permute-start | bytes 589832 | tf_op jit(solution)/shard_map/ppermute | solution.py:145
  141.6 8.4 %collective-permute-start.17 = (bf16[768,128]{1,0:T(8,128)(2,1)S(1)}, bf16[768,128]{1,0:T(8,128)(2,1)S(1)}, u32[]{:S(2)}, u32[]{:S(2)}) collective-permute-start(bf16[768,128]{1,0:T(8,128)(2,1)S(1)} %collective-permute-done.13.refs_2_), channel_id=1, source_target_pairs={{0,128},{32,160},{64,192},{96,224},{128,0},{160,32},{192,64},{224,... | collective-permute-start | bytes 589832 | tf_op jit(solution)/shard_map/ppermute | solution.py:145
  141.7 9.1 %collective-permute-start.24 = (bf16[768,128]{1,0:T(8,128)(2,1)S(1)}, bf16[768,128]{1,0:T(8,128)(2,1)}, u32[]{:S(2)}, u32[]{:S(2)}) collective-permute-start(bf16[768,128]{1,0:T(8,128)(2,1)S(1)} %collective-permute-done.22.refs_12_), channel_id=1, source_target_pairs={{0,96},{32,0},{64,32},{96,64},{128,224},{160,128},{192,160},{224,1... | collective-permute-start | bytes 589832 | tf_op jit(solution)/shard_map/ppermute | solution.py:145
  145.0 5.8 %collective-permute-start.21 = (bf16[768,128]{1,0:T(8,128)(2,1)}, bf16[768,128]{1,0:T(8,128)(2,1)}, u32[]{:S(2)}, u32[]{:S(2)}) collective-permute-start(bf16[768,128]{1,0:T(8,128)(2,1)} %collective-permute-done.20.refs_10_), channel_id=1, source_target_pairs={{0,96},{32,0},{64,32},{96,64},{128,224},{160,128},{192,160},{224,1... | collective-permute-start | bytes 589832 | tf_op jit(solution)/shard_map/ppermute | solution.py:145
  145.9 8.3 %collective-permute-start.18 = (bf16[768,128]{1,0:T(8,128)(2,1)}, bf16[768,128]{1,0:T(8,128)(2,1)}, u32[]{:S(2)}, u32[]{:S(2)}) collective-permute-start(bf16[768,128]{1,0:T(8,128)(2,1)} %collective-permute-done.14.refs_3_), channel_id=1, source_target_pairs={{0,128},{32,160},{64,192},{96,224},{128,0},{160,32},{192,64},{224,... | collective-permute-start | bytes 589832 | tf_op jit(solution)/shard_map/ppermute | solution.py:145
  149.5 6.2 %collective-permute-start.25 = (bf16[768,128]{1,0:T(8,128)(2,1)}, bf16[768,128]{1,0:T(8,128)(2,1)}, u32[]{:S(2)}, u32[]{:S(2)}) collective-permute-start(bf16[768,128]{1,0:T(8,128)(2,1)} %collective-permute-done.23.refs_13_), channel_id=1, source_target_pairs={{0,32},{32,64},{64,96},{96,0},{128,160},{160,192},{192,224},{224,1... | collective-permute-start | bytes 589832 | tf_op jit(solution)/shard_map/ppermute | solution.py:145
  150.0 12.9 %collective-permute-start.26 = (bf16[768,128]{1,0:T(8,128)(2,1)S(1)}, bf16[768,128]{1,0:T(8,128)(2,1)}, u32[]{:S(2)}, u32[]{:S(2)}) collective-permute-start(bf16[768,128]{1,0:T(8,128)(2,1)S(1)} %get-tuple-element.52), channel_id=1, source_target_pairs={{0,128},{32,160},{64,192},{96,224},{128,0},{160,32},{192,64},{224,... | collective-permute-start | bytes 589832 | tf_op jit(solution)/shard_map/ppermute | solution.py:145
  162.9 18.5 %copy-start.6 = (bf16[32,24,896]{2,1,0:T(8,128)(2,1)S(1)}, bf16[32,24,896]{2,1,0:T(8,128)(2,1)}, u32[]{:S(2)}) copy-start(bf16[32,24,896]{2,1,0:T(8,128)(2,1)} %copy-done.5) | copy-start | bytes 4128772
  162.9 51.0 %all-to-all-start.2 = ((bf16[32,24,896]{2,1,0:T(8,128)(2,1)}), bf16[32,24,896]{2,1,0:T(8,128)(2,1)S(1)}, u32[]{:S(2)}, u32[]{:S(2)}) async-start(bf16[32,24,896]{2,1,0:T(8,128)(2,1)} %bitcast.86), calls=%async_computation.2 | async-start | bytes 2752512 | tf_op jit(solution)/shard_map/all_to_all | solution.py:210
  178.6 11.8 %collective-permute-start.27 = (bf16[2,768,128]{2,1,0:T(8,128)(2,1)S(1)}, bf16[2,768,128]{2,1,0:T(8,128)(2,1)S(1)}, u32[]{:S(2)}, u32[]{:S(2)}) collective-permute-start(bf16[2,768,128]{2,1,0:T(8,128)(2,1)S(1)} %pad_maximum_fusion.1.refs_0_), channel_id=1, source_target_pairs={{0,32},{32,64},{64,96},{96,0},{128,160},{160,192},{192,224},{224,1... | collective-permute-start | bytes 1179656 | tf_op jit(solution)/shard_map/ppermute | solution.py:145
  178.7 11.8 %collective-permute-start.28 = (bf16[2,768,128]{2,1,0:T(8,128)(2,1)S(1)}, bf16[2,768,128]{2,1,0:T(8,128)(2,1)S(1)}, u32[]{:S(2)}, u32[]{:S(2)}) collective-permute-start(bf16[2,768,128]{2,1,0:T(8,128)(2,1)S(1)} %pad_maximum_fusion.1.refs_0_), channel_id=1, source_target_pairs={{0,96},{32,0},{64,32},{96,64},{128,224},{160,128},{192,160},{224,1... | collective-permute-start | bytes 1179656 | tf_op jit(solution)/shard_map/ppermute | solution.py:145
  190.4 6.6 %collective-permute-start.29 = (bf16[768,128]{1,0:T(8,128)(2,1)S(1)}, bf16[768,128]{1,0:T(8,128)(2,1)S(1)}, u32[]{:S(2)}, u32[]{:S(2)}) collective-permute-start(bf16[768,128]{1,0:T(8,128)(2,1)S(1)} %slice_bitcast_fusion.1), channel_id=1, source_target_pairs={{0,32},{32,64},{64,96},{96,0},{128,160},{160,192},{192,224},{224,1... | collective-permute-start | bytes 589832 | tf_op jit(solution)/shard_map/ppermute | solution.py:145
  190.6 6.5 %collective-permute-start.30 = (bf16[768,128]{1,0:T(8,128)(2,1)S(1)}, bf16[768,128]{1,0:T(8,128)(2,1)S(1)}, u32[]{:S(2)}, u32[]{:S(2)}) collective-permute-start(bf16[768,128]{1,0:T(8,128)(2,1)S(1)} %slice_bitcast_fusion), channel_id=1, source_target_pairs={{0,96},{32,0},{64,32},{96,64},{128,224},{160,128},{192,160},{224,1... | collective-permute-start | bytes 589832 | tf_op jit(solution)/shard_map/ppermute | solution.py:145
  (12 other events, 57.7 us)

commit v4 on v3

--- a/solution.py
+++ b/solution.py
@@ -153,9 +153,12 @@
     return [by_s[0]] + [move(by_s[s], 0, s) for s in range(1, NX)]
 
 
+def other_z(parts):
+    return add(*(p[1] for p in parts)).astype(bf16)
+
+
 def sum_x_first(parts):
-    other = move(add(*(p[1] for p in parts)).astype(bf16), 1, 0)
-    return add(other, *(p[0] for p in parts))
+    return add(move(other_z(parts), 1, 0), *(p[0] for p in parts))
 
 
 def sum_z_first(by_t):
@@ -234,13 +237,15 @@
         n_smem=1,
     )(dest, rows_s, wd)
     gu, _ = lax.optimization_barrier((gu, dh[0]))
-    gu = sum_x_first(gu)
+    dh_x, gu_z = send_x(dh[:NX]), other_z(gu)
+    dh_x, _ = lax.optimization_barrier((dh_x, gu_z))
+    gu = add(move(gu_z, 1, 0), *(p[0] for p in gu))
     gate, upper = gu[:, :128], gu[:, 128:]
     sig = jax.nn.sigmoid(gate)
     act = gate * sig
     hidden = (act * upper).astype(bf16)
     slope = upper * (sig * (1.0 + gate * (1.0 - sig)))
-    dh = jnp.concatenate([sum_x_first(send_x(dh[:NX])), sum_z_first(dh[NX:])], axis=0)
+    dh = jnp.concatenate([sum_x_first(dh_x), sum_z_first(dh[NX:])], axis=0)
     back, pre_gate, pre_up = call(
         back_body,
         [0] * (2 * NZ * NX) + [None, None],

time: 217 us -> 215 us (level)
  waiting for transfers between devices: 106 us -> 91.1 us
  starting transfers between devices: 59.3 us -> 73.4 us
    ppermute x31, waiting for transfers between devices: 40.2 us -> 25.7 us  [move(): return lax.ppermute(v, 'dp', dp_perm(dz, dx))]
    ppermute x31, starting transfers between devices: 25.6 us -> 35.1 us  [move(): return lax.ppermute(v, 'dp', dp_perm(dz, dx))]
    all_to_all x3, starting transfers between devices: 33.7 us -> 38.3 us  [a2a(): lax.all_to_all(v.reshape(experts, cap, width), 'expert', split_axis=0, co...]
where the time goes in v4:
time: 215 us; the launch traced here: 214 us
  waiting for transfers between devices  91.1 us (42%)
  starting transfers between devices  73.4 us (34%)
  Pallas kernels  28.5 us (13%)
  matrix products  11.7 us (5%)
  other arithmetic  4.51 us (2%)
  local copies, waits for them, and re-layouts  4.19 us (2%)
    all_to_all x3, waiting for transfers between devices, a2a(): lax.all_to_all(v.reshape(experts, cap, width), 'expert', split_axis=0, co...  65.4 us
    all_to_all x3, starting transfers between devices, a2a(): lax.all_to_all(v.reshape(experts, cap, width), 'expert', split_axis=0, co...  38.3 us
    ppermute x31, starting transfers between devices, move(): return lax.ppermute(v, 'dp', dp_perm(dz, dx))  35.1 us
    pallas_call x7, Pallas kernels, run(): pl.pallas_call(body, grid=(steps,), out_shape=tuple(((pltpu.HBM if hbm an...  28.5 us
    ppermute x31, waiting for transfers between devices, move(): return lax.ppermute(v, 'dp', dp_perm(dz, dx))  25.7 us
    dot_general x3, matrix products, dot(): lax.dot_general(a, b, (((ca,), (cb,)), ((), ())), preferred_element_type=...  11.7 us
  transfers between devices with their start and end apart: 34, of which 18 were waited for; matrix products, arithmetic and copies ran while one was open for 8% of the time, Pallas kernels for 11%

profile of v4, /device:TPU:1, one launch (start us, length us, event | category | flops | bytes accessed | tf_op | source)
XLA Modules:
  0.0 214.4 jit_solution(17414126026654102)
XLA Ops:
  0.6 2.8 %shard_map.120 = (bf16[768,896]{1,0:T(8,128)(2,1)}, bf16[768,128]{1,0:T(8,128)(2,1)S(1)}, f32[768,1]{1,0:T(8,128)S(1)}) custom-call(s32[4,128]{1,0:T(4,128)} %bitcast.82, f32[4,128]{1,0:T(4,128)} %bitcast.83, bf16[128,896]{1,0:T(8,128)(2,1)} %tokens_ref.1), custom_call_target="tpu_custom_call" | custom-call | tf_op jit(solution)/shard_map/pallas_call | solution.py:32
  3.4 12.8 %all-to-all-start = ((bf16[32,24,896]{2,1,0:T(8,128)(2,1)}), bf16[32,24,896]{2,1,0:T(8,128)(2,1)S(1)}, u32[]{:S(2)}, u32[]{:S(2)}) async-start(bf16[32,24,896]{2,1,0:T(8,128)(2,1)} %bitcast.2), calls=%async_computation | async-start | bytes 2752512 | tf_op jit(solution)/shard_map/all_to_all | solution.py:213
  16.2 1.6 shard_map.121
  17.7 33.3 %all-to-all-done = bf16[32,24,896]{2,1,0:T(8,128)(2,1)S(1)} async-done(((bf16[32,24,896]{2,1,0:T(8,128)(2,1)}), bf16[32,24,896]{2,1,0:T(8,128)(2,1)S(1)}, u32[]{:S(2)}, u32[]{:S(2)}) %all-to-all-start) | async-done | bytes 1376288 | tf_op jit(solution)/shard_map/all_to_all | solution.py:213
  51.0 1.1 copy-done.5
  52.1 6.2 %all-to-all-start.1 = ((bf16[32,24,896]{2,1,0:T(8,128)(2,1)}), bf16[32,24,896]{2,1,0:T(8,128)(2,1)S(1)}, u32[]{:S(2)}, u32[]{:S(2)}) async-start(bf16[32,24,896]{2,1,0:T(8,128)(2,1)} %bitcast.4), calls=%async_computation.1 | async-start | bytes 2752512 | tf_op jit(solution)/shard_map/all_to_all | solution.py:213
  58.6 7.0 %shard_map.123 = (bf16[2,768,256]{2,1,0:T(8,128)(2,1)}, bf16[2,768,256]{2,1,0:T(8,128)(2,1)}, bf16[2,768,256]{2,1,0:T(8,128)(2,1)}, bf16[2,768,256]{2,1,0:T(8,128)(2,1)}) custom-call(s32[8]{0:T(128)S(1)} %add.184.tab, bf16[768,896]{1,0:T(8,128)(2,1)} %bitcast.76, bf16[896,1024]{1,0:T(8,128)(2,1)S(1)} %bitcast.69, bf16[896,1024]{1,0:T(8,128)(2,1)} %bitcast.72), custom_call_target="tpu_custom_call" | custom-call | tf_op jit(solution)/shard_map/pallas_call | solution.py:32
  65.5 1.2 collective-permute-start.3
  66.8 2.4 %collective-permute-start.4 = (bf16[2,768,256]{2,1,0:T(8,128)(2,1)}, bf16[2,768,256]{2,1,0:T(8,128)(2,1)}, u32[]{:S(2)}, u32[]{:S(2)}) collective-permute-start(bf16[2,768,256]{2,1,0:T(8,128)(2,1)} %get-tuple-element.44), channel_id=1, source_target_pairs={{0,64},{32,96},{64,0},{96,32},{128,192},{160,224},{192,128},{224,1... | collective-permute-start | bytes 2359304 | tf_op jit(solution)/shard_map/ppermute | solution.py:145
  69.2 1.0 collective-permute-start.5
  70.2 23.7 %all-to-all-done.1 = bf16[32,24,896]{2,1,0:T(8,128)(2,1)S(1)} async-done(((bf16[32,24,896]{2,1,0:T(8,128)(2,1)}), bf16[32,24,896]{2,1,0:T(8,128)(2,1)S(1)}, u32[]{:S(2)}, u32[]{:S(2)}) %all-to-all-start.1) | async-done | bytes 1376288 | tf_op jit(solution)/shard_map/all_to_all | solution.py:213
  93.9 1.1 copy-done.3
  94.9 5.4 %shard_map.122 = (bf16[2,384,128]{2,1,0:T(8,128)(2,1)}, bf16[2,384,128]{2,1,0:T(8,128)(2,1)}, bf16[2,384,128]{2,1,0:T(8,128)(2,1)}, bf16[2,384,128]{2,1,0:T(8,12...) custom-call(s32[8]{0:T(128)S(1)} %add.184.tab, bf16[768,896]{1,0:T(8,128)(2,1)} %bitcast.74, ...), custom_call_target="tpu_custom_call" | custom-call | tf_op jit(solution)/shard_map/pallas_call | solution.py:32
  100.3 1.2 collective-permute-start
  101.6 2.5 %collective-permute-start.1 = (bf16[2,384,128]{2,1,0:T(8,128)(2,1)}, bf16[2,384,128]{2,1,0:T(8,128)(2,1)S(1)}, u32[]{:S(2)}, u32[]{:S(2)}) collective-permute-start(bf16[2,384,128]{2,1,0:T(8,128)(2,1)} %get-tuple-element.39), channel_id=1, source_target_pairs={{0,64},{32,96},{64,0},{96,32},{128,192},{160,224},{192,128},{224,1... | collective-permute-start | bytes 589832 | tf_op jit(solution)/shard_map/ppermute | solution.py:145
  105.0 1.5 fusion
  106.5 4.8 %collective-permute-done.1 = bf16[2,384,128]{2,1,0:T(8,128)(2,1)S(1)} collective-permute-done((bf16[2,384,128]{2,1,0:T(8,128)(2,1)}, bf16[2,384,128]{2,1,0:T(8,128)(2,1)S(1)}, u32[]{:S(2)}, u32[]{:S(2)}) %collective-permute-start.1) | collective-permute-done | bytes 196640 | tf_op jit(solution)/shard_map/ppermute | solution.py:145
  111.4 1.2 collective-permute-start.6
  112.9 2.0 collective-permute-done.6
  115.1 3.1 %collective-permute-start.10 = (bf16[384,128]{1,0:T(8,128)(2,1)S(1)}, bf16[384,128]{1,0:T(8,128)(2,1)S(1)}, u32[]{:S(2)}, u32[]{:S(2)}) collective-permute-start(bf16[384,128]{1,0:T(8,128)(2,1)S(1)} %get-tuple-element.66), channel_id=1, source_target_pairs={{0,96},{32,0},{64,32},{96,64},{128,224},{160,128},{192,160},{224,1... | collective-permute-start | bytes 294920 | tf_op jit(solution)/shard_map/ppermute | solution.py:145
  118.2 1.7 collective-permute-start.9
  119.9 1.3 collective-permute-done.11
  121.2 1.5 convert_add_fusion
  123.2 1.4 collective-permute-done.8
  124.9 3.2 %collective-permute-start.12 = (bf16[768,128]{1,0:T(8,128)(2,1)S(1)}, bf16[768,128]{1,0:T(8,128)(2,1)S(1)}, u32[]{:S(2)}, u32[]{:S(2)}) collective-permute-start(bf16[768,128]{1,0:T(8,128)(2,1)S(1)} %get-tuple-element.63.refs_0_), channel_id=1, source_target_pairs={{0,32},{32,64},{64,96},{96,0},{128,160},{160,192},{192,224},{224,1... | collective-permute-start | bytes 589832 | tf_op jit(solution)/shard_map/ppermute | solution.py:145
  129.5 1.5 collective-permute-start.19
  132.8 1.4 collective-permute-start.16
  135.0 1.8 collective-permute-start.23
  137.0 1.0 collective-permute-done.20.refs_10_
  138.1 1.5 collective-permute-done.14.refs_3_
  139.6 1.7 collective-permute-start.18
  141.4 1.7 collective-permute-done.23.refs_13_
  143.0 1.4 collective-permute-start.25
  145.2 1.9 collective-permute-done.21.refs_11_
  147.1 2.5 %collective-permute-done.25.refs_15_ = bf16[768,128]{1,0:T(8,128)(2,1)} collective-permute-done((bf16[768,128]{1,0:T(8,128)(2,1)}, bf16[768,128]{1,0:T(8,128)(2,1)}, u32[]{:S(2)}, u32[]{:S(2)}) %collective-permute-start.25) | collective-permute-done | bytes 196640 | tf_op jit(solution)/shard_map/ppermute | solution.py:145
  149.6 7.2 %shard_map.124 = (bf16[768,896]{1,0:T(8,128)(2,1)}, bf16[768,1024]{1,0:T(8,128)(2,1)}, bf16[768,1024]{1,0:T(8,128)(2,1)}) custom-call(s32[8]{0:T(128)S(1)} %add.179.tab, bf16[768,128]{1,0:T(8,128)(2,1)} %copy-done.11, bf16[768,128]{1,0:T(8,128)(2,1)} %copy-done.14, bf16[768,128]{1,0:T(8,128)(2,1)} %copy-done.15, ...), custom_call_target="tpu_custom_call" | custom-call | tf_op jit(solution)/shard_map/pallas_call | solution.py:32
  156.8 19.3 %all-to-all-start.2 = ((bf16[32,24,896]{2,1,0:T(8,128)(2,1)}), bf16[32,24,896]{2,1,0:T(8,128)(2,1)S(1)}, u32[]{:S(2)}, u32[]{:S(2)}) async-start(bf16[32,24,896]{2,1,0:T(8,128)(2,1)} %bitcast.80), calls=%async_computation.2 | async-start | bytes 2752512 | tf_op jit(solution)/shard_map/all_to_all | solution.py:213
  176.1 1.0 pad_maximum_fusion.1.refs_0_
  177.2 2.7 %collective-permute-start.28 = (bf16[2,768,128]{2,1,0:T(8,128)(2,1)S(1)}, bf16[2,768,128]{2,1,0:T(8,128)(2,1)S(1)}, u32[]{:S(2)}, u32[]{:S(2)}) collective-permute-start(bf16[2,768,128]{2,1,0:T(8,128)(2,1)S(1)} %pad_maximum_fusion.1.refs_0_), channel_id=1, source_target_pairs={{0,96},{32,0},{64,32},{96,64},{128,224},{160,128},{192,160},{224,1... | collective-permute-start | bytes 1179656 | tf_op jit(solution)/shard_map/ppermute | solution.py:145
  179.9 4.4 %convert_bitcast_fusion.2 = bf16[1,896,1024]{2,1,0:T(8,128)(2,1)} fusion(bf16[768,896]{1,0:T(8,128)(2,1)S(1)} %bitcast.77, bf16[768,1024]{1,0:T(8,128)(2,1)} %get-tuple-element.58), kind=kOutput, calls=%fused_computation.2 | convolution fusion | flops 1410203648 | bytes 4784128 | tf_op jit(solution)/shard_map/dot_general | solution.py:46
  184.3 4.6 %collective-permute-done.27.refs_1_ = bf16[2,768,128]{2,1,0:T(8,128)(2,1)S(1)} collective-permute-done((bf16[2,768,128]{2,1,0:T(8,128)(2,1)S(1)}, bf16[2,768,128]{2,1,0:T(8,128)(2,1)S(1)}, u32[]{:S(2)}, u32[]{:S(2)}) %collective-permute-start.27) | collective-permute-done | bytes 393248 | tf_op jit(solution)/shard_map/ppermute | solution.py:145
  189.0 2.7 %collective-permute-start.30 = (bf16[768,128]{1,0:T(8,128)(2,1)S(1)}, bf16[768,128]{1,0:T(8,128)(2,1)S(1)}, u32[]{:S(2)}, u32[]{:S(2)}) collective-permute-start(bf16[768,128]{1,0:T(8,128)(2,1)S(1)} %slice_bitcast_fusion), channel_id=1, source_target_pairs={{0,96},{32,0},{64,32},{96,64},{128,224},{160,128},{192,160},{224,1... | collective-permute-start | bytes 589832 | tf_op jit(solution)/shard_map/ppermute | solution.py:145
  191.8 2.9 %convert_bitcast_fusion.1 = bf16[1,896,1024]{2,1,0:T(8,128)(2,1)} fusion(bf16[768,896]{1,0:T(8,128)(2,1)S(1)} %bitcast.78, bf16[768,1024]{1,0:T(8,128)(2,1)S(1)} %copy-done.25), kind=kOutput, calls=%fused_computation.1 | convolution fusion | flops 1410203648 | bytes 4784128 | tf_op jit(solution)/shard_map/dot_general | solution.py:46
  194.6 0.9 collective-permute-done.29.refs_3_
  196.9 2.7 %shard_map.126 = bf16[768,1024]{1,0:T(8,128)(2,1)} custom-call(s32[8]{0:T(128)S(1)} %add.179.tab, bf16[2,768,128]{2,1,0:T(8,128)(2,1)} %copy-done.7, bf16[2,768,128]{2,1,0:T(8,128)(2,1)} %copy-done.8, bf16[2,768,128]{2,1,0:T(8,128)(2,1)} %copy-done.9, bf16[768,128]{1,0:T(8,128)(2,1)} %copy-done.22, bf16[768,128]{1,0:T(8,128)(2,1)} %copy-done.23), custom_call_target="tpu_custom_call" | custom-call | tf_op jit(solution)/shard_map/pallas_call | solution.py:32
  199.6 4.5 %convert_bitcast_fusion = bf16[1,1024,896]{2,1,0:T(8,128)(2,1)} fusion(bf16[768,1024]{1,0:T(8,128)(2,1)} %shard_map.126, bf16[768,896]{1,0:T(8,128)(2,1)S(1)} %bitcast.75), kind=kOutput, calls=%fused_computation | convolution fusion | flops 1410203648 | bytes 4784128 | tf_op jit(solution)/shard_map/dot_general | solution.py:46
  204.0 8.4 %all-to-all-done.2 = bf16[32,24,896]{2,1,0:T(8,128)(2,1)S(1)} async-done(((bf16[32,24,896]{2,1,0:T(8,128)(2,1)}), bf16[32,24,896]{2,1,0:T(8,128)(2,1)S(1)}, u32[]{:S(2)}, u32[]{:S(2)}) %all-to-all-start.2) | async-done | bytes 1376288 | tf_op jit(solution)/shard_map/all_to_all | solution.py:213
  212.4 2.0 shard_map.125
  (97 shorter events, 9.1 us)
Async XLA Ops:
  0.6 15.5 %copy-start.2 = (bf16[128,896]{1,0:T(8,128)(2,1)S(1)}, bf16[128,896]{1,0:T(8,128)(2,1)}, u32[]{:S(2)}) copy-start(bf16[128,896]{1,0:T(8,128)(2,1)} %cot_ref.1) | copy-start | bytes 688132
  3.4 14.3 %copy-start.1 = (bf16[768,128]{1,0:T(8,128)(2,1)}, bf16[768,128]{1,0:T(8,128)(2,1)S(1)}, u32[]{:S(2)}) copy-start(bf16[768,128]{1,0:T(8,128)(2,1)S(1)} %get-tuple-element.33.sel_ref) | copy-start | bytes 589828
  3.4 47.6 %all-to-all-start = ((bf16[32,24,896]{2,1,0:T(8,128)(2,1)}), bf16[32,24,896]{2,1,0:T(8,128)(2,1)S(1)}, u32[]{:S(2)}, u32[]{:S(2)}) async-start(bf16[32,24,896]{2,1,0:T(8,128)(2,1)} %bitcast.2), calls=%async_computation | async-start | bytes 2752512 | tf_op jit(solution)/shard_map/all_to_all | solution.py:213
  17.7 40.7 %copy-start.24 = (s32[4]{0:T(128)S(1)}, s32[4]{0:T(128)}, u32[]{:S(2)}) copy-start(s32[4]{0:T(128)} %constant.67.clone) | copy-start | bytes 52
  17.7 40.9 %copy-start = (bf16[1,896,1024]{2,1,0:T(8,128)(2,1)S(1)}, bf16[1,896,1024]{2,1,0:T(8,128)(2,1)}, u32[]{:S(2)}) copy-start(bf16[1,896,1024]{2,1,0:T(8,128)(2,1)} %param.13) | copy-start | bytes 5505028
  52.1 41.8 %all-to-all-start.1 = ((bf16[32,24,896]{2,1,0:T(8,128)(2,1)}), bf16[32,24,896]{2,1,0:T(8,128)(2,1)S(1)}, u32[]{:S(2)}, u32[]{:S(2)}) async-start(bf16[32,24,896]{2,1,0:T(8,128)(2,1)} %bitcast.4), calls=%async_computation.1 | async-start | bytes 2752512 | tf_op jit(solution)/shard_map/all_to_all | solution.py:213
  65.5 36.0 %collective-permute-start.3 = (bf16[2,768,256]{2,1,0:T(8,128)(2,1)}, bf16[2,768,256]{2,1,0:T(8,128)(2,1)}, u32[]{:S(2)}, u32[]{:S(2)}) collective-permute-start(bf16[2,768,256]{2,1,0:T(8,128)(2,1)} %get-tuple-element.43), channel_id=1, source_target_pairs={{0,32},{32,64},{64,96},{96,0},{128,160},{160,192},{192,224},{224,1... | collective-permute-start | bytes 2359304 | tf_op jit(solution)/shard_map/ppermute | solution.py:145
  66.8 37.3 %collective-permute-start.4 = (bf16[2,768,256]{2,1,0:T(8,128)(2,1)}, bf16[2,768,256]{2,1,0:T(8,128)(2,1)}, u32[]{:S(2)}, u32[]{:S(2)}) collective-permute-start(bf16[2,768,256]{2,1,0:T(8,128)(2,1)} %get-tuple-element.44), channel_id=1, source_target_pairs={{0,64},{32,96},{64,0},{96,32},{128,192},{160,224},{192,128},{224,1... | collective-permute-start | bytes 2359304 | tf_op jit(solution)/shard_map/ppermute | solution.py:145
  69.2 35.8 %collective-permute-start.5 = (bf16[2,768,256]{2,1,0:T(8,128)(2,1)}, bf16[2,768,256]{2,1,0:T(8,128)(2,1)}, u32[]{:S(2)}, u32[]{:S(2)}) collective-permute-start(bf16[2,768,256]{2,1,0:T(8,128)(2,1)} %get-tuple-element.45), channel_id=1, source_target_pairs={{0,96},{32,0},{64,32},{96,64},{128,224},{160,128},{192,160},{224,1... | collective-permute-start | bytes 2359304 | tf_op jit(solution)/shard_map/ppermute | solution.py:145
  100.3 11.0 %copy-start.21 = (bf16[2,384,128]{2,1,0:T(8,128)(2,1)S(1)}, bf16[2,384,128]{2,1,0:T(8,128)(2,1)}, u32[]{:S(2)}) copy-start(bf16[2,384,128]{2,1,0:T(8,128)(2,1)} %get-tuple-element.50) | copy-start | bytes 589828
  100.3 14.7 %collective-permute-start.7 = (bf16[4,384,128]{2,1,0:T(8,128)(2,1)}, bf16[4,384,128]{2,1,0:T(8,128)(2,1)S(1)}, u32[]{:S(2)}, u32[]{:S(2)}) collective-permute-start(bf16[4,384,128]{2,1,0:T(8,128)(2,1)} %get-tuple-element.55), channel_id=1, source_target_pairs={{0,128},{32,160},{64,192},{96,224},{128,0},{160,32},{192,64},{224,... | collective-permute-start | bytes 1179656 | tf_op jit(solution)/shard_map/ppermute | solution.py:145
  100.3 6.1 %collective-permute-start = (bf16[2,384,128]{2,1,0:T(8,128)(2,1)}, bf16[2,384,128]{2,1,0:T(8,128)(2,1)S(1)}, u32[]{:S(2)}, u32[]{:S(2)}) collective-permute-start(bf16[2,384,128]{2,1,0:T(8,128)(2,1)} %get-tuple-element.38), channel_id=1, source_target_pairs={{0,32},{32,64},{64,96},{96,0},{128,160},{160,192},{192,224},{224,1... | collective-permute-start | bytes 589832 | tf_op jit(solution)/shard_map/ppermute | solution.py:145
  101.6 9.7 %collective-permute-start.1 = (bf16[2,384,128]{2,1,0:T(8,128)(2,1)}, bf16[2,384,128]{2,1,0:T(8,128)(2,1)S(1)}, u32[]{:S(2)}, u32[]{:S(2)}) collective-permute-start(bf16[2,384,128]{2,1,0:T(8,128)(2,1)} %get-tuple-element.39), channel_id=1, source_target_pairs={{0,64},{32,96},{64,0},{96,32},{128,192},{160,224},{192,128},{224,1... | collective-permute-start | bytes 589832 | tf_op jit(solution)/shard_map/ppermute | solution.py:145
  104.1 7.2 %collective-permute-start.2 = (bf16[2,384,128]{2,1,0:T(8,128)(2,1)}, bf16[2,384,128]{2,1,0:T(8,128)(2,1)S(1)}, u32[]{:S(2)}, u32[]{:S(2)}) collective-permute-start(bf16[2,384,128]{2,1,0:T(8,128)(2,1)} %get-tuple-element.40), channel_id=1, source_target_pairs={{0,96},{32,0},{64,32},{96,64},{128,224},{160,128},{192,160},{224,1... | collective-permute-start | bytes 589832 | tf_op jit(solution)/shard_map/ppermute | solution.py:145
  111.4 3.6 %collective-permute-start.6 = (bf16[384,128]{1,0:T(8,128)(2,1)S(1)}, bf16[384,128]{1,0:T(8,128)(2,1)S(1)}, u32[]{:S(2)}, u32[]{:S(2)}) collective-permute-start(bf16[384,128]{1,0:T(8,128)(2,1)S(1)} %fusion.4), channel_id=1, source_target_pairs={{0,128},{32,160},{64,192},{96,224},{128,0},{160,32},{192,64},{224,... | collective-permute-start | bytes 294920 | tf_op jit(solution)/shard_map/ppermute | solution.py:145
  112.6 8.7 %collective-permute-start.11 = (bf16[768,256]{1,0:T(8,128)(2,1)S(1)}, bf16[768,256]{1,0:T(8,128)(2,1)S(1)}, u32[]{:S(2)}, u32[]{:S(2)}) collective-permute-start(bf16[768,256]{1,0:T(8,128)(2,1)S(1)} %fusion), channel_id=1, source_target_pairs={{0,128},{32,160},{64,192},{96,224},{128,0},{160,32},{192,64},{224,... | collective-permute-start | bytes 1179656 | tf_op jit(solution)/shard_map/ppermute | solution.py:145
  115.1 7.6 %collective-permute-start.10 = (bf16[384,128]{1,0:T(8,128)(2,1)S(1)}, bf16[384,128]{1,0:T(8,128)(2,1)S(1)}, u32[]{:S(2)}, u32[]{:S(2)}) collective-permute-start(bf16[384,128]{1,0:T(8,128)(2,1)S(1)} %get-tuple-element.66), channel_id=1, source_target_pairs={{0,96},{32,0},{64,32},{96,64},{128,224},{160,128},{192,160},{224,1... | collective-permute-start | bytes 294920 | tf_op jit(solution)/shard_map/ppermute | solution.py:145
  118.2 5.0 %collective-permute-start.9 = (bf16[384,128]{1,0:T(8,128)(2,1)S(1)}, bf16[384,128]{1,0:T(8,128)(2,1)S(1)}, u32[]{:S(2)}, u32[]{:S(2)}) collective-permute-start(bf16[384,128]{1,0:T(8,128)(2,1)S(1)} %get-tuple-element.67), channel_id=1, source_target_pairs={{0,64},{32,96},{64,0},{96,32},{128,192},{160,224},{192,128},{224,1... | collective-permute-start | bytes 294920 | tf_op jit(solution)/shard_map/ppermute | solution.py:145
  119.9 4.7 %collective-permute-start.8 = (bf16[384,128]{1,0:T(8,128)(2,1)S(1)}, bf16[384,128]{1,0:T(8,128)(2,1)S(1)}, u32[]{:S(2)}, u32[]{:S(2)}) collective-permute-start(bf16[384,128]{1,0:T(8,128)(2,1)S(1)} %get-tuple-element.65), channel_id=1, source_target_pairs={{0,32},{32,64},{64,96},{96,0},{128,160},{160,192},{192,224},{224,1... | collective-permute-start | bytes 294920 | tf_op jit(solution)/shard_map/ppermute | solution.py:145
  124.9 24.7 %copy-start.10 = (bf16[768,128]{1,0:T(8,128)(2,1)}, bf16[768,128]{1,0:T(8,128)(2,1)S(1)}, u32[]{:S(2)}) copy-start(bf16[768,128]{1,0:T(8,128)(2,1)S(1)} %get-tuple-element.62.refs_8_) | copy-start | bytes 589828
  124.9 24.7 %copy-start.11 = (bf16[768,128]{1,0:T(8,128)(2,1)}, bf16[768,128]{1,0:T(8,128)(2,1)S(1)}, u32[]{:S(2)}) copy-start(bf16[768,128]{1,0:T(8,128)(2,1)S(1)} %get-tuple-element.63.refs_0_) | copy-start | bytes 589828
  124.9 6.5 %collective-permute-start.12 = (bf16[768,128]{1,0:T(8,128)(2,1)S(1)}, bf16[768,128]{1,0:T(8,128)(2,1)S(1)}, u32[]{:S(2)}, u32[]{:S(2)}) collective-permute-start(bf16[768,128]{1,0:T(8,128)(2,1)S(1)} %get-tuple-element.63.refs_0_), channel_id=1, source_target_pairs={{0,32},{32,64},{64,96},{96,0},{128,160},{160,192},{192,224},{224,1... | collective-permute-start | bytes 589832 | tf_op jit(solution)/shard_map/ppermute | solution.py:145
  128.1 4.5 %collective-permute-start.13 = (bf16[768,128]{1,0:T(8,128)(2,1)S(1)}, bf16[768,128]{1,0:T(8,128)(2,1)S(1)}, u32[]{:S(2)}, u32[]{:S(2)}) collective-permute-start(bf16[768,128]{1,0:T(8,128)(2,1)S(1)} %get-tuple-element.63.refs_0_), channel_id=1, source_target_pairs={{0,96},{32,0},{64,32},{96,64},{128,224},{160,128},{192,160},{224,1... | collective-permute-start | bytes 589832 | tf_op jit(solution)/shard_map/ppermute | solution.py:145
  128.1 4.7 %collective-permute-start.15 = (bf16[768,128]{1,0:T(8,128)(2,1)S(1)}, bf16[768,128]{1,0:T(8,128)(2,1)S(1)}, u32[]{:S(2)}, u32[]{:S(2)}) collective-permute-start(bf16[768,128]{1,0:T(8,128)(2,1)S(1)} %get-tuple-element.63.refs_0_), channel_id=1, source_target_pairs={{0,128},{32,160},{64,192},{96,224},{128,0},{160,32},{192,64},{224,... | collective-permute-start | bytes 589832 | tf_op jit(solution)/shard_map/ppermute | solution.py:145
  128.7 6.3 %collective-permute-start.22 = (bf16[768,128]{1,0:T(8,128)(2,1)S(1)}, bf16[768,128]{1,0:T(8,128)(2,1)S(1)}, u32[]{:S(2)}, u32[]{:S(2)}) collective-permute-start(bf16[768,128]{1,0:T(8,128)(2,1)S(1)} %get-tuple-element.62.refs_8_), channel_id=1, source_target_pairs={{0,128},{32,160},{64,192},{96,224},{128,0},{160,32},{192,64},{224,... | collective-permute-start | bytes 589832 | tf_op jit(solution)/shard_map/ppermute | solution.py:145
  129.5 7.3 %collective-permute-start.19 = (bf16[768,128]{1,0:T(8,128)(2,1)S(1)}, bf16[768,128]{1,0:T(8,128)(2,1)S(1)}, u32[]{:S(2)}, u32[]{:S(2)}) collective-permute-start(bf16[768,128]{1,0:T(8,128)(2,1)S(1)} %get-tuple-element.62.refs_8_), channel_id=1, source_target_pairs={{0,32},{32,64},{64,96},{96,0},{128,160},{160,192},{192,224},{224,1... | collective-permute-start | bytes 589832 | tf_op jit(solution)/shard_map/ppermute | solution.py:145
  131.3 18.2 %copy-start.14 = (bf16[768,128]{1,0:T(8,128)(2,1)}, bf16[768,128]{1,0:T(8,128)(2,1)S(1)}, u32[]{:S(2)}) copy-start(bf16[768,128]{1,0:T(8,128)(2,1)S(1)} %collective-permute-done.12.refs_1_) | copy-start | bytes 589828
  131.3 6.7 %collective-permute-start.20 = (bf16[768,128]{1,0:T(8,128)(2,1)S(1)}, bf16[768,128]{1,0:T(8,128)(2,1)}, u32[]{:S(2)}, u32[]{:S(2)}) collective-permute-start(bf16[768,128]{1,0:T(8,128)(2,1)S(1)} %get-tuple-element.62.refs_8_), channel_id=1, source_target_pairs={{0,96},{32,0},{64,32},{96,64},{128,224},{160,128},{192,160},{224,1... | collective-permute-start | bytes 589832 | tf_op jit(solution)/shard_map/ppermute | solution.py:145
  132.6 17.0 %copy-start.15 = (bf16[768,128]{1,0:T(8,128)(2,1)}, bf16[768,128]{1,0:T(8,128)(2,1)S(1)}, u32[]{:S(2)}) copy-start(bf16[768,128]{1,0:T(8,128)(2,1)S(1)} %collective-permute-done.13.refs_2_) | copy-start | bytes 589828
  132.6 7.0 %collective-permute-start.14 = (bf16[768,128]{1,0:T(8,128)(2,1)S(1)}, bf16[768,128]{1,0:T(8,128)(2,1)}, u32[]{:S(2)}, u32[]{:S(2)}) collective-permute-start(bf16[768,128]{1,0:T(8,128)(2,1)S(1)} %collective-permute-done.12.refs_1_), channel_id=1, source_target_pairs={{0,32},{32,64},{64,96},{96,0},{128,160},{160,192},{192,224},{224,1... | collective-permute-start | bytes 589832 | tf_op jit(solution)/shard_map/ppermute | solution.py:145
  132.8 16.8 %copy-start.16 = (bf16[768,128]{1,0:T(8,128)(2,1)}, bf16[768,128]{1,0:T(8,128)(2,1)S(1)}, u32[]{:S(2)}) copy-start(bf16[768,128]{1,0:T(8,128)(2,1)S(1)} %collective-permute-done.15.refs_4_) | copy-start | bytes 589828
  132.8 6.8 %collective-permute-start.16 = (bf16[768,128]{1,0:T(8,128)(2,1)S(1)}, bf16[768,128]{1,0:T(8,128)(2,1)S(1)}, u32[]{:S(2)}, u32[]{:S(2)}) collective-permute-start(bf16[768,128]{1,0:T(8,128)(2,1)S(1)} %collective-permute-done.12.refs_1_), channel_id=1, source_target_pairs={{0,128},{32,160},{64,192},{96,224},{128,0},{160,32},{192,64},{224,... | collective-permute-start | bytes 589832 | tf_op jit(solution)/shard_map/ppermute | solution.py:145
  135.0 14.6 %copy-start.17 = (bf16[768,128]{1,0:T(8,128)(2,1)}, bf16[768,128]{1,0:T(8,128)(2,1)S(1)}, u32[]{:S(2)}) copy-start(bf16[768,128]{1,0:T(8,128)(2,1)S(1)} %collective-permute-done.22.refs_12_) | copy-start | bytes 589828
  135.0 8.0 %collective-permute-start.23 = (bf16[768,128]{1,0:T(8,128)(2,1)S(1)}, bf16[768,128]{1,0:T(8,128)(2,1)}, u32[]{:S(2)}, u32[]{:S(2)}) collective-permute-start(bf16[768,128]{1,0:T(8,128)(2,1)S(1)} %collective-permute-done.22.refs_12_), channel_id=1, source_target_pairs={{0,32},{32,64},{64,96},{96,0},{128,160},{160,192},{192,224},{224,1... | collective-permute-start | bytes 589832 | tf_op jit(solution)/shard_map/ppermute | solution.py:145
  136.8 12.8 %copy-start.18 = (bf16[768,128]{1,0:T(8,128)(2,1)}, bf16[768,128]{1,0:T(8,128)(2,1)S(1)}, u32[]{:S(2)}) copy-start(bf16[768,128]{1,0:T(8,128)(2,1)S(1)} %collective-permute-done.19.refs_9_) | copy-start | bytes 589828
  136.8 7.6 %collective-permute-start.17 = (bf16[768,128]{1,0:T(8,128)(2,1)S(1)}, bf16[768,128]{1,0:T(8,128)(2,1)S(1)}, u32[]{:S(2)}, u32[]{:S(2)}) collective-permute-start(bf16[768,128]{1,0:T(8,128)(2,1)S(1)} %collective-permute-done.13.refs_2_), channel_id=1, source_target_pairs={{0,128},{32,160},{64,192},{96,224},{128,0},{160,32},{192,64},{224,... | collective-permute-start | bytes 589832 | tf_op jit(solution)/shard_map/ppermute | solution.py:145
  138.0 9.0 %collective-permute-start.24 = (bf16[768,128]{1,0:T(8,128)(2,1)S(1)}, bf16[768,128]{1,0:T(8,128)(2,1)}, u32[]{:S(2)}, u32[]{:S(2)}) collective-permute-start(bf16[768,128]{1,0:T(8,128)(2,1)S(1)} %collective-permute-done.22.refs_12_), channel_id=1, source_target_pairs={{0,96},{32,0},{64,32},{96,64},{128,224},{160,128},{192,160},{224,1... | collective-permute-start | bytes 589832 | tf_op jit(solution)/shard_map/ppermute | solution.py:145
  139.6 7.5 %collective-permute-start.21 = (bf16[768,128]{1,0:T(8,128)(2,1)}, bf16[768,128]{1,0:T(8,128)(2,1)}, u32[]{:S(2)}, u32[]{:S(2)}) collective-permute-start(bf16[768,128]{1,0:T(8,128)(2,1)} %collective-permute-done.20.refs_10_), channel_id=1, source_target_pairs={{0,96},{32,0},{64,32},{96,64},{128,224},{160,128},{192,160},{224,1... | collective-permute-start | bytes 589832 | tf_op jit(solution)/shard_map/ppermute | solution.py:145
  139.6 7.5 %collective-permute-start.18 = (bf16[768,128]{1,0:T(8,128)(2,1)}, bf16[768,128]{1,0:T(8,128)(2,1)}, u32[]{:S(2)}, u32[]{:S(2)}) collective-permute-start(bf16[768,128]{1,0:T(8,128)(2,1)} %collective-permute-done.14.refs_3_), channel_id=1, source_target_pairs={{0,128},{32,160},{64,192},{96,224},{128,0},{160,32},{192,64},{224,... | collective-permute-start | bytes 589832 | tf_op jit(solution)/shard_map/ppermute | solution.py:145
  143.0 6.5 %collective-permute-start.25 = (bf16[768,128]{1,0:T(8,128)(2,1)}, bf16[768,128]{1,0:T(8,128)(2,1)}, u32[]{:S(2)}, u32[]{:S(2)}) collective-permute-start(bf16[768,128]{1,0:T(8,128)(2,1)} %collective-permute-done.23.refs_13_), channel_id=1, source_target_pairs={{0,32},{32,64},{64,96},{96,0},{128,160},{160,192},{192,224},{224,1... | collective-permute-start | bytes 589832 | tf_op jit(solution)/shard_map/ppermute | solution.py:145
  144.4 12.4 %collective-permute-start.26 = (bf16[768,128]{1,0:T(8,128)(2,1)S(1)}, bf16[768,128]{1,0:T(8,128)(2,1)}, u32[]{:S(2)}, u32[]{:S(2)}) collective-permute-start(bf16[768,128]{1,0:T(8,128)(2,1)S(1)} %get-tuple-element.60), channel_id=1, source_target_pairs={{0,128},{32,160},{64,192},{96,224},{128,0},{160,32},{192,64},{224,... | collective-permute-start | bytes 589832 | tf_op jit(solution)/shard_map/ppermute | solution.py:145
  156.8 23.0 %copy-start.6 = (bf16[32,24,896]{2,1,0:T(8,128)(2,1)S(1)}, bf16[32,24,896]{2,1,0:T(8,128)(2,1)}, u32[]{:S(2)}) copy-start(bf16[32,24,896]{2,1,0:T(8,128)(2,1)} %copy-done.5) | copy-start | bytes 4128772
  156.8 55.6 %all-to-all-start.2 = ((bf16[32,24,896]{2,1,0:T(8,128)(2,1)}), bf16[32,24,896]{2,1,0:T(8,128)(2,1)S(1)}, u32[]{:S(2)}, u32[]{:S(2)}) async-start(bf16[32,24,896]{2,1,0:T(8,128)(2,1)} %bitcast.80), calls=%async_computation.2 | async-start | bytes 2752512 | tf_op jit(solution)/shard_map/all_to_all | solution.py:213
  177.1 11.8 %collective-permute-start.27 = (bf16[2,768,128]{2,1,0:T(8,128)(2,1)S(1)}, bf16[2,768,128]{2,1,0:T(8,128)(2,1)S(1)}, u32[]{:S(2)}, u32[]{:S(2)}) collective-permute-start(bf16[2,768,128]{2,1,0:T(8,128)(2,1)S(1)} %pad_maximum_fusion.1.refs_0_), channel_id=1, source_target_pairs={{0,32},{32,64},{64,96},{96,0},{128,160},{160,192},{192,224},{224,1... | collective-permute-start | bytes 1179656 | tf_op jit(solution)/shard_map/ppermute | solution.py:145
  177.2 11.8 %collective-permute-start.28 = (bf16[2,768,128]{2,1,0:T(8,128)(2,1)S(1)}, bf16[2,768,128]{2,1,0:T(8,128)(2,1)S(1)}, u32[]{:S(2)}, u32[]{:S(2)}) collective-permute-start(bf16[2,768,128]{2,1,0:T(8,128)(2,1)S(1)} %pad_maximum_fusion.1.refs_0_), channel_id=1, source_target_pairs={{0,96},{32,0},{64,32},{96,64},{128,224},{160,128},{192,160},{224,1... | collective-permute-start | bytes 1179656 | tf_op jit(solution)/shard_map/ppermute | solution.py:145
  179.9 11.9 %copy-start.25 = (bf16[768,1024]{1,0:T(8,128)(2,1)S(1)}, bf16[768,1024]{1,0:T(8,128)(2,1)}, u32[]{:S(2)}) copy-start(bf16[768,1024]{1,0:T(8,128)(2,1)} %get-tuple-element.59) | copy-start | bytes 4718596
  188.9 6.6 %collective-permute-start.29 = (bf16[768,128]{1,0:T(8,128)(2,1)S(1)}, bf16[768,128]{1,0:T(8,128)(2,1)S(1)}, u32[]{:S(2)}, u32[]{:S(2)}) collective-permute-start(bf16[768,128]{1,0:T(8,128)(2,1)S(1)} %slice_bitcast_fusion.1), channel_id=1, source_target_pairs={{0,32},{32,64},{64,96},{96,0},{128,160},{160,192},{192,224},{224,1... | collective-permute-start | bytes 589832 | tf_op jit(solution)/shard_map/ppermute | solution.py:145
  189.0 6.5 %collective-permute-start.30 = (bf16[768,128]{1,0:T(8,128)(2,1)S(1)}, bf16[768,128]{1,0:T(8,128)(2,1)S(1)}, u32[]{:S(2)}, u32[]{:S(2)}) collective-permute-start(bf16[768,128]{1,0:T(8,128)(2,1)S(1)} %slice_bitcast_fusion), channel_id=1, source_target_pairs={{0,96},{32,0},{64,32},{96,64},{128,224},{160,128},{192,160},{224,1... | collective-permute-start | bytes 589832 | tf_op jit(solution)/shard_map/ppermute | solution.py:145
  (12 other events, 52.8 us)
